TPU v7x, 512 devices: a whole 4x8x8 slice. The times are simulated.
512 devices in a mesh: tile: 128 (over z, y, core), gz: 4 (over x).
Axes of the slice: x: 4, y: 8, z: 8, core: 2. Of those that a mesh axis runs over, the one named last changes fastest.
Arguments:
- images: bfloat16 [32768, 3, 16, 128], P('tile', None, 'gz'), may hold values from 0.19921875 to 2
- partner: int32 [128], replicated, may hold values from 0 to 127, as said below
- dest: int32 [16384, 1], P('tile'), may hold values from 0 to 127; in each aligned block of 128 rows (0 to 127, 128 to 255, ...) at most 2 rows name the same one
- offset: int32 [16384], P('tile'), may hold values from 0 to 254
- extent: int32 [16384], P('tile'), may hold values from 1 to 2
Outputs:
- corrected: bfloat16 [32768, 3, 16, 128], P('tile', None, 'gz')
- joined: bfloat16 [32768, 3, 16, 128], P('tile', None, 'gz')
Inputs may be any that keep to these rules, and one draw needn't show every extreme that they name: partner[partner[t]] = t; partner[t] is t (no neighbour) or differs from t in exactly one bit of the index. `dest`: in each aligned block of 128 rows (one tile's pieces) no group is named more than 2 times, a bound that some block reaches.
All inputs are finite; a program needn't handle non-finite values.
Results may differ from a plain program's by a relative error of at most 0.0024.
Values may be sent and summed in bfloat16 or wider, within the bound.
No kernel may reach another device: no remote copies, remote signals or barrier semaphores. Data moves between devices by JAX's collectives and lax.ppermute only.
A program may use at most 64 MiB of HBM per device.

v0:
```python
import math

import jax
import jax.numpy as jnp
from jax import lax
from jax.sharding import PartitionSpec as P

CAP = 2
HALO = 3


gauss_raw = [math.exp(-0.5 * k * k) for k in range(-2, 3)]
gauss_taps = [w / sum(gauss_raw) for w in gauss_raw]


def with_halo(block, sides, width):
    for axis, dim in sides:
        count = lax.axis_size(axis)
        forward = [(i, i + 1) for i in range(count - 1)]
        backward = [(target, source) for source, target in forward]
        low = lax.ppermute(
            lax.slice_in_dim(block, block.shape[dim] - width, None, axis=dim), axis, forward
        )
        high = lax.ppermute(lax.slice_in_dim(block, 0, width, axis=dim), axis, backward)
        block = jnp.concatenate([low, block, high], axis=dim)
    return block


def central(values, axis):
    size = values.shape[axis]
    padded = jnp.pad(values, [(1, 1) if a == axis else (0, 0) for a in range(values.ndim)])
    upper = lax.slice_in_dim(padded, 2, size + 2, axis=axis)
    lower = lax.slice_in_dim(padded, 0, size, axis=axis)
    return (upper - lower) * 0.5


def smooth(values, axis):
    size = values.shape[axis]
    reach = len(gauss_taps) // 2
    padded = jnp.pad(values, [(reach, reach) if a == axis else (0, 0) for a in range(values.ndim)])
    total = jnp.zeros(values.shape, jnp.float32)
    for k in range(len(gauss_taps)):
        total = total + gauss_taps[k] * lax.slice_in_dim(padded, k, k + size, axis=axis)
    return total


def correct_channel(own, facing, inside, depth):
    first = own.astype(jnp.float32)
    second = facing.astype(jnp.float32)
    dy_a, dz_a, dx_a = (central(first, 0), central(first, 1), central(first, 2))
    dy_b, dz_b, dx_b = (central(second, 0), central(second, 1), central(second, 2))
    prod_one = first * second + dy_a * dy_b + dz_a * dz_b + dx_a * dx_b
    prod_two = second * second + dy_b * dy_b + dz_b * dz_b + dx_b * dx_b
    prod_one = jnp.where(inside[None, :, None], prod_one, 0.0)
    prod_two = jnp.where(inside[None, :, None], prod_two, 0.0)
    deep_one = lax.slice_in_dim(smooth(prod_one, 1), HALO, HALO + depth, axis=1)
    deep_two = lax.slice_in_dim(smooth(prod_two, 1), HALO, HALO + depth, axis=1)
    smooth_one = smooth(smooth(deep_one, 0), 2)
    smooth_two = smooth(smooth(deep_two, 0), 2)
    centre = lax.slice_in_dim(first, HALO, HALO + depth, axis=1)
    return (centre * (smooth_one + 1.0) / (smooth_two + 1.0)).astype(jnp.bfloat16)


def body(images, partner, dest, offset, extent):
    ntile = lax.axis_size("tile")
    plane_idx = lax.axis_index("gz")
    nplane = lax.axis_size("gz")
    rows, chans, depth, cols = images.shape
    piece_rows = rows // ntile
    blocks = images.reshape(ntile, piece_rows, chans, depth, cols)
    spread = lax.all_to_all(blocks, "tile", split_axis=0, concat_axis=0, tiled=True)
    everyone = jnp.arange(ntile, dtype=jnp.int32)
    picked = jnp.take(spread, partner, axis=0)
    keep = (partner != everyone)[:, None, None, None, None]
    picked = jnp.where(keep, picked, jnp.zeros_like(picked))
    returned = lax.all_to_all(picked, "tile", split_axis=0, concat_axis=0, tiled=True)
    facing = returned.reshape(rows, chans, depth, cols)
    facing = jnp.flip(facing, axis=3)
    extended = with_halo(jnp.stack([images, facing]), (("gz", 3),), HALO)
    positions = plane_idx * depth - HALO + jnp.arange(depth + 2 * HALO, dtype=jnp.int32)
    inside = (positions >= 0) & (positions < depth * nplane)
    outs = [
        correct_channel(extended[0, :, c], extended[1, :, c], inside, depth) for c in range(chans)
    ]
    corrected = jnp.stack(outs, axis=1)
    width = chans * depth * cols
    pieces = corrected.reshape(ntile, piece_rows * width)
    targets = dest[:, 0]
    order_idx = jnp.arange(ntile, dtype=jnp.int32)
    same_owner = targets[:, None] == targets[None, :]
    earlier = order_idx[:, None] > order_idx[None, :]
    slot = jnp.sum((same_owner & earlier).astype(jnp.int32), axis=1)
    owners = jnp.arange(ntile, dtype=jnp.int32)
    slots = jnp.arange(CAP, dtype=jnp.int32)
    select = (owners[:, None, None] == targets[None, None, :]) & (
        slots[None, :, None] == slot[None, None, :]
    )
    outgoing = jnp.einsum(
        "dcj,jm->dcm", select.astype(jnp.bfloat16), pieces, preferred_element_type=jnp.float32
    )
    outgoing = outgoing.astype(jnp.bfloat16).reshape(ntile, CAP, piece_rows, width)
    send_offset = jnp.sum(jnp.where(select, offset[None, None, :], 0), axis=2)
    send_extent = jnp.sum(jnp.where(select, extent[None, None, :], 0), axis=2)
    labels = jnp.stack([send_offset, send_extent], axis=-1)
    received, info = (
        lax.all_to_all(outgoing, "tile", split_axis=0, concat_axis=0, tiled=True),
        lax.all_to_all(labels, "tile", split_axis=0, concat_axis=0, tiled=True),
    )
    within = jnp.arange(piece_rows, dtype=jnp.int32)
    starts = info[:, :, 0][:, :, None] + within[None, None, :]
    live = within[None, None, :] < info[:, :, 1][:, :, None]
    group_rows = jnp.arange(rows, dtype=jnp.int32)
    place = (group_rows[:, None, None, None] == starts[None]) & live[None]
    summed = jnp.einsum(
        "fabp,abpm->fm", place.astype(jnp.bfloat16), received, preferred_element_type=jnp.float32
    )
    counts = jnp.sum(place.astype(jnp.float32), axis=(1, 2, 3))
    joined = (summed / jnp.maximum(counts, 1.0)[:, None]).astype(jnp.bfloat16)
    return (corrected, joined.reshape(rows, chans, depth, cols))


def solution(mesh):
    in_specs = (P("tile", None, "gz", None), P(), P("tile", None), P("tile"), P("tile"))
    out_specs = (P("tile", None, "gz", None), P("tile", None, "gz", None))
    return jax.shard_map(body, mesh=mesh, in_specs=in_specs, out_specs=out_specs, check_vma=False)
```

profile of v0, /device:TPU:8, one launch (start us, length us, event | category | flops | bytes accessed | tf_op | source)
XLA Modules:
  0.0 196.4 jit_solution(5442641778875161923)
XLA Ops:
  0.6 17.4 %all-to-all-start = ((bf16[128,2,3,4,128]{4,3,2,1,0:T(4,128)(2,1)}), bf16[128,2,3,4,128]{4,3,2,1,0:T(4,128)(2,1)S(1)}, u32[]{:S(2)}, u32[]{:S(2)}) async-start(bf16[128,2,3,4,128]{4,3,2,1,0:T(4,128)(2,1)} %bitcast.74), calls=%async_computation | async-start | bytes 1572864 | tf_op jit(solution)/shard_map/all_to_all | solution.py:71
  18.1 25.7 %all-to-all-done = bf16[128,2,3,4,128]{4,3,2,1,0:T(4,128)(2,1)S(1)} async-done(((bf16[128,2,3,4,128]{4,3,2,1,0:T(4,128)(2,1)}), bf16[128,2,3,4,128]{4,3,2,1,0:T(4,128)(2,1)S(1)}, u32[]{:S(2)}, u32[]{:S(2)}) %all-to-all-start) | async-done | bytes 786464 | tf_op jit(solution)/shard_map/all_to_all | solution.py:71
  43.8 1.3 gather_fusion
  45.1 1.6 select_select_fusion
  46.7 5.8 %all-to-all-start.1 = ((bf16[128,2,3,4,128]{4,3,2,1,0:T(4,128)(2,1)}), bf16[128,2,3,4,128]{4,3,2,1,0:T(4,128)(2,1)S(1)}, u32[]{:S(2)}, u32[]{:S(2)}) async-start(bf16[128,2,3,4,128]{4,3,2,1,0:T(4,128)(2,1)} %select_select_fusion), calls=%async_computation.1 | async-start | bytes 1572864 | tf_op jit(solution)/shard_map/all_to_all | solution.py:76
  52.6 25.6 %all-to-all-done.1 = bf16[128,2,3,4,128]{4,3,2,1,0:T(4,128)(2,1)S(1)} async-done(((bf16[128,2,3,4,128]{4,3,2,1,0:T(4,128)(2,1)}), bf16[128,2,3,4,128]{4,3,2,1,0:T(4,128)(2,1)S(1)}, u32[]{:S(2)}, u32[]{:S(2)}) %all-to-all-start.1) | async-done | bytes 786464 | tf_op jit(solution)/shard_map/all_to_all | solution.py:76
  78.4 2.3 %rev.4 = bf16[256,3,4,128]{3,0,2,1:T(8,128)(2,1)S(1)} reverse(bf16[256,3,4,128]{3,0,2,1:T(8,128)(2,1)S(1)} %copy.36), dimensions={3} | reverse | bytes 1572864 | tf_op jit(solution)/shard_map/jit(_flip)/rev | solution.py:78
  80.7 1.6 fusion.42
  82.3 3.5 %collective-permute-start = (bf16[2,256,3,3,128]{4,1,3,2,0:T(8,128)(2,1)}, bf16[2,256,3,3,128]{4,1,3,2,0:T(8,128)(2,1)S(1)}, u32[]{:S(2)}, u32[]{:S(2)}) collective-permute-start(bf16[2,256,3,3,128]{4,1,3,2,0:T(8,128)(2,1)} %get-tuple-element.22), channel_id=1, source_target_pairs={{0,1},{1,2},{2,3},{4,5},{5,6},{6,7},{8,9},{9,10},{10,11},{12,13},{... | collective-permute-start | bytes 3538952 | tf_op jit(solution)/shard_map/ppermute | solution.py:21
  85.8 1.3 collective-permute-start.1
  87.5 0.8 copy.37
  88.3 5.8 %all-to-all-start.2 = ((s32[128,2,2]{1,2,0:T(2,128)}), s32[128,2,2]{1,2,0:T(2,128)S(1)}, u32[]{:S(2)}, u32[]{:S(2)}) async-start(s32[128,2,2]{1,2,0:T(2,128)} %copy.37), calls=%async_computation.2 | async-start | bytes 262144 | tf_op jit(solution)/shard_map/all_to_all | solution.py:107
  94.1 16.8 %collective-permute-done = bf16[2,256,3,3,128]{4,1,3,2,0:T(8,128)(2,1)S(1)} collective-permute-done((bf16[2,256,3,3,128]{4,1,3,2,0:T(8,128)(2,1)}, bf16[2,256,3,3,128]{4,1,3,2,0:T(8,128)(2,1)S(1)}, u32[]{:S(2)}, u32[]{:S(2)}) %collective-permute-start) | collective-permute-done | bytes 1179680 | tf_op jit(solution)/shard_map/ppermute | solution.py:21
  110.9 4.2 %collective-permute-done.1 = bf16[2,256,3,3,128]{4,1,3,2,0:T(8,128)(2,1)} collective-permute-done((bf16[2,256,3,3,128]{4,1,3,2,0:T(8,128)(2,1)}, bf16[2,256,3,3,128]{4,1,3,2,0:T(8,128)(2,1)}, u32[]{:S(2)}, u32[]{:S(2)}) %collective-permute-start.1) | collective-permute-done | bytes 1179680 | tf_op jit(solution)/shard_map/ppermute | solution.py:24
  115.1 1.6 pad_maximum_fusion
  116.7 1.0 fusion.48
  117.7 2.4 %fusion.16 = (f32[256,10,128]{2,0,1:T(8,128)S(1)}, f32[256,10,128]{2,0,1:T(8,128)S(1)}) fusion(f32[256,10,128]{2,0,1:T(8,128)S(1)} %get-tuple-element.20, pred[10]{0:T(512)(128)(4,1)S(1)} %compare_and_fusion, bf16[2,256,3,10,128]{4,1,3,2,0:T(8,128)(2,1)S(1)} %pad_maximum_fusion, f32[256,10,128]{2,0,1:T(8,128)S(1)} %get-tuple-element.19), kind=kLoop, calls=%fused_computation.94 | loop fusion | flops 11468800 | bytes 5898250 | tf_op jit(solution)/shard_map/jit(_where)/select_n | solution.py:54
  120.1 0.4 pad_slice_fusion.27
  120.5 0.2 fusion.121
  120.7 1.1 multiply_add_fusion.3
  121.8 0.5 pad_slice_fusion.23
  122.3 0.2 fusion.117
  122.5 1.1 multiply_add_fusion.2
  123.6 2.4 %fusion.8 = (f32[256,10,128]{2,0,1:T(8,128)S(1)}, f32[256,10,128]{2,0,1:T(8,128)S(1)}) fusion(f32[256,10,128]{2,0,1:T(8,128)S(1)} %get-tuple-element.16, pred[10]{0:T(512)(128)(4,1)S(1)} %compare_and_fusion, bf16[2,256,3,10,128]{4,1,3,2,0:T(8,128)(2,1)S(1)} %pad_maximum_fusion, f32[256,10,128]{2,0,1:T(8,128)S(1)} %get-tuple-element.21), kind=kLoop, calls=%fused_computation.86 | loop fusion | flops 11468800 | bytes 5898250 | tf_op jit(solution)/shard_map/jit(_where)/select_n | solution.py:54
  126.0 0.5 pad_slice_fusion.35
  126.5 0.2 fusion.129
  126.7 1.1 multiply_add_fusion.5
  127.8 0.5 pad_slice_fusion.31
  128.3 0.2 fusion.125
  128.5 1.1 multiply_add_fusion.4
  129.6 2.6 %fusion.24 = (f32[256,10,128]{2,0,1:T(8,128)S(1)}, f32[256,10,128]{2,0,1:T(8,128)S(1)}) fusion(f32[256,10,128]{2,0,1:T(8,128)S(1)} %get-tuple-element.18, pred[10]{0:T(512)(128)(4,1)S(1)} %compare_and_fusion, bf16[2,256,3,10,128]{4,1,3,2,0:T(8,128)(2,1)S(1)} %pad_maximum_fusion, f32[256,10,128]{2,0,1:T(8,128)S(1)} %get-tuple-element.17), kind=kLoop, calls=%fused_computation.102 | loop fusion | flops 11468800 | bytes 5898250 | tf_op jit(solution)/shard_map/jit(_where)/select_n | solution.py:54
  132.2 2.3 %pad_slice_fusion.15 = (f32[256,10,128]{2,0,1:T(8,128)S(1)}, f32[256,10,128]{2,0,1:T(8,128)S(1)}, f32[256,10,128]{2,0,1:T(8,128)S(1)}, f32[256,10,128]{2,0,1:T(8...) fusion(f32[256,10,128]{2,0,1:T(8,128)S(1)} %get-tuple-element.1, ...), kind=kLoop, calls=%fused_computation.19 | loop fusion | bytes 13107200 | tf_op jit(solution)/shard_map/slice | solution.py:43
  134.5 1.3 fusion.113
  135.7 0.3 multiply_add_fusion.1
  136.0 0.2 fusion.109
  136.3 0.3 multiply_add_fusion
  136.6 1.2 fusion.148
  137.8 2.2 %fusion.146 = (bf16[256,1,4,128]{3,0,2,1:T(8,128)(2,1)S(1)}, bf16[256,1,4,128]{3,0,2,1:T(8,128)(2,1)S(1)}) fusion(f32[256,4,128]{2,0,1:T(8,128)S(1)} %copy-done.5, f32[256,4,128]{2,0,1:T(8,128)S(1)} %copy-done.4, f32[256,10,128]{2,0,1:T(8,128)S(1)} %get-tuple-element.16, f32[256,4,128]{2,0,1:T(8,128)S(1)} %copy-done.3, f32[256,4,128]{2,0,1:T(8,128)S(1)} %copy-done.2, ...), kind=kLoop, calls=%fused_computation.283 | loop fusion | flops 6029312 | bytes 3670016 | tf_op jit(solution)/shard_map/stack | solution.py:85
  140.1 0.6 copy.43
  140.8 0.6 reshape.125
  141.3 0.3 copy-done.1
  141.6 0.6 convolution_convert_fusion
  142.2 1.2 reshape.108
  143.4 2.2 %copy.41 = bf16[128,2,2,1536]{3,2,1,0:T(2,128)(2,1)} copy(bf16[128,2,2,1536]{3,2,0,1:T(2,128)(2,1)S(1)} %reshape.108) | data formatting | bytes 3145728 | tf_op jit(solution)/shard_map/reshape | solution.py:101
  145.6 6.3 %all-to-all-start.3 = ((bf16[128,2,2,1536]{3,2,1,0:T(2,128)(2,1)}), bf16[128,2,2,1536]{3,2,1,0:T(2,128)(2,1)S(1)}, u32[]{:S(2)}, u32[]{:S(2)}) async-start(bf16[128,2,2,1536]{3,2,1,0:T(2,128)(2,1)} %copy.41), calls=%async_computation.3 | async-start | bytes 3145728 | tf_op jit(solution)/shard_map/all_to_all | solution.py:106
  152.4 42.2 %all-to-all-done.3 = bf16[128,2,2,1536]{3,2,1,0:T(2,128)(2,1)S(1)} async-done(((bf16[128,2,2,1536]{3,2,1,0:T(2,128)(2,1)}), bf16[128,2,2,1536]{3,2,1,0:T(2,128)(2,1)S(1)}, u32[]{:S(2)}, u32[]{:S(2)}) %all-to-all-start.3) | async-done | bytes 1572896 | tf_op jit(solution)/shard_map/all_to_all | solution.py:106
  194.6 0.7 fusion.1
  195.3 1.1 reshape.109
  (39 shorter events, 1.2 us)
Async XLA Ops:
  0.6 17.4 %copy-start.9 = (s32[128]{0:T(128)S(1)}, s32[128]{0:T(128)}, u32[]{:S(2)}) copy-start(s32[128]{0:T(128)} %param.6) | copy-start | bytes 1540
  0.6 43.1 %all-to-all-start = ((bf16[128,2,3,4,128]{4,3,2,1,0:T(4,128)(2,1)}), bf16[128,2,3,4,128]{4,3,2,1,0:T(4,128)(2,1)S(1)}, u32[]{:S(2)}, u32[]{:S(2)}) async-start(bf16[128,2,3,4,128]{4,3,2,1,0:T(4,128)(2,1)} %bitcast.74), calls=%async_computation | async-start | bytes 1572864 | tf_op jit(solution)/shard_map/all_to_all | solution.py:71
  45.0 7.4 %copy-start = (bf16[256,3,4,128]{3,2,1,0:T(4,128)(2,1)S(1)}, bf16[256,3,4,128]{3,2,1,0:T(4,128)(2,1)}, u32[]{:S(2)}) copy-start(bf16[256,3,4,128]{3,2,1,0:T(4,128)(2,1)} %param.5) | copy-start | bytes 2359300
  46.7 31.6 %all-to-all-start.1 = ((bf16[128,2,3,4,128]{4,3,2,1,0:T(4,128)(2,1)}), bf16[128,2,3,4,128]{4,3,2,1,0:T(4,128)(2,1)S(1)}, u32[]{:S(2)}, u32[]{:S(2)}) async-start(bf16[128,2,3,4,128]{4,3,2,1,0:T(4,128)(2,1)} %select_select_fusion), calls=%async_computation.1 | async-start | bytes 1572864 | tf_op jit(solution)/shard_map/all_to_all | solution.py:76
  80.7 6.4 %copy-start.6 = (s32[128,1]{0,1:T(1,128)S(1)}, s32[128,1]{0,1:T(1,128)}, u32[]{:S(2)}) copy-start(s32[128,1]{0,1:T(1,128)} %param.7) | copy-start | bytes 1540
  80.7 6.6 %copy-start.7 = (s32[128]{0:T(128)S(1)}, s32[128]{0:T(128)}, u32[]{:S(2)}) copy-start(s32[128]{0:T(128)} %param.8) | copy-start | bytes 1540
  80.7 6.6 %copy-start.8 = (s32[128]{0:T(128)S(1)}, s32[128]{0:T(128)}, u32[]{:S(2)}) copy-start(s32[128]{0:T(128)} %param.9) | copy-start | bytes 1540
  82.3 28.7 %collective-permute-start = (bf16[2,256,3,3,128]{4,1,3,2,0:T(8,128)(2,1)}, bf16[2,256,3,3,128]{4,1,3,2,0:T(8,128)(2,1)S(1)}, u32[]{:S(2)}, u32[]{:S(2)}) collective-permute-start(bf16[2,256,3,3,128]{4,1,3,2,0:T(8,128)(2,1)} %get-tuple-element.22), channel_id=1, source_target_pairs={{0,1},{1,2},{2,3},{4,5},{5,6},{6,7},{8,9},{9,10},{10,11},{12,13},{... | collective-permute-start | bytes 3538952 | tf_op jit(solution)/shard_map/ppermute | solution.py:21
  85.8 29.4 %collective-permute-start.1 = (bf16[2,256,3,3,128]{4,1,3,2,0:T(8,128)(2,1)}, bf16[2,256,3,3,128]{4,1,3,2,0:T(8,128)(2,1)}, u32[]{:S(2)}, u32[]{:S(2)}) collective-permute-start(bf16[2,256,3,3,128]{4,1,3,2,0:T(8,128)(2,1)} %get-tuple-element.23), channel_id=1, source_target_pairs={{1,0},{2,1},{3,2},{5,4},{6,5},{7,6},{9,8},{10,9},{11,10},{13,12},{... | collective-permute-start | bytes 3538952 | tf_op jit(solution)/shard_map/ppermute | solution.py:24
  88.3 57.4 %all-to-all-start.2 = ((s32[128,2,2]{1,2,0:T(2,128)}), s32[128,2,2]{1,2,0:T(2,128)S(1)}, u32[]{:S(2)}, u32[]{:S(2)}) async-start(s32[128,2,2]{1,2,0:T(2,128)} %copy.37), calls=%async_computation.2 | async-start | bytes 262144 | tf_op jit(solution)/shard_map/all_to_all | solution.py:107
  136.2 1.5 copy-start.2
  136.3 1.5 copy-start.3
  136.3 1.5 copy-start.4
  136.3 1.5 copy-start.5
  140.7 0.9 copy-start.1
  145.6 49.0 %all-to-all-start.3 = ((bf16[128,2,2,1536]{3,2,1,0:T(2,128)(2,1)}), bf16[128,2,2,1536]{3,2,1,0:T(2,128)(2,1)S(1)}, u32[]{:S(2)}, u32[]{:S(2)}) async-start(bf16[128,2,2,1536]{3,2,1,0:T(2,128)(2,1)} %copy.41), calls=%async_computation.3 | async-start | bytes 3145728 | tf_op jit(solution)/shard_map/all_to_all | solution.py:106
where the time goes:
time: 197 us; the launch traced here: 196 us
  waiting for transfers between devices  115 us (58%)
  starting transfers between devices  40.1 us (20%)
  other arithmetic  24.3 us (12%)
  local copies, waits for them, and re-layouts  15 us (8%)
    all_to_all x1, waiting for transfers between devices, body(): lax.all_to_all(outgoing, 'tile', split_axis=0, concat_axis=0, tiled=True)  42.2 us
    all_to_all x1, waiting for transfers between devices, body(): lax.all_to_all(blocks, 'tile', split_axis=0, concat_axis=0, tiled=True)  25.7 us
    all_to_all x1, waiting for transfers between devices, body(): lax.all_to_all(picked, 'tile', split_axis=0, concat_axis=0, tiled=True)  25.6 us
    all_to_all x1, starting transfers between devices, body(): lax.all_to_all(blocks, 'tile', split_axis=0, concat_axis=0, tiled=True)  17.4 us
    ppermute x1, waiting for transfers between devices, with_halo(): lax.ppermute(lax.slice_in_dim(block, block.shape[dim] - width, None, axis...  16.8 us
    select_n x3, other arithmetic, correct_channel(): prod_one = jnp.where(inside[None, :, None], prod_one, 0.0)  7.42 us
    add x12, other arithmetic, smooth(): total + gauss_taps[k] * lax.slice_in_dim(padded, k, k + size, axis=axis)  7.2 us
    all_to_all x1, starting transfers between devices, body(): lax.all_to_all(outgoing, 'tile', split_axis=0, concat_axis=0, tiled=True)  6.32 us
  transfers between devices with their start and end apart: 6, of which 5 were waited for; matrix products, arithmetic and copies ran while one was open for 16% of the time, Pallas kernels for 0%

commit v1 on v0

v1 whole, which is shorter than its diff:
```python
import math

import jax
import jax.numpy as jnp
from jax import lax
from jax.experimental import pallas as pl
from jax.experimental.pallas import tpu as pltpu
from jax.sharding import PartitionSpec as P

CAP = 2
HALO = 3

gauss_raw = [math.exp(-0.5 * k * k) for k in range(-2, 3)]
gauss_taps = [w / sum(gauss_raw) for w in gauss_raw]

F32 = jnp.float32
BF16 = jnp.bfloat16


def dot(a, b):
    return jnp.dot(a, b, preferred_element_type=F32)


def iotas(rows, cols):
    return (
        lax.broadcasted_iota(jnp.int32, (rows, cols), 0),
        lax.broadcasted_iota(jnp.int32, (rows, cols), 1),
    )


def band(i, j):
    total = jnp.zeros(i.shape, F32)
    for k in range(5):
        total = jnp.where(i - j == k - 2, jnp.float32(gauss_taps[k]), total)
    high = total.astype(BF16)
    return high, (total - high.astype(F32)).astype(BF16)


def split(v):
    high = v.astype(BF16)
    return high, (v - high.astype(F32)).astype(BF16)


def correct_kernel(
    flags, own, own_lo, own_hi, fac, fac_lo, fac_hi, out, b, dxa, dxb, dya, dyb, deep
):
    rows, cols = own.shape[2:]
    depth = own.shape[1]
    wide = depth + 2 * HALO
    low, high, face = flags[0], flags[1], flags[2]

    def plane(mid, lo, hi, k):
        if k < HALO:
            return lo, k
        if k < HALO + depth:
            return mid, k - HALO
        return hi, k - HALO - depth

    i, j = iotas(cols, cols)
    half = jnp.float32(0.5)
    zero = jnp.float32(0.0)
    turn = jnp.where(i + j == cols - 1, face, zero)
    turned_dx = jnp.where(i + j == cols - 2, half * face, zero) - jnp.where(
        i + j == cols, half * face, zero
    )
    turn = jnp.concatenate([turn, turned_dx], axis=1).astype(BF16)
    across = (jnp.where(i == j + 1, half, zero) - jnp.where(i == j - 1, half, zero)).astype(BF16)
    g_hi, g_lo = band(i, j)
    smooth_x = jnp.concatenate(
        [
            jnp.concatenate([g_hi, g_lo], axis=1),
            jnp.concatenate([g_hi, jnp.zeros_like(g_lo)], axis=1),
        ],
        axis=0,
    )
    i, j = iotas(rows, rows)
    along = (jnp.where(j == i + 1, half, zero) - jnp.where(j == i - 1, half, zero)).astype(BF16)
    y_hi, y_lo = band(i, j)
    smooth_y = jnp.concatenate([y_hi, y_lo], axis=0)

    for k in range(wide):
        ref, at = plane(fac, fac_lo, fac_hi, k)
        both = dot(ref[0, at], turn)
        b[k] = both[:, :cols]
        if 0 < k < wide - 1:
            dxb[k - 1] = both[:, cols:]
            ref, at = plane(own, own_lo, own_hi, k)
            a = ref[0, at]
            dxa[k - 1] = dot(a, across)
            dy = dot(along, jnp.concatenate([a, both[:, :cols].astype(BF16)], axis=1))
            dya[k - 1] = dy[:, :cols]
            dyb[k - 1] = dy[:, cols:]

    step = 32

    def chunk(r, carry):
        at_rows = pl.ds(pl.multiple_of(r * step, step), step)

        def a_of(k):
            ref, at = plane(own, own_lo, own_hi, k)
            return ref[0, at, at_rows, :].astype(F32)

        one = [jnp.zeros((step, cols), F32) for _ in range(depth)]
        two = [jnp.zeros((step, cols), F32) for _ in range(depth)]
        for k in range(1, wide - 1):
            av, bv = a_of(k), b[k, at_rows, :]
            dza = (a_of(k + 1) - a_of(k - 1)) * half
            dzb = (b[k + 1, at_rows, :] - b[k - 1, at_rows, :]) * half
            ya, yb = dya[k - 1, at_rows, :], dyb[k - 1, at_rows, :]
            xa, xb = dxa[k - 1, at_rows, :], dxb[k - 1, at_rows, :]
            p1 = av * bv + ya * yb + dza * dzb + xa * xb
            p2 = bv * bv + yb * yb + dzb * dzb + xb * xb
            if k < HALO:
                p1, p2 = p1 * low, p2 * low
            if k >= HALO + depth:
                p1, p2 = p1 * high, p2 * high
            for z in range(depth):
                tap = k - (HALO + z) + 2
                if 0 <= tap < 5:
                    one[z] = one[z] + gauss_taps[tap] * p1
                    two[z] = two[z] + gauss_taps[tap] * p2
        for z in range(depth):
            for s, v in ((0, one[z]), (1, two[z])):
                h, l = split(v)
                deep[2 * z + s, at_rows, :cols] = h
                deep[2 * z + s, at_rows, cols:] = l
        return carry

    lax.fori_loop(0, rows // step, chunk, 0)

    for z in range(depth):
        parts = []
        for s in range(2):
            r = dot(deep[2 * z + s], smooth_x)
            parts.append(split(r[:, :cols] + r[:, cols:]))
        r_hi = jnp.concatenate([parts[0][0], parts[1][0]], axis=1)
        r_lo = jnp.concatenate([parts[0][1], parts[1][1]], axis=1)
        main = dot(smooth_y, r_hi)
        q = main[:rows] + main[rows:] + dot(y_hi, r_lo)
        a = own[0, z].astype(F32)
        out[0, z] = (a * (q[:, :cols] + 1.0) / (q[:, cols:] + 1.0)).astype(BF16)


def correct(flags, own, own_lo, own_hi, fac, fac_lo, fac_hi):
    chans, depth, rows, cols = own.shape
    wide = depth + 2 * HALO

    def spec(n):
        return pl.BlockSpec((1, n, rows, cols), lambda c: (c, 0, 0, 0))

    def vmem(n):
        return pltpu.VMEM((n, rows, cols), F32)

    return pl.pallas_call(
        correct_kernel,
        grid=(chans,),
        in_specs=[pl.BlockSpec(memory_space=pltpu.SMEM)]
        + [spec(depth), spec(HALO), spec(HALO)] * 2,
        out_specs=spec(depth),
        out_shape=jax.ShapeDtypeStruct(own.shape, BF16),
        scratch_shapes=[
            vmem(wide),
            vmem(wide - 2),
            vmem(wide - 2),
            vmem(wide - 2),
            vmem(wide - 2),
            pltpu.VMEM((2 * depth, rows, 2 * cols), BF16),
        ],
        compiler_params=pltpu.CompilerParams(vmem_limit_bytes=24 << 20),
        name="correct",
    )(flags, own, own_lo, own_hi, fac, fac_lo, fac_hi)


def pack_kernel(code, planes, out):
    count, rows, cols = planes.shape
    step = 256
    for m in range(out.shape[0] // step):
        i = lax.broadcasted_iota(jnp.int32, (step, 2 * rows), 0) + m * step
        pick = jnp.where(i == code[...], jnp.float32(1.0), jnp.float32(0.0)).astype(BF16)
        for n in range(count // 4):
            left = planes[4 * n : 4 * n + 2].reshape(2 * rows, cols)
            right = planes[4 * n + 2 : 4 * n + 4].reshape(2 * rows, cols)
            v = dot(pick, jnp.concatenate([left, right], axis=1))
            out[m * step : (m + 1) * step, 2 * n * cols : 2 * (n + 1) * cols] = v.astype(BF16)


def pack(code, planes, blocks):
    count, rows, cols = planes.shape
    return pl.pallas_call(
        pack_kernel,
        out_shape=jax.ShapeDtypeStruct((blocks * 8, count // 2 * cols), BF16),
        compiler_params=pltpu.CompilerParams(vmem_limit_bytes=16 << 20),
        name="pack",
    )(code, planes)


def join_kernel(code, got, out):
    count, rows, cols = out.shape
    lines = got.shape[0]
    i = lax.broadcasted_iota(jnp.int32, (rows, lines), 0)
    one, zero = jnp.float32(1.0), jnp.float32(0.0)
    counts = None
    for h in range(2):
        place = jnp.where(i == code[h : h + 1, :], one, zero).astype(BF16)
        if h == 0:
            counts = dot(place, jnp.ones((lines, cols), BF16))
            counts = jnp.maximum(counts, 1.0)
        for n in range(count // 4):
            v = dot(place, got[:, 2 * n * cols : 2 * (n + 1) * cols])
            out[4 * n + h] = (v[:, :cols] / counts).astype(BF16)
            out[4 * n + 2 + h] = (v[:, cols:] / counts).astype(BF16)


def join(code, got, rows, cols):
    count = got.shape[1] // cols * 2
    return pl.pallas_call(
        join_kernel,
        out_shape=jax.ShapeDtypeStruct((count, rows, cols), BF16),
        compiler_params=pltpu.CompilerParams(vmem_limit_bytes=16 << 20),
        name="join",
    )(code, got)


def halo(block):
    count = lax.axis_size("gz")
    forward = [(i, i + 1) for i in range(count - 1)]
    backward = [(i + 1, i) for i in range(count - 1)]
    depth = block.shape[1]
    low = lax.ppermute(block[:, depth - HALO :], "gz", forward)
    high = lax.ppermute(block[:, :HALO], "gz", backward)
    return low, high


def swap(blocks):
    return lax.all_to_all(blocks, "tile", split_axis=0, concat_axis=0, tiled=True)


def body(images, partner, dest, offset, extent):
    ntile = lax.axis_size("tile")
    tile = lax.axis_index("tile")
    plane_idx = lax.axis_index("gz")
    nplane = lax.axis_size("gz")
    rows, chans, depth, cols = images.shape
    lines = chans * depth * rows
    own = jnp.transpose(images, (1, 2, 0, 3))
    own = lax.optimization_barrier(own)
    own_lo, own_hi = halo(own)
    spread = swap(own.reshape(ntile, lines // ntile, cols))
    picked = jnp.take(spread, partner, axis=0, mode="clip")
    fac = swap(picked).reshape(chans, depth, rows, cols)

    targets = dest[:, 0]
    order_idx = jnp.arange(ntile, dtype=jnp.int32)
    same_owner = targets[:, None] == targets[None, :]
    earlier = order_idx[:, None] > order_idx[None, :]
    slot = jnp.sum((same_owner & earlier).astype(jnp.int32), axis=1)
    slots = jnp.arange(CAP, dtype=jnp.int32)
    select = (order_idx[:, None, None] == targets[None, None, :]) & (
        slots[None, :, None] == slot[None, None, :]
    )
    label = offset * 4 + extent
    labels = jnp.sum(jnp.where(select, label[None, None, :], 0), axis=2)
    within = jnp.arange(2, dtype=jnp.int32)
    code = (targets * 8 + slot * 2)[:, None] + within[None, :]
    code = code.reshape(1, rows)
    code = jnp.concatenate([code, code + 4], axis=1)

    fac, labels = lax.optimization_barrier((fac, labels))
    fac_lo, fac_hi = halo(fac)
    info = swap(labels)

    flags = jnp.stack(
        [plane_idx > 0, plane_idx < nplane - 1, partner[tile] != tile]
    ).astype(F32)
    corrected = correct(flags, own, own_lo, own_hi, fac, fac_lo, fac_hi)
    planes = corrected.reshape(chans * depth, rows, cols)
    outgoing = pack(code, planes, ntile)
    received = swap(outgoing.reshape(ntile, 8, outgoing.shape[1]))

    start, span = info // 4, info % 4
    spots = jnp.where(within < span[:, :, None], start[:, :, None] + within, -1)
    spots = spots.reshape(ntile, 2 * CAP)
    none = jnp.full_like(spots, -1)
    code_in = jnp.stack(
        [
            jnp.concatenate([spots, none], axis=1).reshape(-1),
            jnp.concatenate([none, spots], axis=1).reshape(-1),
        ]
    )
    joined = join(code_in, received.reshape(ntile * 8, -1), rows, cols)

    def home(v):
        return jnp.transpose(v.reshape(chans, depth, rows, cols), (2, 0, 1, 3))

    return home(corrected), home(joined)


def solution(mesh):
    in_specs = (P("tile", None, "gz", None), P(), P("tile", None), P("tile"), P("tile"))
    out_specs = (P("tile", None, "gz", None), P("tile", None, "gz", None))
    return jax.shard_map(body, mesh=mesh, in_specs=in_specs, out_specs=out_specs, check_vma=False)
```

time: 197 us -> 170 us (0.86)
  other arithmetic: 24.3 us -> 0.64 us
  waiting for transfers between devices: 115 us -> 91.5 us
  Pallas kernels: 0 us -> 15.1 us
  starting transfers between devices: 40.1 us -> 44.9 us
    pallas_call x0 -> x3, Pallas kernels: none -> 15.1 us  [the longest x1 13.1 us: correct(): pl.pallas_call(correct_kernel, grid=(chans,), in_specs=[pl.BlockSpec(memo...]
    ppermute x2 -> x4, waiting for transfers between devices: 21 us -> 8.44 us  [the longest x2 4.4 us: halo(): low = lax.ppermute(block[:, depth - HALO:], 'gz', forward)]
    all_to_all x4, waiting for transfers between devices: 93.5 us -> 83.1 us  [swap(): lax.all_to_all(blocks, 'tile', split_axis=0, concat_axis=0, tiled=True)]
    select_n x5 -> x2, other arithmetic: 9.03 us -> 0.14 us  [the longest x1 0.08 us: body(): spots = jnp.where(within < span[:, :, None], start[:, :, None] + within, -1)]
    add x13 -> x4, other arithmetic: 7.22 us -> 0.09 us  [the longest x2 0.08 us: body(): code = (targets * 8 + slot * 2)[:, None] + within[None, :]]
    unnamed x22 -> x17, local copies, waits for them, and re-layouts: 1.07 us -> 6.83 us
    another operation x5 -> x1, other arithmetic: 5.03 us -> 0.01 us  [body(): jnp.stack([jnp.concatenate([spots, none], axis=1).reshape(-1), jnp.concat...]
    ppermute x2 -> x4, starting transfers between devices: 4.75 us -> 9.42 us  [the longest x2 6.84 us: halo(): low = lax.ppermute(block[:, depth - HALO:], 'gz', forward)]
  transfers between devices with their start and end apart: 6 -> 8, of which waited for: 5 -> 5; matrix products, arithmetic and copies ran while one was open for 16% -> 5% of each run, Pallas kernels for 0% -> 8%
where the time goes in v1:
time: 170 us; the launch traced here: 169 us
  waiting for transfers between devices  91.5 us (54%)
  starting transfers between devices  44.9 us (26%)
  local copies, waits for them, and re-layouts  15.5 us (9%)
  Pallas kernels  15.1 us (9%)
    all_to_all x4, waiting for transfers between devices, swap(): lax.all_to_all(blocks, 'tile', split_axis=0, concat_axis=0, tiled=True)  83.1 us
    all_to_all x4, starting transfers between devices, swap(): lax.all_to_all(blocks, 'tile', split_axis=0, concat_axis=0, tiled=True)  35.5 us
    pallas_call x1, Pallas kernels, correct(): pl.pallas_call(correct_kernel, grid=(chans,), in_specs=[pl.BlockSpec(memo...  13.1 us
    ppermute x2, starting transfers between devices, halo(): low = lax.ppermute(block[:, depth - HALO:], 'gz', forward)  6.84 us
    unnamed x17, local copies, waits for them, and re-layouts  6.83 us
    ppermute x2, waiting for transfers between devices, halo(): low = lax.ppermute(block[:, depth - HALO:], 'gz', forward)  4.4 us
    ppermute x2, waiting for transfers between devices, halo(): high = lax.ppermute(block[:, :HALO], 'gz', backward)  4.05 us
    slice x2, local copies, waits for them, and re-layouts, halo(): high = lax.ppermute(block[:, :HALO], 'gz', backward)  3.62 us
  transfers between devices with their start and end apart: 8, of which 5 were waited for; matrix products, arithmetic and copies ran while one was open for 5% of the time, Pallas kernels for 8%

profile of v1, /device:TPU:8, one launch (start us, length us, event | category | flops | bytes accessed | tf_op | source)
XLA Modules:
  0.0 169.3 jit_solution(15097329478502880045)
XLA Ops:
  0.6 2.2 %copy.35 = bf16[256,3,4,128]{3,0,2,1:T(8,128)(2,1)} copy(bf16[256,3,4,128]{3,2,1,0:T(4,128)(2,1)} %param.5) | data formatting | bytes 1572864 | tf_op args[0]
  2.8 17.4 %all-to-all-start = ((bf16[128,24,128]{2,1,0:T(8,128)(2,1)}), bf16[128,24,128]{2,1,0:T(8,128)(2,1)S(1)}, u32[]{:S(2)}, u32[]{:S(2)}) async-start(bf16[128,24,128]{2,1,0:T(8,128)(2,1)} %bitcast.5), calls=%async_computation | async-start | bytes 1572864 | tf_op jit(solution)/shard_map/all_to_all | solution.py:235
  20.2 25.7 %all-to-all-done = bf16[128,24,128]{2,1,0:T(8,128)(2,1)S(1)} async-done(((bf16[128,24,128]{2,1,0:T(8,128)(2,1)}), bf16[128,24,128]{2,1,0:T(8,128)(2,1)S(1)}, u32[]{:S(2)}, u32[]{:S(2)}) %all-to-all-start) | async-done | bytes 786464 | tf_op jit(solution)/shard_map/all_to_all | solution.py:235
  45.9 1.6 gather_fusion
  47.5 5.8 %all-to-all-start.1 = ((bf16[128,24,128]{2,1,0:T(8,128)(2,1)}), bf16[128,24,128]{2,1,0:T(8,128)(2,1)S(1)}, u32[]{:S(2)}, u32[]{:S(2)}) async-start(bf16[128,24,128]{2,1,0:T(8,128)(2,1)} %gather_fusion), calls=%async_computation.1 | async-start | bytes 1572864 | tf_op jit(solution)/shard_map/all_to_all | solution.py:235
  53.3 0.0 copy-start.4
  53.3 0.0 copy-start.5
  53.3 0.0 copy-start.6
  53.4 2.4 %fusion.5 = (bf16[3,3,256,128]{3,2,1,0:T(8,128)(2,1)}, bf16[3,3,256,128]{3,2,1,0:T(8,128)(2,1)}) fusion(bf16[3,4,256,128]{3,2,1,0:T(8,128)(2,1)} %bitcast.27.own), kind=kLoop, calls=%fused_computation.28 | loop fusion | bytes 2359296 | tf_op jit(solution)/shard_map/slice | solution.py:230
  55.8 3.4 %collective-permute-start = (bf16[3,3,256,128]{3,2,1,0:T(8,128)(2,1)}, bf16[3,3,256,128]{3,2,1,0:T(8,128)(2,1)S(1)}, u32[]{:S(2)}, u32[]{:S(2)}) collective-permute-start(bf16[3,3,256,128]{3,2,1,0:T(8,128)(2,1)} %get-tuple-element.17), channel_id=1, source_target_pairs={{0,1},{1,2},{2,3},{4,5},{5,6},{6,7},{8,9},{9,10},{10,11},{12,13},{... | collective-permute-start | bytes 1769480 | tf_op jit(solution)/shard_map/ppermute | solution.py:229
  59.2 1.3 collective-permute-start.1
  60.5 0.6 dynamic_slice.3
  61.7 0.2 convert_reduce_fusion
  61.9 0.0 copy-done.5
  62.0 0.1 select_reduce_fusion
  62.1 17.0 %all-to-all-done.1 = bf16[128,24,128]{2,1,0:T(8,128)(2,1)S(1)} async-done(((bf16[128,24,128]{2,1,0:T(8,128)(2,1)}), bf16[128,24,128]{2,1,0:T(8,128)(2,1)S(1)}, u32[]{:S(2)}, u32[]{:S(2)}) %all-to-all-start.1) | async-done | bytes 786464 | tf_op jit(solution)/shard_map/all_to_all | solution.py:235
  79.1 1.2 fusion.4
  80.3 3.4 %collective-permute-start.2 = (bf16[3,3,256,128]{3,2,1,0:T(8,128)(2,1)}, bf16[3,3,256,128]{3,2,1,0:T(8,128)(2,1)S(1)}, u32[]{:S(2)}, u32[]{:S(2)}) collective-permute-start(bf16[3,3,256,128]{3,2,1,0:T(8,128)(2,1)} %get-tuple-element.15), channel_id=1, source_target_pairs={{0,1},{1,2},{2,3},{4,5},{5,6},{6,7},{8,9},{9,10},{10,11},{12,13},{... | collective-permute-start | bytes 1769480 | tf_op jit(solution)/shard_map/ppermute | solution.py:229
  83.7 1.3 collective-permute-start.3
  85.0 0.1 iota_add_fusion
  85.1 0.1 add.98
  85.3 0.7 copy.23
  86.0 5.8 %all-to-all-start.2 = ((s32[128,1,2]{2,1,0:T(1,128)}), s32[128,1,2]{2,1,0:T(1,128)S(1)}, u32[]{:S(2)}, u32[]{:S(2)}) async-start(s32[128,1,2]{2,1,0:T(1,128)} %copy.23), calls=%async_computation.2 | async-start | bytes 131072 | tf_op jit(solution)/shard_map/all_to_all | solution.py:235
  91.8 0.1 add_convert_fusion.flags
  91.9 0.0 collective-permute-done.own_lo
  91.9 0.0 collective-permute-done.1.own_hi
  91.9 4.4 %collective-permute-done.2.fac_lo = bf16[3,3,256,128]{3,2,1,0:T(8,128)(2,1)S(1)} collective-permute-done((bf16[3,3,256,128]{3,2,1,0:T(8,128)(2,1)}, bf16[3,3,256,128]{3,2,1,0:T(8,128)(2,1)S(1)}, u32[]{:S(2)}, u32[]{:S(2)}) %collective-permute-start.2) | collective-permute-done | bytes 589856 | tf_op jit(solution)/shard_map/ppermute | solution.py:229
  96.3 4.0 %collective-permute-done.3.fac_hi = bf16[3,3,256,128]{3,2,1,0:T(8,128)(2,1)S(1)} collective-permute-done((bf16[3,3,256,128]{3,2,1,0:T(8,128)(2,1)}, bf16[3,3,256,128]{3,2,1,0:T(8,128)(2,1)S(1)}, u32[]{:S(2)}, u32[]{:S(2)}) %collective-permute-start.3) | collective-permute-done | bytes 589856 | tf_op jit(solution)/shard_map/ppermute | solution.py:230
  100.4 0.8 copy-done.1
  101.2 1.1 copy-done.2
  102.2 13.1 %correct.1 = bf16[3,4,256,128]{3,2,1,0:T(8,128)(2,1)S(1)} custom-call(f32[3]{0:T(128)S(1)} %add_convert_fusion.flags, bf16[3,4,256,128]{3,2,1,0:T(8,128)(2,1)} %bitcast.27.own, bf16[3,3,256,128]{3,2,1,0:T(8,128)(2,1)S(1)} %collective-permute-done.own_lo, bf16[3,3,256,128]{3,2,1,0:T(8,128)(2,1)S(1)} %collective-permute-done.1.own_hi, ...), custom_call_target="tpu_custom_call" | custom-call | tf_op jit(solution)/shard_map/correct/pallas_call | solution.py:154
  115.3 1.0 pack.1
  116.3 1.2 copy-done
  117.5 0.0 all-to-all-done.2
  117.5 6.5 %all-to-all-start.3 = ((bf16[128,8,768]{2,1,0:T(8,128)(2,1)}), bf16[128,8,768]{2,1,0:T(8,128)(2,1)S(1)}, u32[]{:S(2)}, u32[]{:S(2)}) async-start(bf16[128,8,768]{2,1,0:T(8,128)(2,1)} %bitcast.33), calls=%async_computation.3 | async-start | bytes 3145728 | tf_op jit(solution)/shard_map/all_to_all | solution.py:235
  124.0 0.1 lt.41
  124.1 0.1 add_select_fusion.1
  124.1 0.1 copy.24
  124.2 0.1 copy.25
  124.3 0.1 add_select_fusion.2
  124.4 0.1 copy.30
  124.5 0.1 fusion.6
  124.6 0.1 stack_reshape.6
  124.7 0.1 stack_reshape.7
  124.8 1.5 copy.29
  126.3 40.4 %all-to-all-done.3 = bf16[128,8,768]{2,1,0:T(8,128)(2,1)S(1)} async-done(((bf16[128,8,768]{2,1,0:T(8,128)(2,1)}), bf16[128,8,768]{2,1,0:T(8,128)(2,1)S(1)}, u32[]{:S(2)}, u32[]{:S(2)}) %all-to-all-start.3) | async-done | bytes 1572896 | tf_op jit(solution)/shard_map/all_to_all | solution.py:235
  166.7 1.1 join.1
  167.8 1.5 copy.34
  (18 shorter events, 0.1 us)
Async XLA Ops:
  0.6 19.5 %copy-start.3 = (s32[128]{0:T(128)S(1)}, s32[128]{0:T(128)}, u32[]{:S(2)}) copy-start(s32[128]{0:T(128)} %param.6) | copy-start | bytes 1540
  2.8 43.1 %all-to-all-start = ((bf16[128,24,128]{2,1,0:T(8,128)(2,1)}), bf16[128,24,128]{2,1,0:T(8,128)(2,1)S(1)}, u32[]{:S(2)}, u32[]{:S(2)}) async-start(bf16[128,24,128]{2,1,0:T(8,128)(2,1)} %bitcast.5), calls=%async_computation | async-start | bytes 1572864 | tf_op jit(solution)/shard_map/all_to_all | solution.py:235
  47.5 31.6 %all-to-all-start.1 = ((bf16[128,24,128]{2,1,0:T(8,128)(2,1)}), bf16[128,24,128]{2,1,0:T(8,128)(2,1)S(1)}, u32[]{:S(2)}, u32[]{:S(2)}) async-start(bf16[128,24,128]{2,1,0:T(8,128)(2,1)} %gather_fusion), calls=%async_computation.1 | async-start | bytes 1572864 | tf_op jit(solution)/shard_map/all_to_all | solution.py:235
  53.3 8.4 %copy-start.4 = (s32[128,1]{0,1:T(1,128)S(1)}, s32[128,1]{0,1:T(1,128)}, u32[]{:S(2)}) copy-start(s32[128,1]{0,1:T(1,128)} %param.7) | copy-start | bytes 1540
  53.3 8.6 %copy-start.5 = (s32[128]{0:T(128)S(1)}, s32[128]{0:T(128)}, u32[]{:S(2)}) copy-start(s32[128]{0:T(128)} %param.9) | copy-start | bytes 1540
  53.3 8.6 %copy-start.6 = (s32[128]{0:T(128)S(1)}, s32[128]{0:T(128)}, u32[]{:S(2)}) copy-start(s32[128]{0:T(128)} %param.8) | copy-start | bytes 1540
  55.8 36.2 %collective-permute-start = (bf16[3,3,256,128]{3,2,1,0:T(8,128)(2,1)}, bf16[3,3,256,128]{3,2,1,0:T(8,128)(2,1)S(1)}, u32[]{:S(2)}, u32[]{:S(2)}) collective-permute-start(bf16[3,3,256,128]{3,2,1,0:T(8,128)(2,1)} %get-tuple-element.17), channel_id=1, source_target_pairs={{0,1},{1,2},{2,3},{4,5},{5,6},{6,7},{8,9},{9,10},{10,11},{12,13},{... | collective-permute-start | bytes 1769480 | tf_op jit(solution)/shard_map/ppermute | solution.py:229
  59.2 32.7 %collective-permute-start.1 = (bf16[3,3,256,128]{3,2,1,0:T(8,128)(2,1)}, bf16[3,3,256,128]{3,2,1,0:T(8,128)(2,1)S(1)}, u32[]{:S(2)}, u32[]{:S(2)}) collective-permute-start(bf16[3,3,256,128]{3,2,1,0:T(8,128)(2,1)} %get-tuple-element.16), channel_id=1, source_target_pairs={{1,0},{2,1},{3,2},{5,4},{6,5},{7,6},{9,8},{10,9},{11,10},{13,12},{... | collective-permute-start | bytes 1769480 | tf_op jit(solution)/shard_map/ppermute | solution.py:230
  80.3 16.0 %collective-permute-start.2 = (bf16[3,3,256,128]{3,2,1,0:T(8,128)(2,1)}, bf16[3,3,256,128]{3,2,1,0:T(8,128)(2,1)S(1)}, u32[]{:S(2)}, u32[]{:S(2)}) collective-permute-start(bf16[3,3,256,128]{3,2,1,0:T(8,128)(2,1)} %get-tuple-element.15), channel_id=1, source_target_pairs={{0,1},{1,2},{2,3},{4,5},{5,6},{6,7},{8,9},{9,10},{10,11},{12,13},{... | collective-permute-start | bytes 1769480 | tf_op jit(solution)/shard_map/ppermute | solution.py:229
  83.7 16.6 %collective-permute-start.3 = (bf16[3,3,256,128]{3,2,1,0:T(8,128)(2,1)}, bf16[3,3,256,128]{3,2,1,0:T(8,128)(2,1)S(1)}, u32[]{:S(2)}, u32[]{:S(2)}) collective-permute-start(bf16[3,3,256,128]{3,2,1,0:T(8,128)(2,1)} %get-tuple-element.14), channel_id=1, source_target_pairs={{1,0},{2,1},{3,2},{5,4},{6,5},{7,6},{9,8},{10,9},{11,10},{13,12},{... | collective-permute-start | bytes 1769480 | tf_op jit(solution)/shard_map/ppermute | solution.py:230
  86.0 31.5 %all-to-all-start.2 = ((s32[128,1,2]{2,1,0:T(1,128)}), s32[128,1,2]{2,1,0:T(1,128)S(1)}, u32[]{:S(2)}, u32[]{:S(2)}) async-start(s32[128,1,2]{2,1,0:T(1,128)} %copy.23), calls=%async_computation.2 | async-start | bytes 131072 | tf_op jit(solution)/shard_map/all_to_all | solution.py:235
  100.4 0.8 copy-start.1
  101.2 1.1 copy-start.2
  116.3 1.2 copy-start
  117.5 49.2 %all-to-all-start.3 = ((bf16[128,8,768]{2,1,0:T(8,128)(2,1)}), bf16[128,8,768]{2,1,0:T(8,128)(2,1)S(1)}, u32[]{:S(2)}, u32[]{:S(2)}) async-start(bf16[128,8,768]{2,1,0:T(8,128)(2,1)} %bitcast.33), calls=%async_computation.3 | async-start | bytes 3145728 | tf_op jit(solution)/shard_map/all_to_all | solution.py:235

commit v2 on v1

v2 whole, which is shorter than its diff:
```python
import functools
import math

import jax
import jax.numpy as jnp
from jax import lax
from jax.experimental import pallas as pl
from jax.experimental.pallas import tpu as pltpu
from jax.sharding import PartitionSpec as P

CAP = 2
HALO = 3

gauss_raw = [math.exp(-0.5 * k * k) for k in range(-2, 3)]
gauss_taps = [w / sum(gauss_raw) for w in gauss_raw]

F32 = jnp.float32
BF16 = jnp.bfloat16


def dot(a, b):
    return jnp.dot(a, b, preferred_element_type=F32)


def iotas(rows, cols):
    return (
        lax.broadcasted_iota(jnp.int32, (rows, cols), 0),
        lax.broadcasted_iota(jnp.int32, (rows, cols), 1),
    )


def band(i, j):
    total = jnp.zeros(i.shape, F32)
    for k in range(5):
        total = jnp.where(i - j == k - 2, jnp.float32(gauss_taps[k]), total)
    high = total.astype(BF16)
    return high, (total - high.astype(F32)).astype(BF16)


def split(v):
    high = v.astype(BF16)
    return high, (v - high.astype(F32)).astype(BF16)


def matrices(rows, cols, face):
    i, j = iotas(cols, cols)
    half = jnp.float32(0.5)
    zero = jnp.float32(0.0)
    turn = jnp.where(i + j == cols - 1, face, zero)
    turned_dx = jnp.where(i + j == cols - 2, half * face, zero) - jnp.where(
        i + j == cols, half * face, zero
    )
    turn = jnp.concatenate([turn, turned_dx], axis=1).astype(BF16)
    across = (jnp.where(i == j + 1, half, zero) - jnp.where(i == j - 1, half, zero)).astype(BF16)
    g_hi, g_lo = band(i, j)
    smooth_x = jnp.concatenate(
        [
            jnp.concatenate([g_hi, g_lo], axis=1),
            jnp.concatenate([g_hi, jnp.zeros_like(g_lo)], axis=1),
        ],
        axis=0,
    )
    i, j = iotas(rows, rows)
    along = (jnp.where(j == i + 1, half, zero) - jnp.where(j == i - 1, half, zero)).astype(BF16)
    smooth_y = jnp.concatenate(band(i, j), axis=0)
    return turn, across, along, smooth_x, smooth_y


def prepare_kernel(across, along, own, own_lo, own_hi, a10, dxa, dya):
    depth, _, rows, cols = own.shape
    for k in range(depth + 2 * HALO):
        if k < HALO:
            a = own_lo[k, 0]
        elif k < HALO + depth:
            a = own[k - HALO, 0]
        else:
            a = own_hi[k - HALO - depth, 0]
        a10[0, k] = a
        if 0 < k < depth + 2 * HALO - 1:
            dxa[0, k - 1] = dot(a, across[...])
            if k % 2 == 0:
                dy = dot(along[...], jnp.concatenate([before, a], axis=1))
                dya[0, k - 2] = dy[:, :cols]
                dya[0, k - 1] = dy[:, cols:]
        before = a


def prepare(across, along, own, own_lo, own_hi):
    depth, chans, rows, cols = own.shape
    wide = depth + 2 * HALO

    def spec(n):
        return pl.BlockSpec((n, 1, rows, cols), lambda c: (0, c, 0, 0))

    def result(n):
        return pl.BlockSpec((1, n, rows, cols), lambda c: (c, 0, 0, 0))

    def whole(m):
        return pl.BlockSpec(m.shape, lambda c: (0, 0))

    def shape(n, dtype):
        return jax.ShapeDtypeStruct((chans, n, rows, cols), dtype)

    return pl.pallas_call(
        prepare_kernel,
        grid=(chans,),
        in_specs=[whole(across), whole(along), spec(depth), spec(HALO), spec(HALO)],
        out_specs=[result(wide), result(wide - 2), result(wide - 2)],
        out_shape=[shape(wide, BF16), shape(wide - 2, F32), shape(wide - 2, F32)],
        compiler_params=pltpu.CompilerParams(vmem_limit_bytes=10 << 20),
        name="prepare",
    )(across, along, own, own_lo, own_hi)


def correct_kernel(
    chan,
    flags,
    turn,
    along,
    smooth_x,
    smooth_y,
    a10_far,
    dxa_far,
    dya_far,
    fac,
    fac_lo,
    fac_hi,
    out,
    b,
    dxb,
    dyb,
    deep,
    a10,
    dxa,
    dya,
    sems,
):
    depth, _, rows, cols = fac.shape
    wide = depth + 2 * HALO
    fetches = [
        pltpu.make_async_copy(far.at[chan], near, sems.at[n])
        for n, (far, near) in enumerate(((a10_far, a10), (dxa_far, dxa), (dya_far, dya)))
    ]
    for fetch in fetches:
        fetch.start()
    low, high = flags[0], flags[1]
    half = jnp.float32(0.5)
    for k in range(wide):
        if k < HALO:
            f = fac_lo[k]
        elif k < HALO + depth:
            f = fac[k - HALO, chan]
        else:
            f = fac_hi[k - HALO - depth]
        both = dot(f, turn[...])
        b[k] = both[:, :cols]
        now = both[:, :cols].astype(BF16)
        if 0 < k < wide - 1:
            dxb[k - 1] = both[:, cols:]
            if k % 2 == 0:
                dy = dot(along[...], jnp.concatenate([before, now], axis=1))
                dyb[k - 2] = dy[:, :cols]
                dyb[k - 1] = dy[:, cols:]
        before = now
    for fetch in fetches:
        fetch.wait()

    step = 32

    def chunk(r, carry):
        at_rows = pl.ds(pl.multiple_of(r * step, step), step)

        def a_of(k):
            return a10[k, at_rows, :].astype(F32)

        one = [jnp.zeros((step, cols), F32) for _ in range(depth)]
        two = [jnp.zeros((step, cols), F32) for _ in range(depth)]
        for k in range(1, wide - 1):
            av, bv = a_of(k), b[k, at_rows, :]
            dza = (a_of(k + 1) - a_of(k - 1)) * half
            dzb = (b[k + 1, at_rows, :] - b[k - 1, at_rows, :]) * half
            ya, yb = dya[k - 1, at_rows, :], dyb[k - 1, at_rows, :]
            xa, xb = dxa[k - 1, at_rows, :], dxb[k - 1, at_rows, :]
            p1 = av * bv + ya * yb + dza * dzb + xa * xb
            p2 = bv * bv + yb * yb + dzb * dzb + xb * xb
            if k < HALO:
                p1, p2 = p1 * low, p2 * low
            if k >= HALO + depth:
                p1, p2 = p1 * high, p2 * high
            for z in range(depth):
                tap = k - (HALO + z) + 2
                if 0 <= tap < 5:
                    one[z] = one[z] + gauss_taps[tap] * p1
                    two[z] = two[z] + gauss_taps[tap] * p2
        for z in range(depth):
            for s, v in ((0, one[z]), (1, two[z])):
                h, l = split(v)
                deep[2 * z + s, at_rows, :cols] = h
                deep[2 * z + s, at_rows, cols:] = l
        return carry

    lax.fori_loop(0, rows // step, chunk, 0)

    for z in range(depth):
        parts = []
        for s in range(2):
            r = dot(deep[2 * z + s], smooth_x[...])
            parts.append(split(r[:, :cols] + r[:, cols:]))
        r_hi = jnp.concatenate([parts[0][0], parts[1][0]], axis=1)
        r_lo = jnp.concatenate([parts[0][1], parts[1][1]], axis=1)
        main = dot(smooth_y[...], r_hi)
        q = main[:rows] + main[rows:] + dot(smooth_y[:rows], r_lo)
        a = a10[z + HALO].astype(F32)
        out[z] = (a * (q[:, :cols] + 1.0) / (q[:, cols:] + 1.0)).astype(BF16)


def correct(chan, flags, turn, along, smooth_x, smooth_y, a10, dxa, dya, fac, fac_lo, fac_hi):
    depth, _, rows, cols = fac.shape
    wide = depth + 2 * HALO

    def vmem(n):
        return pltpu.VMEM((n, rows, cols), F32)

    near = pl.BlockSpec(memory_space=pltpu.VMEM)
    far = pl.BlockSpec(memory_space=pltpu.HBM)
    return pl.pallas_call(
        functools.partial(correct_kernel, chan),
        in_specs=[pl.BlockSpec(memory_space=pltpu.SMEM)] + [near] * 4 + [far] * 3 + [near] * 3,
        out_specs=near,
        out_shape=jax.ShapeDtypeStruct((depth, rows, cols), BF16),
        scratch_shapes=[
            vmem(wide),
            vmem(wide - 2),
            vmem(wide - 2),
            pltpu.VMEM((2 * depth, rows, 2 * cols), BF16),
            pltpu.VMEM((wide, rows, cols), BF16),
            vmem(wide - 2),
            vmem(wide - 2),
            pltpu.SemaphoreType.DMA((3,)),
        ],
        compiler_params=pltpu.CompilerParams(vmem_limit_bytes=12 << 20),
        cost_estimate=pl.CostEstimate(
            flops=2000000000, bytes_accessed=12000000, transcendentals=0
        ),
        name="correct",
    )(flags, turn, along, smooth_x, smooth_y, a10, dxa, dya, fac, fac_lo, fac_hi)


def pack_kernel(code, first, second, third, out, held, sems):
    rows, cols = first.shape[1:]
    step = held.shape[0] // sems.shape[0]
    copies = []
    for m in range(sems.shape[0]):
        at = pl.ds(m * step, step)
        i = lax.broadcasted_iota(jnp.int32, (step, 2 * rows), 0) + m * step
        pick = jnp.where(i == code[...], jnp.float32(1.0), jnp.float32(0.0)).astype(BF16)
        for n, planes in enumerate((first, second, third)):
            left = planes[0:2].reshape(2 * rows, cols)
            right = planes[2:4].reshape(2 * rows, cols)
            v = dot(pick, jnp.concatenate([left, right], axis=1))
            held[m * step : (m + 1) * step, 2 * n * cols : 2 * (n + 1) * cols] = v.astype(BF16)
        copies.append(pltpu.make_async_copy(held.at[at], out.at[at], sems.at[m]))
        copies[-1].start()
    for copy in copies:
        copy.wait()


def pack(code, planes, blocks):
    depth, rows, cols = planes[0].shape
    shape = (blocks * 8, len(planes) * depth // 2 * cols)
    return pl.pallas_call(
        pack_kernel,
        in_specs=[pl.BlockSpec(memory_space=pltpu.VMEM)] * (1 + len(planes)),
        out_specs=pl.BlockSpec(memory_space=pltpu.HBM),
        out_shape=jax.ShapeDtypeStruct(shape, BF16),
        scratch_shapes=[pltpu.VMEM(shape, BF16), pltpu.SemaphoreType.DMA((4,))],
        compiler_params=pltpu.CompilerParams(vmem_limit_bytes=6 << 20),
        name="pack",
    )(code, *planes)


def join_kernel(code, got, out):
    count, rows, cols = out.shape
    lines = got.shape[0]
    i = lax.broadcasted_iota(jnp.int32, (rows, lines), 0)
    one, zero = jnp.float32(1.0), jnp.float32(0.0)
    counts = None
    for h in range(2):
        place = jnp.where(i == code[h : h + 1, :], one, zero).astype(BF16)
        if h == 0:
            counts = dot(place, jnp.ones((lines, cols), BF16))
            counts = jnp.maximum(counts, 1.0)
        for n in range(count // 4):
            v = dot(place, got[:, 2 * n * cols : 2 * (n + 1) * cols])
            out[4 * n + h] = (v[:, :cols] / counts).astype(BF16)
            out[4 * n + 2 + h] = (v[:, cols:] / counts).astype(BF16)


def join(code, got, rows, cols):
    count = got.shape[1] // cols * 2
    return pl.pallas_call(
        join_kernel,
        out_shape=jax.ShapeDtypeStruct((count, rows, cols), BF16),
        compiler_params=pltpu.CompilerParams(vmem_limit_bytes=6 << 20),
        name="join",
    )(code, got)


def halo(block, axis):
    count = lax.axis_size("gz")
    forward = [(i, i + 1) for i in range(count - 1)]
    backward = [(i + 1, i) for i in range(count - 1)]
    depth = block.shape[axis]
    low = lax.ppermute(lax.slice_in_dim(block, depth - HALO, depth, axis=axis), "gz", forward)
    high = lax.ppermute(lax.slice_in_dim(block, 0, HALO, axis=axis), "gz", backward)
    return low, high


def gather_all(v, first, last):
    count = lax.axis_size("tile")
    for bit in range(first, last):
        other = lax.ppermute(v, "tile", [(i, i ^ (1 << bit)) for i in range(count)])
        v = jnp.concatenate([v, other], axis=0)
    return v


def swap(blocks):
    return lax.all_to_all(blocks, "tile", split_axis=0, concat_axis=0, tiled=True)


def body(images, partner, dest, offset, extent):
    ntile = lax.axis_size("tile")
    tile = lax.axis_index("tile")
    plane_idx = lax.axis_index("gz")
    nplane = lax.axis_size("gz")
    rows, chans, depth, cols = images.shape
    lines = chans * depth * rows
    own = jnp.transpose(images, (2, 1, 0, 3))
    own = lax.optimization_barrier(own)
    turn, across, along, smooth_x, smooth_y = matrices(
        rows, cols, (partner[tile] != tile).astype(F32)
    )
    targets = dest[:, 0]
    order_idx = jnp.arange(ntile, dtype=jnp.int32)
    label = (targets * 1024 + offset * 4 + extent)[None, :]
    early = 3
    spread = swap(own.reshape(ntile, lines // ntile, cols))
    label = gather_all(label, 0, early)
    partner, label = lax.optimization_barrier((partner, label))
    picked = jnp.take(spread, partner, axis=0, mode="clip")
    fac = swap(picked).reshape(depth, chans, rows, cols)
    own_lo, own_hi = halo(own, 0)
    a10, dxa, dya = prepare(across, along, own, own_lo, own_hi)
    label = gather_all(label, early, ntile.bit_length() - 1)

    same_owner = targets[:, None] == targets[None, :]
    earlier = order_idx[:, None] > order_idx[None, :]
    slot = jnp.sum((same_owner & earlier).astype(jnp.int32), axis=1)
    within = jnp.arange(2, dtype=jnp.int32)
    code = (targets * 8 + slot * 2)[:, None] + within[None, :]
    code = code.reshape(1, rows)
    code = jnp.concatenate([code, code + 4], axis=1)

    mine = (label // 1024) == tile
    spot = label % 1024
    head = jnp.min(jnp.where(mine, order_idx[None, :], ntile), axis=1, keepdims=True)
    is_head = order_idx[None, :] == head
    first = jnp.sum(jnp.where(mine & is_head, spot, 0), axis=1)
    second = jnp.sum(jnp.where(mine & ~is_head, spot, 0), axis=1)
    info = jnp.take(jnp.stack([first, second], axis=1), order_idx ^ tile, axis=0, mode="clip")
    start, span = info // 4, info % 4
    spots = jnp.where(within < span[:, :, None], start[:, :, None] + within, -1)
    spots = spots.reshape(ntile, 2 * CAP)
    none = jnp.full_like(spots, -1)
    code_in = jnp.stack(
        [
            jnp.concatenate([spots, none], axis=1).reshape(-1),
            jnp.concatenate([none, spots], axis=1).reshape(-1),
        ]
    )
    flags = jnp.stack([plane_idx > 0, plane_idx < nplane - 1]).astype(F32)
    fac, a10, dxa, dya, turn, code, code_in, flags = lax.optimization_barrier(
        (fac, a10, dxa, dya, turn, code, code_in, flags)
    )

    sides = [halo(fac[:, c], 0) for c in range(chans)]
    planes = [
        correct(c, flags, turn, along, smooth_x, smooth_y, a10, dxa, dya, fac, *sides[c])
        for c in range(chans)
    ]
    outgoing = pack(code, planes, ntile)
    received = swap(outgoing.reshape(ntile, 8, outgoing.shape[1]))
    joined = join(code_in, received.reshape(ntile * 8, -1), rows, cols)

    def home(v):
        return jnp.transpose(v.reshape(chans, depth, rows, cols), (2, 0, 1, 3))

    return home(jnp.stack(planes)), home(joined)


def solution(mesh):
    in_specs = (P("tile", None, "gz", None), P(), P("tile", None), P("tile"), P("tile"))
    out_specs = (P("tile", None, "gz", None), P("tile", None, "gz", None))
    return jax.shard_map(body, mesh=mesh, in_specs=in_specs, out_specs=out_specs, check_vma=False)
```

time: 170 us -> 218 us (1.28)
  the two profiles are of different devices: /device:TPU:8 before, /device:TPU:10 now
where the time goes in v2:
time: 218 us; the launch traced here: 217 us
  starting transfers between devices  96.7 us (44%)
  waiting for transfers between devices  56.3 us (26%)
  local copies, waits for them, and re-layouts  27.7 us (13%)
  Pallas kernels  21.7 us (10%)
  other arithmetic  12.6 us (6%)
    all_to_all x3, starting transfers between devices, swap(): lax.all_to_all(blocks, 'tile', split_axis=0, concat_axis=0, tiled=True)  42.4 us
    all_to_all x3, waiting for transfers between devices, swap(): lax.all_to_all(blocks, 'tile', split_axis=0, concat_axis=0, tiled=True)  41 us
    ppermute x7, starting transfers between devices, gather_all(): other = lax.ppermute(v, 'tile', [(i, i ^ 1 << bit) for i in range(count)])  30.7 us
    unnamed x51, local copies, waits for them, and re-layouts  17 us
    pallas_call x3, Pallas kernels, correct(): pl.pallas_call(functools.partial(correct_kernel, chan), in_specs=[pl.Bloc...  15.9 us
    ppermute x7, waiting for transfers between devices, gather_all(): other = lax.ppermute(v, 'tile', [(i, i ^ 1 << bit) for i in range(count)])  15.3 us
    ppermute x4, starting transfers between devices, halo(): lax.ppermute(lax.slice_in_dim(block, depth - HALO, depth, axis=axis), 'gz...  13.5 us
    ppermute x4, starting transfers between devices, halo(): lax.ppermute(lax.slice_in_dim(block, 0, HALO, axis=axis), 'gz', backward)  10.1 us
  transfers between devices with their start and end apart: 18, of which 6 were waited for; matrix products, arithmetic and copies ran while one was open for 12% of the time, Pallas kernels for 6%

profile of v2, /device:TPU:10, one launch (start us, length us, event | category | flops | bytes accessed | tf_op | source)
XLA Modules:
  0.0 216.9 jit_solution(2195874426150139629)
XLA Ops:
  0.7 2.2 %copy.65 = bf16[256,3,4,128]{3,0,1,2:T(8,128)(2,1)} copy(bf16[256,3,4,128]{3,2,1,0:T(4,128)(2,1)} %param.5) | data formatting | bytes 1572864 | tf_op args[0]
  2.8 17.5 %all-to-all-start = ((bf16[128,24,128]{2,1,0:T(8,128)(2,1)}), bf16[128,24,128]{2,1,0:T(8,128)(2,1)S(1)}, u32[]{:S(2)}, u32[]{:S(2)}) async-start(bf16[128,24,128]{2,1,0:T(8,128)(2,1)} %bitcast.1), calls=%async_computation | async-start | bytes 1572864 | tf_op jit(solution)/shard_map/all_to_all | solution.py:328
  20.4 2.0 collective-permute-start
  22.4 1.3 fusion.28
  23.7 3.4 %collective-permute-start.3 = (bf16[3,3,256,128]{3,2,1,0:T(8,128)(2,1)S(1)}, bf16[3,3,256,128]{3,2,1,0:T(8,128)(2,1)S(1)}, u32[]{:S(2)}, u32[]{:S(2)}) collective-permute-start(bf16[3,3,256,128]{3,2,1,0:T(8,128)(2,1)S(1)} %get-tuple-element.47), channel_id=1, source_target_pairs={{0,1},{1,2},{2,3},{4,5},{5,6},{6,7},{8,9},{9,10},{10,11},{12,13},{... | collective-permute-start | bytes 1769480 | tf_op jit(solution)/shard_map/ppermute | solution.py:314
  27.1 2.5 %collective-permute-start.4 = (bf16[3,3,256,128]{3,2,1,0:T(8,128)(2,1)S(1)}, bf16[3,3,256,128]{3,2,1,0:T(8,128)(2,1)S(1)}, u32[]{:S(2)}, u32[]{:S(2)}) collective-permute-start(bf16[3,3,256,128]{3,2,1,0:T(8,128)(2,1)S(1)} %get-tuple-element.46), channel_id=1, source_target_pairs={{1,0},{2,1},{3,2},{5,4},{6,5},{7,6},{9,8},{10,9},{11,10},{13,12},{... | collective-permute-start | bytes 1769480 | tf_op jit(solution)/shard_map/ppermute | solution.py:315
  33.9 0.9 pad_maximum_fusion.smooth_y
  36.8 2.7 %collective-permute-start.1 = (s32[2,128]{1,0:T(2,128)}, s32[2,128]{1,0:T(2,128)}, u32[]{:S(2)}, u32[]{:S(2)}) collective-permute-start(s32[2,128]{1,0:T(2,128)} %pad_add_fusion.7), channel_id=1, source_target_pairs={{0,8},{4,12},{8,0},{12,4},{16,24},{20,28},{24,16},{28,20},{32,40},... | collective-permute-start | bytes 3080 | tf_op jit(solution)/shard_map/ppermute | solution.py:322
  39.5 3.1 %collective-permute-done.1 = s32[2,128]{1,0:T(2,128)} collective-permute-done((s32[2,128]{1,0:T(2,128)}, s32[2,128]{1,0:T(2,128)}, u32[]{:S(2)}, u32[]{:S(2)}) %collective-permute-start.1) | collective-permute-done | bytes 1056 | tf_op jit(solution)/shard_map/ppermute | solution.py:322
  43.2 4.3 %collective-permute-start.2 = (s32[4,128]{1,0:T(4,128)S(1)}, s32[4,128]{1,0:T(4,128)}, u32[]{:S(2)}, u32[]{:S(2)}) collective-permute-start(s32[4,128]{1,0:T(4,128)S(1)} %pad_add_fusion.5), channel_id=1, source_target_pairs={{0,16},{4,20},{8,24},{12,28},{16,0},{20,4},{24,8},{28,12},{32,48},... | collective-permute-start | bytes 6152 | tf_op jit(solution)/shard_map/ppermute | solution.py:322
  48.1 1.3 lt.46
  50.4 6.4 %collective-permute-start.5 = (s32[8,128]{1,0:T(8,128)S(1)}, s32[8,128]{1,0:T(8,128)S(1)}, u32[]{:S(2)}, u32[]{:S(2)}) collective-permute-start(s32[8,128]{1,0:T(8,128)S(1)} %pad_add_fusion.4), channel_id=1, source_target_pairs={{0,32},{4,36},{8,40},{12,44},{16,48},{20,52},{24,56},{28,60},{32,0... | collective-permute-start | bytes 12296 | tf_op jit(solution)/shard_map/ppermute | solution.py:322
  57.4 1.2 pad_clamp_fusion.1
  58.6 1.2 collective-permute-done.5
  59.8 3.4 %collective-permute-start.6 = (s32[16,128]{1,0:T(8,128)S(1)}, s32[16,128]{1,0:T(8,128)S(1)}, u32[]{:S(2)}, u32[]{:S(2)}) collective-permute-start(s32[16,128]{1,0:T(8,128)S(1)} %pad_add_fusion.2), channel_id=1, source_target_pairs={{0,64},{4,68},{8,72},{12,76},{16,80},{20,84},{24,88},{28,92},{32,9... | collective-permute-start | bytes 24584 | tf_op jit(solution)/shard_map/ppermute | solution.py:322
  63.7 1.6 collective-permute-done.6
  65.9 4.4 %collective-permute-start.7 = (s32[32,128]{1,0:T(8,128)}, s32[32,128]{1,0:T(8,128)}, u32[]{:S(2)}, u32[]{:S(2)}) collective-permute-start(s32[32,128]{1,0:T(8,128)} %pad_add_fusion.1), channel_id=1, source_target_pairs={{0,128},{4,132},{8,136},{12,140},{16,144},{20,148},{24,152},{28,15... | collective-permute-start | bytes 49160 | tf_op jit(solution)/shard_map/ppermute | solution.py:322
  70.3 1.7 gather_fusion
  72.0 12.5 %all-to-all-start.1 = ((bf16[128,24,128]{2,1,0:T(8,128)(2,1)}), bf16[128,24,128]{2,1,0:T(8,128)(2,1)}, u32[]{:S(2)}, u32[]{:S(2)}) async-start(bf16[128,24,128]{2,1,0:T(8,128)(2,1)} %gather_fusion), calls=%async_computation.1 | async-start | bytes 1572864 | tf_op jit(solution)/shard_map/all_to_all | solution.py:328
  84.5 1.3 constant_dynamic-update-slice_fusion.2
  86.5 7.6 %collective-permute-start.8 = (s32[64,128]{1,0:T(8,128)S(1)}, s32[64,128]{1,0:T(8,128)S(1)}, u32[]{:S(2)}, u32[]{:S(2)}) collective-permute-start(s32[64,128]{1,0:T(8,128)S(1)} %pad_add_fusion), channel_id=1, source_target_pairs={{0,256},{4,260},{8,264},{12,268},{16,272},{20,276},{24,280},{28,28... | collective-permute-start | bytes 98312 | tf_op jit(solution)/shard_map/ppermute | solution.py:322
  94.1 1.3 constant_dynamic-update-slice_fusion.1
  95.4 9.3 %collective-permute-done.8 = s32[64,128]{1,0:T(8,128)S(1)} collective-permute-done((s32[64,128]{1,0:T(8,128)S(1)}, s32[64,128]{1,0:T(8,128)S(1)}, u32[]{:S(2)}, u32[]{:S(2)}) %collective-permute-start.8) | collective-permute-done | bytes 32800 | tf_op jit(solution)/shard_map/ppermute | solution.py:322
  105.3 1.0 select_reduce_fusion.2
  106.3 1.0 select_reduce_fusion.1
  110.4 0.9 copy-done.13
  111.3 1.1 copy-done.12
  112.3 1.1 copy-done.14
  114.1 2.8 %prepare.1 = (bf16[3,10,256,128]{3,2,1,0:T(8,128)(2,1)S(1)}, f32[3,8,256,128]{3,2,1,0:T(8,128)S(1)}, f32[3,8,256,128]{3,2,1,0:T(8,128)S(1)}) custom-call(bf16[128,128]{1,0:T(8,128)(2,1)S(1)} %copy-done.15, bf16[256,256]{1,0:T(8,128)(2,1)S(1)} %subtract_convert_fusion.1.along, bf16[4,3,256,128]{3,2,1,0:T(8,128)(2,1)} %bitcast.46.own, ...), custom_call_target="tpu_custom_call" | custom-call | tf_op jit(solution)/shard_map/prepare/pallas_call | solution.py:104
  117.0 1.6 copy-done
  118.6 1.3 copy-done.2
  119.9 1.6 slice_bitcast_fusion.4
  121.5 3.4 %collective-permute-start.13 = (bf16[3,256,128]{2,1,0:T(8,128)(2,1)S(1)}, bf16[3,256,128]{2,1,0:T(8,128)(2,1)S(1)}, u32[]{:S(2)}, u32[]{:S(2)}) collective-permute-start(bf16[3,256,128]{2,1,0:T(8,128)(2,1)S(1)} %get-tuple-element.42), channel_id=1, source_target_pairs={{0,1},{1,2},{2,3},{4,5},{5,6},{6,7},{8,9},{9,10},{10,11},{12,13},{... | collective-permute-start | bytes 589832 | tf_op jit(solution)/shard_map/ppermute | solution.py:314
  124.9 2.5 %collective-permute-start.14 = (bf16[3,256,128]{2,1,0:T(8,128)(2,1)S(1)}, bf16[3,256,128]{2,1,0:T(8,128)(2,1)S(1)}, u32[]{:S(2)}, u32[]{:S(2)}) collective-permute-start(bf16[3,256,128]{2,1,0:T(8,128)(2,1)S(1)} %get-tuple-element.41), channel_id=1, source_target_pairs={{1,0},{2,1},{3,2},{5,4},{6,5},{7,6},{9,8},{10,9},{11,10},{13,12},{... | collective-permute-start | bytes 589832 | tf_op jit(solution)/shard_map/ppermute | solution.py:315
  127.4 3.4 %collective-permute-start.11 = (bf16[3,256,128]{2,1,0:T(8,128)(2,1)S(1)}, bf16[3,256,128]{2,1,0:T(8,128)(2,1)S(1)}, u32[]{:S(2)}, u32[]{:S(2)}) collective-permute-start(bf16[3,256,128]{2,1,0:T(8,128)(2,1)S(1)} %get-tuple-element.44), channel_id=1, source_target_pairs={{0,1},{1,2},{2,3},{4,5},{5,6},{6,7},{8,9},{9,10},{10,11},{12,13},{... | collective-permute-start | bytes 589832 | tf_op jit(solution)/shard_map/ppermute | solution.py:314
  130.8 2.5 %collective-permute-start.12 = (bf16[3,256,128]{2,1,0:T(8,128)(2,1)S(1)}, bf16[3,256,128]{2,1,0:T(8,128)(2,1)S(1)}, u32[]{:S(2)}, u32[]{:S(2)}) collective-permute-start(bf16[3,256,128]{2,1,0:T(8,128)(2,1)S(1)} %get-tuple-element.43), channel_id=1, source_target_pairs={{1,0},{2,1},{3,2},{5,4},{6,5},{7,6},{9,8},{10,9},{11,10},{13,12},{... | collective-permute-start | bytes 589832 | tf_op jit(solution)/shard_map/ppermute | solution.py:315
  133.3 3.4 %collective-permute-start.9 = (bf16[3,256,128]{2,1,0:T(8,128)(2,1)S(1)}, bf16[3,256,128]{2,1,0:T(8,128)(2,1)S(1)}, u32[]{:S(2)}, u32[]{:S(2)}) collective-permute-start(bf16[3,256,128]{2,1,0:T(8,128)(2,1)S(1)} %get-tuple-element.45), channel_id=1, source_target_pairs={{0,1},{1,2},{2,3},{4,5},{5,6},{6,7},{8,9},{9,10},{10,11},{12,13},{... | collective-permute-start | bytes 589832 | tf_op jit(solution)/shard_map/ppermute | solution.py:314
  136.7 2.7 %collective-permute-start.10 = (bf16[3,256,128]{2,1,0:T(8,128)(2,1)S(1)}, bf16[3,256,128]{2,1,0:T(8,128)(2,1)S(1)}, u32[]{:S(2)}, u32[]{:S(2)}) collective-permute-start(bf16[3,256,128]{2,1,0:T(8,128)(2,1)S(1)} %get-tuple-element.40), channel_id=1, source_target_pairs={{1,0},{2,1},{3,2},{5,4},{6,5},{7,6},{9,8},{10,9},{11,10},{13,12},{... | collective-permute-start | bytes 589832 | tf_op jit(solution)/shard_map/ppermute | solution.py:315
  139.4 1.9 copy-done.1
  141.3 5.3 %correct.5.third = bf16[4,256,128]{2,1,0:T(8,128)(2,1)S(1)} custom-call(f32[2]{0:T(128)S(1)} %add_convert_fusion.flags, bf16[128,256]{1,0:T(8,128)(2,1)S(1)} %copy-done.10, bf16[256,256]{1,0:T(8,128)(2,1)S(1)} %subtract_convert_fusion.1.along, bf16[256,256]{1,0:T(8,128)(2,1)S(1)} %fusion.7.smooth_x, bf16[512,256]{1,0:T(8,128)(2,1)S(1)} %pad_maximum_fusion.smooth_y, ...), custom_call_target="tpu_custom_call" | custom-call | flops 2000000000 | bytes 12000000 | tf_op jit(solution)/shard_map/correct/pallas_call | solution.py:226
  146.6 5.3 %correct.4.second = bf16[4,256,128]{2,1,0:T(8,128)(2,1)S(1)} custom-call(f32[2]{0:T(128)S(1)} %add_convert_fusion.flags, bf16[128,256]{1,0:T(8,128)(2,1)S(1)} %copy-done.10, bf16[256,256]{1,0:T(8,128)(2,1)S(1)} %subtract_convert_fusion.1.along, bf16[256,256]{1,0:T(8,128)(2,1)S(1)} %fusion.7.smooth_x, bf16[512,256]{1,0:T(8,128)(2,1)S(1)} %pad_maximum_fusion.smooth_y, ...), custom_call_target="tpu_custom_call" | custom-call | flops 2000000000 | bytes 12000000 | tf_op jit(solution)/shard_map/correct/pallas_call | solution.py:226
  152.0 5.3 %correct.3.first = bf16[4,256,128]{2,1,0:T(8,128)(2,1)S(1)} custom-call(f32[2]{0:T(128)S(1)} %add_convert_fusion.flags, bf16[128,256]{1,0:T(8,128)(2,1)S(1)} %copy-done.10, bf16[256,256]{1,0:T(8,128)(2,1)S(1)} %subtract_convert_fusion.1.along, bf16[256,256]{1,0:T(8,128)(2,1)S(1)} %fusion.7.smooth_x, bf16[512,256]{1,0:T(8,128)(2,1)S(1)} %pad_maximum_fusion.smooth_y, ...), custom_call_target="tpu_custom_call" | custom-call | flops 2000000000 | bytes 12000000 | tf_op jit(solution)/shard_map/correct/pallas_call | solution.py:226
  157.4 1.8 pack.1
  159.2 12.5 %all-to-all-start.2 = ((bf16[128,8,768]{2,1,0:T(8,128)(2,1)}), bf16[128,8,768]{2,1,0:T(8,128)(2,1)S(1)}, u32[]{:S(2)}, u32[]{:S(2)}) async-start(bf16[128,8,768]{2,1,0:T(8,128)(2,1)} %bitcast.25), calls=%async_computation.2 | async-start | bytes 3145728 | tf_op jit(solution)/shard_map/all_to_all | solution.py:328
  171.8 1.5 copy.57
  173.3 41.0 %all-to-all-done.2 = bf16[128,8,768]{2,1,0:T(8,128)(2,1)S(1)} async-done(((bf16[128,8,768]{2,1,0:T(8,128)(2,1)}), bf16[128,8,768]{2,1,0:T(8,128)(2,1)S(1)}, u32[]{:S(2)}, u32[]{:S(2)}) %all-to-all-start.2) | async-done | bytes 1572896 | tf_op jit(solution)/shard_map/all_to_all | solution.py:328
  214.2 1.1 join.1
  215.4 1.5 copy.64
  (97 shorter events, 15.0 us)
Async XLA Ops:
  0.6 19.7 %copy-start.19 = (s32[128]{0:T(128)S(1)}, s32[128]{0:T(128)}, u32[]{:S(2)}) copy-start(s32[128]{0:T(128)} %param.9) | copy-start | bytes 1540
  0.6 19.7 %copy-start.20 = (s32[128]{0:T(128)S(1)}, s32[128]{0:T(128)}, u32[]{:S(2)}) copy-start(s32[128]{0:T(128)} %param.8) | copy-start | bytes 1540
  0.7 19.7 %copy-start.21 = (s32[128,1]{0,1:T(1,128)S(1)}, s32[128,1]{0,1:T(1,128)}, u32[]{:S(2)}) copy-start(s32[128,1]{0,1:T(1,128)} %param.7) | copy-start | bytes 1540
  2.8 28.1 %copy-start.18 = (s32[128]{0:T(128)S(1)}, s32[128]{0:T(128)}, u32[]{:S(2)}) copy-start(s32[128]{0:T(128)} %param.6) | copy-start | bytes 1540
  2.8 67.5 %all-to-all-start = ((bf16[128,24,128]{2,1,0:T(8,128)(2,1)}), bf16[128,24,128]{2,1,0:T(8,128)(2,1)S(1)}, u32[]{:S(2)}, u32[]{:S(2)}) async-start(bf16[128,24,128]{2,1,0:T(8,128)(2,1)} %bitcast.1), calls=%async_computation | async-start | bytes 1572864 | tf_op jit(solution)/shard_map/all_to_all | solution.py:328
  20.4 15.8 %collective-permute-start = (s32[1,128]{1,0:T(1,128)S(1)}, s32[1,128]{1,0:T(1,128)S(1)}, u32[]{:S(2)}, u32[]{:S(2)}) collective-permute-start(s32[1,128]{1,0:T(1,128)S(1)} %add_bitcast_fusion), channel_id=1, source_target_pairs={{0,4},{4,0},{8,12},{12,8},{16,20},{20,16},{24,28},{28,24},{32,36},... | collective-permute-start | bytes 1544 | tf_op jit(solution)/shard_map/ppermute | solution.py:322
  23.7 85.8 %collective-permute-start.3 = (bf16[3,3,256,128]{3,2,1,0:T(8,128)(2,1)S(1)}, bf16[3,3,256,128]{3,2,1,0:T(8,128)(2,1)S(1)}, u32[]{:S(2)}, u32[]{:S(2)}) collective-permute-start(bf16[3,3,256,128]{3,2,1,0:T(8,128)(2,1)S(1)} %get-tuple-element.47), channel_id=1, source_target_pairs={{0,1},{1,2},{2,3},{4,5},{5,6},{6,7},{8,9},{9,10},{10,11},{12,13},{... | collective-permute-start | bytes 1769480 | tf_op jit(solution)/shard_map/ppermute | solution.py:314
  27.1 83.2 %collective-permute-start.4 = (bf16[3,3,256,128]{3,2,1,0:T(8,128)(2,1)S(1)}, bf16[3,3,256,128]{3,2,1,0:T(8,128)(2,1)S(1)}, u32[]{:S(2)}, u32[]{:S(2)}) collective-permute-start(bf16[3,3,256,128]{3,2,1,0:T(8,128)(2,1)S(1)} %get-tuple-element.46), channel_id=1, source_target_pairs={{1,0},{2,1},{3,2},{5,4},{6,5},{7,6},{9,8},{10,9},{11,10},{13,12},{... | collective-permute-start | bytes 1769480 | tf_op jit(solution)/shard_map/ppermute | solution.py:315
  36.2 11.3 %copy-start.17 = (s32[1,128]{1,0:T(1,128)}, s32[1,128]{1,0:T(1,128)S(1)}, u32[]{:S(2)}) copy-start(s32[1,128]{1,0:T(1,128)S(1)} %collective-permute-done) | copy-start | bytes 1540
  36.8 5.8 %collective-permute-start.1 = (s32[2,128]{1,0:T(2,128)}, s32[2,128]{1,0:T(2,128)}, u32[]{:S(2)}, u32[]{:S(2)}) collective-permute-start(s32[2,128]{1,0:T(2,128)} %pad_add_fusion.7), channel_id=1, source_target_pairs={{0,8},{4,12},{8,0},{12,4},{16,24},{20,28},{24,16},{28,20},{32,40},... | collective-permute-start | bytes 3080 | tf_op jit(solution)/shard_map/ppermute | solution.py:322
  43.2 6.5 %collective-permute-start.2 = (s32[4,128]{1,0:T(4,128)S(1)}, s32[4,128]{1,0:T(4,128)}, u32[]{:S(2)}, u32[]{:S(2)}) collective-permute-start(s32[4,128]{1,0:T(4,128)S(1)} %pad_add_fusion.5), channel_id=1, source_target_pairs={{0,16},{4,20},{8,24},{12,28},{16,0},{20,4},{24,8},{28,12},{32,48},... | collective-permute-start | bytes 6152 | tf_op jit(solution)/shard_map/ppermute | solution.py:322
  50.4 9.4 %collective-permute-start.5 = (s32[8,128]{1,0:T(8,128)S(1)}, s32[8,128]{1,0:T(8,128)S(1)}, u32[]{:S(2)}, u32[]{:S(2)}) collective-permute-start(s32[8,128]{1,0:T(8,128)S(1)} %pad_add_fusion.4), channel_id=1, source_target_pairs={{0,32},{4,36},{8,40},{12,44},{16,48},{20,52},{24,56},{28,60},{32,0... | collective-permute-start | bytes 12296 | tf_op jit(solution)/shard_map/ppermute | solution.py:322
  59.8 5.5 %collective-permute-start.6 = (s32[16,128]{1,0:T(8,128)S(1)}, s32[16,128]{1,0:T(8,128)S(1)}, u32[]{:S(2)}, u32[]{:S(2)}) collective-permute-start(s32[16,128]{1,0:T(8,128)S(1)} %pad_add_fusion.2), channel_id=1, source_target_pairs={{0,64},{4,68},{8,72},{12,76},{16,80},{20,84},{24,88},{28,92},{32,9... | collective-permute-start | bytes 24584 | tf_op jit(solution)/shard_map/ppermute | solution.py:322
  65.3 0.6 copy-start.16
  65.9 19.9 %collective-permute-start.7 = (s32[32,128]{1,0:T(8,128)}, s32[32,128]{1,0:T(8,128)}, u32[]{:S(2)}, u32[]{:S(2)}) collective-permute-start(s32[32,128]{1,0:T(8,128)} %pad_add_fusion.1), channel_id=1, source_target_pairs={{0,128},{4,132},{8,136},{12,140},{16,144},{20,148},{24,152},{28,15... | collective-permute-start | bytes 49160 | tf_op jit(solution)/shard_map/ppermute | solution.py:322
  72.0 47.9 %all-to-all-start.1 = ((bf16[128,24,128]{2,1,0:T(8,128)(2,1)}), bf16[128,24,128]{2,1,0:T(8,128)(2,1)}, u32[]{:S(2)}, u32[]{:S(2)}) async-start(bf16[128,24,128]{2,1,0:T(8,128)(2,1)} %gather_fusion), calls=%async_computation.1 | async-start | bytes 1572864 | tf_op jit(solution)/shard_map/all_to_all | solution.py:328
  86.5 18.2 %collective-permute-start.8 = (s32[64,128]{1,0:T(8,128)S(1)}, s32[64,128]{1,0:T(8,128)S(1)}, u32[]{:S(2)}, u32[]{:S(2)}) collective-permute-start(s32[64,128]{1,0:T(8,128)S(1)} %pad_add_fusion), channel_id=1, source_target_pairs={{0,256},{4,260},{8,264},{12,268},{16,272},{20,276},{24,280},{28,28... | collective-permute-start | bytes 98312 | tf_op jit(solution)/shard_map/ppermute | solution.py:322
  109.6 0.8 copy-start.11
  110.4 0.9 copy-start.13
  111.3 1.1 copy-start.12
  112.3 1.1 copy-start.14
  113.4 0.8 copy-start.15
  117.0 1.6 copy-start
  118.6 1.3 copy-start.2
  119.9 19.5 %copy-start.3 = (bf16[3,10,256,128]{3,2,1,0:T(8,128)(2,1)S(1)}, bf16[3,10,256,128]{3,2,1,0:T(8,128)(2,1)}, u32[]{:S(2)}) copy-start(bf16[3,10,256,128]{3,2,1,0:T(8,128)(2,1)} %copy-done.2) | copy-start | bytes 5898244
  119.9 19.5 %copy-start.10 = (bf16[128,256]{1,0:T(8,128)(2,1)S(1)}, bf16[128,256]{1,0:T(8,128)(2,1)}, u32[]{:S(2)}) copy-start(bf16[128,256]{1,0:T(8,128)(2,1)} %pad_maximum_fusion.1.turn) | copy-start | bytes 196612
  121.5 15.2 %collective-permute-start.13 = (bf16[3,256,128]{2,1,0:T(8,128)(2,1)S(1)}, bf16[3,256,128]{2,1,0:T(8,128)(2,1)S(1)}, u32[]{:S(2)}, u32[]{:S(2)}) collective-permute-start(bf16[3,256,128]{2,1,0:T(8,128)(2,1)S(1)} %get-tuple-element.42), channel_id=1, source_target_pairs={{0,1},{1,2},{2,3},{4,5},{5,6},{6,7},{8,9},{9,10},{10,11},{12,13},{... | collective-permute-start | bytes 589832 | tf_op jit(solution)/shard_map/ppermute | solution.py:314
  124.9 14.5 %collective-permute-start.14 = (bf16[3,256,128]{2,1,0:T(8,128)(2,1)S(1)}, bf16[3,256,128]{2,1,0:T(8,128)(2,1)S(1)}, u32[]{:S(2)}, u32[]{:S(2)}) collective-permute-start(bf16[3,256,128]{2,1,0:T(8,128)(2,1)S(1)} %get-tuple-element.41), channel_id=1, source_target_pairs={{1,0},{2,1},{3,2},{5,4},{6,5},{7,6},{9,8},{10,9},{11,10},{13,12},{... | collective-permute-start | bytes 589832 | tf_op jit(solution)/shard_map/ppermute | solution.py:315
  127.4 19.1 %collective-permute-start.11 = (bf16[3,256,128]{2,1,0:T(8,128)(2,1)S(1)}, bf16[3,256,128]{2,1,0:T(8,128)(2,1)S(1)}, u32[]{:S(2)}, u32[]{:S(2)}) collective-permute-start(bf16[3,256,128]{2,1,0:T(8,128)(2,1)S(1)} %get-tuple-element.44), channel_id=1, source_target_pairs={{0,1},{1,2},{2,3},{4,5},{5,6},{6,7},{8,9},{9,10},{10,11},{12,13},{... | collective-permute-start | bytes 589832 | tf_op jit(solution)/shard_map/ppermute | solution.py:314
  130.8 15.8 %collective-permute-start.12 = (bf16[3,256,128]{2,1,0:T(8,128)(2,1)S(1)}, bf16[3,256,128]{2,1,0:T(8,128)(2,1)S(1)}, u32[]{:S(2)}, u32[]{:S(2)}) collective-permute-start(bf16[3,256,128]{2,1,0:T(8,128)(2,1)S(1)} %get-tuple-element.43), channel_id=1, source_target_pairs={{1,0},{2,1},{3,2},{5,4},{6,5},{7,6},{9,8},{10,9},{11,10},{13,12},{... | collective-permute-start | bytes 589832 | tf_op jit(solution)/shard_map/ppermute | solution.py:315
  133.3 18.6 %collective-permute-start.9 = (bf16[3,256,128]{2,1,0:T(8,128)(2,1)S(1)}, bf16[3,256,128]{2,1,0:T(8,128)(2,1)S(1)}, u32[]{:S(2)}, u32[]{:S(2)}) collective-permute-start(bf16[3,256,128]{2,1,0:T(8,128)(2,1)S(1)} %get-tuple-element.45), channel_id=1, source_target_pairs={{0,1},{1,2},{2,3},{4,5},{5,6},{6,7},{8,9},{9,10},{10,11},{12,13},{... | collective-permute-start | bytes 589832 | tf_op jit(solution)/shard_map/ppermute | solution.py:314
  136.7 15.3 %collective-permute-start.10 = (bf16[3,256,128]{2,1,0:T(8,128)(2,1)S(1)}, bf16[3,256,128]{2,1,0:T(8,128)(2,1)S(1)}, u32[]{:S(2)}, u32[]{:S(2)}) collective-permute-start(bf16[3,256,128]{2,1,0:T(8,128)(2,1)S(1)} %get-tuple-element.40), channel_id=1, source_target_pairs={{1,0},{2,1},{3,2},{5,4},{6,5},{7,6},{9,8},{10,9},{11,10},{13,12},{... | collective-permute-start | bytes 589832 | tf_op jit(solution)/shard_map/ppermute | solution.py:315
  139.4 1.9 copy-start.1
  146.6 10.8 %copy-start.4 = (bf16[4,256,128]{2,1,0:T(8,128)(2,1)}, bf16[4,256,128]{2,1,0:T(8,128)(2,1)S(1)}, u32[]{:S(2)}) copy-start(bf16[4,256,128]{2,1,0:T(8,128)(2,1)S(1)} %correct.5.third) | copy-start | bytes 786436
  152.0 5.4 %copy-start.6 = (bf16[4,256,128]{2,1,0:T(8,128)(2,1)}, bf16[4,256,128]{2,1,0:T(8,128)(2,1)S(1)}, u32[]{:S(2)}) copy-start(bf16[4,256,128]{2,1,0:T(8,128)(2,1)S(1)} %correct.4.second) | copy-start | bytes 786436
  157.4 1.8 copy-start.8
  159.2 12.5 %copy-start.5 = (bf16[4,256,128]{2,1,0:T(8,128)(2,1)S(1)}, bf16[4,256,128]{2,1,0:T(8,128)(2,1)}, u32[]{:S(2)}) copy-start(bf16[4,256,128]{2,1,0:T(8,128)(2,1)} %copy-done.4) | copy-start | bytes 786436
  159.2 12.5 %copy-start.7 = (bf16[4,256,128]{2,1,0:T(8,128)(2,1)S(1)}, bf16[4,256,128]{2,1,0:T(8,128)(2,1)}, u32[]{:S(2)}) copy-start(bf16[4,256,128]{2,1,0:T(8,128)(2,1)} %copy-done.6) | copy-start | bytes 786436
  159.2 12.5 %copy-start.9 = (bf16[4,256,128]{2,1,0:T(8,128)(2,1)S(1)}, bf16[4,256,128]{2,1,0:T(8,128)(2,1)}, u32[]{:S(2)}) copy-start(bf16[4,256,128]{2,1,0:T(8,128)(2,1)} %copy-done.8) | copy-start | bytes 786436
  159.2 55.0 %all-to-all-start.2 = ((bf16[128,8,768]{2,1,0:T(8,128)(2,1)}), bf16[128,8,768]{2,1,0:T(8,128)(2,1)S(1)}, u32[]{:S(2)}, u32[]{:S(2)}) async-start(bf16[128,8,768]{2,1,0:T(8,128)(2,1)} %bitcast.25), calls=%async_computation.2 | async-start | bytes 3145728 | tf_op jit(solution)/shard_map/all_to_all | solution.py:328

commit v3 on v1

v3 whole, which is shorter than its diff:
```python
import math

import jax
import jax.numpy as jnp
import numpy as np
from jax import lax
from jax.experimental import pallas as pl
from jax.experimental.pallas import tpu as pltpu
from jax.sharding import PartitionSpec as P

CAP = 2
HALO = 3

gauss_raw = [math.exp(-0.5 * k * k) for k in range(-2, 3)]
gauss_taps = [w / sum(gauss_raw) for w in gauss_raw]

F32 = jnp.float32
BF16 = jnp.bfloat16


def dot(a, b):
    return jnp.dot(a, b, preferred_element_type=F32)


def split(v):
    high = v.astype(BF16)
    return high, (v - high.astype(F32)).astype(BF16)


def constants(rows, cols):
    def near(n):
        i, j = np.indices((n, n))
        return i - j

    def band(n):
        total = np.zeros((n, n), np.float32)
        for k in range(5):
            total[near(n) == k - 2] = gauss_taps[k]
        high = total.astype(BF16)
        return high, (total - high.astype(np.float32)).astype(BF16)

    turn = np.eye(cols, dtype=np.float32)[:, ::-1].astype(BF16)
    gap = near(cols)
    across = (0.5 * (gap == 1) - 0.5 * (gap == -1)).astype(BF16)
    gap = near(rows)
    along = (0.5 * (gap == -1) - 0.5 * (gap == 1)).astype(BF16)
    high, low = (m[:, ::-1] for m in band(cols))
    smooth_x = np.block([[high, low], [high, np.zeros_like(low)]])
    smooth_y = np.concatenate(band(rows), axis=0)
    return turn, across, along, smooth_x, smooth_y


def plane_of(own, own_lo, own_hi, k):
    depth = own.shape[1]
    if k < HALO:
        return own_lo, k
    if k < HALO + depth:
        return own, k - HALO
    return own_hi, k - HALO - depth


def prepare_kernel(turn, across, along, own, own_lo, own_hi, a10, dxa, dya):
    depth, _, cols = own.shape[1:]
    for k in range(depth + 2 * HALO):
        ref, at = plane_of(own, own_lo, own_hi, k)
        a = dot(ref[0, at], turn[...]).astype(BF16)
        a10[0, k] = a
        if 0 < k < depth + 2 * HALO - 1:
            dxa[0, k - 1] = dot(a, across[...])
            if k % 2 == 0:
                dy = dot(along[...], jnp.concatenate([before, a], axis=1))
                dya[0, k - 2] = dy[:, :cols]
                dya[0, k - 1] = dy[:, cols:]
        before = a


def prepare(turn, across, along, own, own_lo, own_hi):
    chans, depth, rows, cols = own.shape
    wide = depth + 2 * HALO

    def spec(n):
        return pl.BlockSpec((1, n, rows, cols), lambda c: (c, 0, 0, 0))

    def whole(m):
        return pl.BlockSpec(m.shape, lambda c: (0, 0))

    def shape(n, dtype):
        return jax.ShapeDtypeStruct((chans, n, rows, cols), dtype)

    return pl.pallas_call(
        prepare_kernel,
        grid=(chans,),
        in_specs=[whole(turn), whole(across), whole(along)]
        + [spec(depth), spec(HALO), spec(HALO)],
        out_specs=[spec(wide), spec(wide - 2), spec(wide - 2)],
        out_shape=[shape(wide, BF16), shape(wide - 2, F32), shape(wide - 2, F32)],
        compiler_params=pltpu.CompilerParams(vmem_limit_bytes=60 << 20),
        name="prepare",
    )(turn, across, along, own, own_lo, own_hi)


def pack(code, planes, out, held, sems):
    chans, _, rows, cols = planes.shape
    step = held.shape[0] // sems.shape[0]
    copies = []
    for m in range(sems.shape[0]):
        at = pl.ds(m * step, step)
        i = lax.broadcasted_iota(jnp.int32, (step, 2 * rows), 0) + m * step
        pick = jnp.where(i == code[...], jnp.float32(1.0), jnp.float32(0.0)).astype(BF16)
        for n in range(chans):
            left = planes[n, 0:2].reshape(2 * rows, cols)
            right = planes[n, 2:4].reshape(2 * rows, cols)
            v = dot(pick, jnp.concatenate([left, right], axis=1))
            held[m * step : (m + 1) * step, 2 * n * cols : 2 * (n + 1) * cols] = v.astype(BF16)
        copies.append(pltpu.make_async_copy(held.at[at], out.at[at], sems.at[m]))
        copies[-1].start()
    for copy in copies:
        copy.wait()


def correct_kernel(
    flags,
    across,
    along,
    smooth_x,
    smooth_y,
    code,
    a10,
    dxa,
    dya,
    own,
    fac,
    fac_lo,
    fac_hi,
    out,
    sent,
    dxb,
    dyb,
    deep,
    kept,
    held,
    sems,
):
    chan = pl.program_id(0)
    depth, rows, cols = fac.shape[1:]
    wide = depth + 2 * HALO
    low, high = flags[0], flags[1]
    half = jnp.float32(0.5)
    for k in range(1, wide - 1):
        ref, at = plane_of(fac, fac_lo, fac_hi, k)
        now = ref[0, at]
        dxb[k - 1] = dot(now, across[...])
        if k % 2 == 0:
            dy = dot(along[...], jnp.concatenate([before, now], axis=1))
            dyb[k - 2] = dy[:, :cols]
            dyb[k - 1] = dy[:, cols:]
        before = now

    step = 32

    def chunk(r, carry):
        at_rows = pl.ds(pl.multiple_of(r * step, step), step)

        def a_of(k):
            return a10[0, k, at_rows, :].astype(F32)

        def b_of(k):
            ref, at = plane_of(fac, fac_lo, fac_hi, k)
            return ref[0, at, at_rows, :].astype(F32)

        one = [None] * depth
        two = [None] * depth
        a_last, av, a_next = None, a_of(0), a_of(1)
        b_last, bv, b_next = None, b_of(0), b_of(1)
        for k in range(1, wide - 1):
            a_last, av, a_next = av, a_next, a_of(k + 1)
            b_last, bv, b_next = bv, b_next, b_of(k + 1)
            dza = (a_next - a_last) * half
            dzb = (b_next - b_last) * half
            ya, yb = dya[0, k - 1, at_rows, :], dyb[k - 1, at_rows, :]
            xa, xb = dxa[0, k - 1, at_rows, :], dxb[k - 1, at_rows, :]
            p1 = av * bv + ya * yb + dza * dzb + xa * xb
            p2 = bv * bv + yb * yb + dzb * dzb + xb * xb
            if k < HALO:
                p1, p2 = p1 * low, p2 * low
            if k >= HALO + depth:
                p1, p2 = p1 * high, p2 * high
            for t in range(3):
                v1, v2 = gauss_taps[t] * p1, gauss_taps[t] * p2
                for z in {k - HALO + 2 - t, k - HALO - 2 + t}:
                    if 0 <= z < depth:
                        one[z] = v1 if one[z] is None else one[z] + v1
                        two[z] = v2 if two[z] is None else two[z] + v2
        for z in range(depth):
            for s, v in ((0, one[z]), (1, two[z])):
                h, l = split(v)
                deep[2 * z + s, at_rows, :cols] = h
                deep[2 * z + s, at_rows, cols:] = l
        return carry

    lax.fori_loop(0, rows // step, chunk, 0)

    for z in range(depth):
        parts = []
        for s in range(2):
            r = dot(deep[2 * z + s], smooth_x[...])
            parts.append(split(r[:, :cols] + r[:, cols:]))
        r_hi = jnp.concatenate([parts[0][0], parts[1][0]], axis=1)
        r_lo = jnp.concatenate([parts[0][1], parts[1][1]], axis=1)
        main = dot(smooth_y[...], r_hi)
        q = main[:rows] + main[rows:] + dot(smooth_y[:rows], r_lo)
        a = own[0, z].astype(F32)
        done = (a * (q[:, :cols] + 1.0) / (q[:, cols:] + 1.0)).astype(BF16)
        out[0, z] = done
        kept[chan, z] = done

    @pl.when(chan == kept.shape[0] - 1)
    def _():
        pack(code, kept, sent, held, sems)


def correct(
    flags, across, along, smooth_x, smooth_y, code, a10, dxa, dya, own, fac, fac_lo, fac_hi, blocks
):
    chans, depth, rows, cols = own.shape
    wide = depth + 2 * HALO
    packed = (blocks * 8, chans * depth // 2 * cols)

    def spec(n):
        return pl.BlockSpec((1, n, rows, cols), lambda c: (c, 0, 0, 0))

    def whole(m):
        return pl.BlockSpec(m.shape, lambda c: (0, 0))

    inner = pltpu.VMEM((wide - 2, rows, cols), F32)
    return pl.pallas_call(
        correct_kernel,
        grid=(chans,),
        in_specs=[pl.BlockSpec(memory_space=pltpu.SMEM)]
        + [whole(m) for m in (across, along, smooth_x, smooth_y, code)]
        + [spec(wide), spec(wide - 2), spec(wide - 2)]
        + [spec(depth), spec(depth), spec(HALO), spec(HALO)],
        out_specs=[spec(depth), pl.BlockSpec(memory_space=pltpu.HBM)],
        out_shape=[
            jax.ShapeDtypeStruct(own.shape, BF16),
            jax.ShapeDtypeStruct(packed, BF16),
        ],
        scratch_shapes=[
            inner,
            inner,
            pltpu.VMEM((2 * depth, rows, 2 * cols), BF16),
            pltpu.VMEM(own.shape, BF16),
            pltpu.VMEM(packed, BF16),
            pltpu.SemaphoreType.DMA((4,)),
        ],
        compiler_params=pltpu.CompilerParams(vmem_limit_bytes=60 << 20),
        cost_estimate=pl.CostEstimate(
            flops=4000000000, bytes_accessed=12000000, transcendentals=0
        ),
        name="correct",
    )(flags, across, along, smooth_x, smooth_y, code, a10, dxa, dya, own, fac, fac_lo, fac_hi)


def join_kernel(code, got, out):
    count, rows, cols = out.shape
    lines = got.shape[0]
    i = lax.broadcasted_iota(jnp.int32, (rows, lines), 0)
    one, zero = jnp.float32(1.0), jnp.float32(0.0)
    counts = None
    for h in range(2):
        place = jnp.where(i == code[h : h + 1, :], one, zero).astype(BF16)
        if h == 0:
            counts = dot(place, jnp.ones((lines, cols), BF16))
            counts = jnp.maximum(counts, 1.0)
        for n in range(count // 4):
            v = dot(place, got[:, 2 * n * cols : 2 * (n + 1) * cols])
            out[4 * n + h] = (v[:, :cols] / counts).astype(BF16)
            out[4 * n + 2 + h] = (v[:, cols:] / counts).astype(BF16)


def join(code, got, rows, cols):
    count = got.shape[1] // cols * 2
    return pl.pallas_call(
        join_kernel,
        out_shape=jax.ShapeDtypeStruct((count, rows, cols), BF16),
        compiler_params=pltpu.CompilerParams(vmem_limit_bytes=16 << 20),
        name="join",
    )(code, got)


def halo(block):
    count = lax.axis_size("gz")
    forward = [(i, i + 1) for i in range(count - 1)]
    backward = [(i + 1, i) for i in range(count - 1)]
    depth = block.shape[1]
    low = lax.ppermute(block[:, depth - HALO :], "gz", forward)
    high = lax.ppermute(block[:, :HALO], "gz", backward)
    return low, high


def swap(blocks):
    return lax.all_to_all(blocks, "tile", split_axis=0, concat_axis=0, tiled=True)


def body(images, partner, dest, offset, extent):
    ntile = lax.axis_size("tile")
    tile = lax.axis_index("tile")
    plane_idx = lax.axis_index("gz")
    nplane = lax.axis_size("gz")
    rows, chans, depth, cols = images.shape
    lines = chans * depth * rows
    own = jnp.transpose(images, (1, 2, 0, 3))
    own = lax.optimization_barrier(own)
    own_lo, own_hi = halo(own)
    spread = swap(own.reshape(ntile, lines // ntile, cols))
    picked = jnp.take(spread, partner, axis=0, mode="clip")
    fac = swap(picked).reshape(chans, depth, rows, cols)

    targets = dest[:, 0]
    order_idx = jnp.arange(ntile, dtype=jnp.int32)
    same_owner = targets[:, None] == targets[None, :]
    earlier = order_idx[:, None] > order_idx[None, :]
    slot = jnp.sum((same_owner & earlier).astype(jnp.int32), axis=1)
    slots = jnp.arange(CAP, dtype=jnp.int32)
    select = (order_idx[:, None, None] == targets[None, None, :]) & (
        slots[None, :, None] == slot[None, None, :]
    )
    label = offset * 4 + extent
    labels = jnp.sum(jnp.where(select, label[None, None, :], 0), axis=2)
    within = jnp.arange(2, dtype=jnp.int32)
    code = (targets * 8 + slot * 2)[:, None] + within[None, :]
    code = code.reshape(1, rows)
    code = jnp.concatenate([code, code + 4], axis=1)

    turn, across, along, smooth_x, smooth_y = (
        jnp.asarray(m) for m in constants(rows, cols)
    )
    smooth_x = smooth_x * (partner[tile] != tile).astype(BF16)
    flags = jnp.stack([plane_idx > 0, plane_idx < nplane - 1]).astype(F32)
    a10, dxa, dya = prepare(turn, across, along, own, own_lo, own_hi)
    fac, labels, code, a10, dxa, dya, smooth_x, flags = lax.optimization_barrier(
        (fac, labels, code, a10, dxa, dya, smooth_x, flags)
    )
    fac_lo, fac_hi = halo(fac)
    info = swap(labels)

    corrected, outgoing = correct(
        flags, across, along, smooth_x, smooth_y, code, a10, dxa, dya, own, fac, fac_lo, fac_hi, ntile
    )
    received = swap(outgoing.reshape(ntile, 8, outgoing.shape[1]))

    start, span = info // 4, info % 4
    spots = jnp.where(within < span[:, :, None], start[:, :, None] + within, -1)
    spots = spots.reshape(ntile, 2 * CAP)
    none = jnp.full_like(spots, -1)
    code_in = jnp.stack(
        [
            jnp.concatenate([spots, none], axis=1).reshape(-1),
            jnp.concatenate([none, spots], axis=1).reshape(-1),
        ]
    )
    joined = join(code_in, received.reshape(ntile * 8, -1), rows, cols)

    def home(v):
        return jnp.transpose(v.reshape(chans, depth, rows, cols), (2, 0, 1, 3))

    return home(corrected), home(joined)


def solution(mesh):
    in_specs = (P("tile", None, "gz", None), P(), P("tile", None), P("tile"), P("tile"))
    out_specs = (P("tile", None, "gz", None), P("tile", None, "gz", None))
    return jax.shard_map(body, mesh=mesh, in_specs=in_specs, out_specs=out_specs, check_vma=False)
```

time: 170 us -> 167 us (0.982)
  the two profiles are of different devices: /device:TPU:8 before, /device:TPU:14 now
where the time goes in v3:
time: 167 us
  waiting for transfers between devices  76.8 us (46%)
  starting transfers between devices  51.8 us (31%)
  Pallas kernels  21.9 us (13%)
  local copies, waits for them, and re-layouts  12.1 us (7%)
  other arithmetic  2.41 us (1%)
    all_to_all x4, waiting for transfers between devices, swap(): lax.all_to_all(blocks, 'tile', split_axis=0, concat_axis=0, tiled=True)  72.2 us
    all_to_all x4, starting transfers between devices, swap(): lax.all_to_all(blocks, 'tile', split_axis=0, concat_axis=0, tiled=True)  39.2 us
    pallas_call x1, Pallas kernels, correct(): pl.pallas_call(correct_kernel, grid=(chans,), in_specs=[pl.BlockSpec(memo...  14 us
    ppermute x2, starting transfers between devices, halo(): high = lax.ppermute(block[:, :HALO], 'gz', backward)  9.97 us
    pallas_call x1, Pallas kernels, prepare(): pl.pallas_call(prepare_kernel, grid=(chans,), in_specs=[whole(turn), whol...  6.77 us
    unnamed x23, local copies, waits for them, and re-layouts  5.49 us
    ppermute x2, waiting for transfers between devices, halo(): low = lax.ppermute(block[:, depth - HALO:], 'gz', forward)  3.46 us
  transfers between devices with their start and end apart: 8, of which 5 were waited for; matrix products, arithmetic and copies ran while one was open for 5% of the time, Pallas kernels for 12%

profile of v3, /device:TPU:14, one launch (start us, length us, event | category | flops | bytes accessed | tf_op | source)
XLA Modules:
  0.0 166.6 jit_solution(17250668352757979330)
XLA Ops:
  0.6 2.1 %copy.40 = bf16[256,3,4,128]{3,0,2,1:T(8,128)(2,1)} copy(bf16[256,3,4,128]{3,2,1,0:T(4,128)(2,1)} %param.10) | data formatting | bytes 1572864 | tf_op args[0]
  2.8 17.5 %all-to-all-start = ((bf16[128,24,128]{2,1,0:T(8,128)(2,1)}), bf16[128,24,128]{2,1,0:T(8,128)(2,1)S(1)}, u32[]{:S(2)}, u32[]{:S(2)}) async-start(bf16[128,24,128]{2,1,0:T(8,128)(2,1)} %bitcast.1), calls=%async_computation | async-start | bytes 1572864 | tf_op jit(solution)/shard_map/all_to_all | solution.py:302
  20.3 1.3 fusion.5
  21.6 0.0 copy-start.8
  21.6 0.0 copy-start.9
  21.6 0.0 copy-start.4
  21.7 1.4 collective-permute-start
  23.1 4.6 %collective-permute-start.1 = (bf16[3,3,256,128]{3,2,1,0:T(8,128)(2,1)S(1)}, bf16[3,3,256,128]{3,2,1,0:T(8,128)(2,1)S(1)}, u32[]{:S(2)}, u32[]{:S(2)}) collective-permute-start(bf16[3,3,256,128]{3,2,1,0:T(8,128)(2,1)S(1)} %get-tuple-element.38), channel_id=1, source_target_pairs={{1,0},{2,1},{3,2},{5,4},{6,5},{7,6},{9,8},{10,9},{11,10},{13,12},{... | collective-permute-start | bytes 1769480 | tf_op jit(solution)/shard_map/ppermute | solution.py:297
  27.7 0.2 convert_reduce_fusion
  27.9 18.1 %all-to-all-done = bf16[128,24,128]{2,1,0:T(8,128)(2,1)S(1)} async-done(((bf16[128,24,128]{2,1,0:T(8,128)(2,1)}), bf16[128,24,128]{2,1,0:T(8,128)(2,1)S(1)}, u32[]{:S(2)}, u32[]{:S(2)}) %all-to-all-start) | async-done | bytes 786464 | tf_op jit(solution)/shard_map/all_to_all | solution.py:302
  46.0 1.6 gather_fusion
  47.6 5.8 %all-to-all-start.1 = ((bf16[128,24,128]{2,1,0:T(8,128)(2,1)}), bf16[128,24,128]{2,1,0:T(8,128)(2,1)S(1)}, u32[]{:S(2)}, u32[]{:S(2)}) async-start(bf16[128,24,128]{2,1,0:T(8,128)(2,1)} %gather_fusion), calls=%async_computation.1 | async-start | bytes 1572864 | tf_op jit(solution)/shard_map/all_to_all | solution.py:302
  53.4 0.1 iota_add_fusion
  53.5 0.1 add.93
  53.7 0.5 pad_add_fusion.1.code
  54.3 0.7 add_convert_fusion.flags
  54.9 0.6 dynamic_slice.3
  56.2 0.1 select_reduce_fusion
  56.3 0.7 broadcast_multiply_fusion.smooth_x
  57.0 0.0 collective-permute-done.own_lo
  57.0 0.0 collective-permute-done.1.own_hi
  57.0 0.8 copy-done.2
  57.8 0.8 copy-done.3
  58.7 6.8 %prepare.1 = (bf16[3,10,256,128]{3,2,1,0:T(8,128)(2,1)}, f32[3,8,256,128]{3,2,1,0:T(8,128)}, f32[3,8,256,128]{3,2,1,0:T(8,128)}) custom-call(bf16[128,128]{1,0:T(8,128)(2,1)} %constant.58.clone.turn, bf16[128,128]{1,0:T(8,128)(2,1)} %constant.59.clone.across, bf16[256,256]{1,0:T(8,128)(2,1)} %constant.60.clone.along, bf16[3,4,256,128]{3,2,1,0:T(8,128)(2,1)} %bitcast.25.own, ...), custom_call_target="tpu_custom_call" | custom-call | tf_op jit(solution)/shard_map/prepare/pallas_call | solution.py:90
  65.5 13.8 %all-to-all-done.1 = bf16[128,24,128]{2,1,0:T(8,128)(2,1)S(1)} async-done(((bf16[128,24,128]{2,1,0:T(8,128)(2,1)}), bf16[128,24,128]{2,1,0:T(8,128)(2,1)S(1)}, u32[]{:S(2)}, u32[]{:S(2)}) %all-to-all-start.1) | async-done | bytes 786464 | tf_op jit(solution)/shard_map/all_to_all | solution.py:302
  79.2 0.2 fusion.4
  79.4 1.3 collective-permute-start.2
  80.7 5.4 %collective-permute-start.3 = (bf16[3,3,256,128]{3,2,1,0:T(8,128)(2,1)S(1)}, bf16[3,3,256,128]{3,2,1,0:T(8,128)(2,1)}, u32[]{:S(2)}, u32[]{:S(2)}) collective-permute-start(bf16[3,3,256,128]{3,2,1,0:T(8,128)(2,1)S(1)} %get-tuple-element.36), channel_id=1, source_target_pairs={{1,0},{2,1},{3,2},{5,4},{6,5},{7,6},{9,8},{10,9},{11,10},{13,12},{... | collective-permute-start | bytes 1769480 | tf_op jit(solution)/shard_map/ppermute | solution.py:297
  86.1 0.7 copy.28
  86.8 5.8 %all-to-all-start.2 = ((s32[128,1,2]{2,1,0:T(1,128)}), s32[128,1,2]{2,1,0:T(1,128)S(1)}, u32[]{:S(2)}, u32[]{:S(2)}) async-start(s32[128,1,2]{2,1,0:T(1,128)} %copy.28), calls=%async_computation.2 | async-start | bytes 131072 | tf_op jit(solution)/shard_map/all_to_all | solution.py:302
  92.7 3.5 %collective-permute-done.2.fac_lo = bf16[3,3,256,128]{3,2,1,0:T(8,128)(2,1)S(1)} collective-permute-done((bf16[3,3,256,128]{3,2,1,0:T(8,128)(2,1)S(1)}, bf16[3,3,256,128]{3,2,1,0:T(8,128)(2,1)S(1)}, u32[]{:S(2)}, u32[]{:S(2)}) %collective-permute-start.2) | collective-permute-done | bytes 589856 | tf_op jit(solution)/shard_map/ppermute | solution.py:296
  96.1 1.2 collective-permute-done.3.fac_hi
  97.3 14.0 %correct.1 = (bf16[3,4,256,128]{3,2,1,0:T(8,128)(2,1)}, bf16[1024,768]{1,0:T(8,128)(2,1)}) custom-call(f32[2]{0:T(128)} %add_convert_fusion.flags, bf16[128,128]{1,0:T(8,128)(2,1)} %constant.59.clone.across, bf16[256,256]{1,0:T(8,128)(2,1)} %constant.60.clone.along, bf16[256,256]{1,0:T(8,128)(2,1)} %broadcast_multiply_fusion.smooth_x, ...), custom_call_target="tpu_custom_call" | custom-call | flops 4000000000 | bytes 12000000 | tf_op jit(solution)/shard_map/correct/pallas_call | solution.py:236
  111.4 0.0 all-to-all-done.2
  111.4 10.0 %all-to-all-start.3 = ((bf16[128,8,768]{2,1,0:T(8,128)(2,1)}), bf16[128,8,768]{2,1,0:T(8,128)(2,1)S(1)}, u32[]{:S(2)}, u32[]{:S(2)}) async-start(bf16[128,8,768]{2,1,0:T(8,128)(2,1)} %bitcast.30), calls=%async_computation.3 | async-start | bytes 3145728 | tf_op jit(solution)/shard_map/all_to_all | solution.py:302
  121.4 0.1 lt.41
  121.5 0.1 add_select_fusion.1
  121.6 0.1 copy.30
  121.6 0.1 copy.29
  121.7 0.1 add_select_fusion.2
  121.8 0.1 copy.35
  121.9 0.1 fusion.6
  122.0 0.1 stack_reshape.7
  122.1 0.1 stack_reshape.6
  122.2 1.5 copy.34
  123.7 40.2 %all-to-all-done.3 = bf16[128,8,768]{2,1,0:T(8,128)(2,1)S(1)} async-done(((bf16[128,8,768]{2,1,0:T(8,128)(2,1)}), bf16[128,8,768]{2,1,0:T(8,128)(2,1)S(1)}, u32[]{:S(2)}, u32[]{:S(2)}) %all-to-all-start.3) | async-done | bytes 1572896 | tf_op jit(solution)/shard_map/all_to_all | solution.py:302
  164.0 1.1 join.1
  165.1 1.5 copy.39
  (25 shorter events, 0.1 us)
Async XLA Ops:
  2.8 24.9 %copy-start.5 = (s32[128]{0:T(128)S(1)}, s32[128]{0:T(128)}, u32[]{:S(2)}) copy-start(s32[128]{0:T(128)} %param.11) | copy-start | bytes 1540
  2.8 24.9 %copy-start.6 = (s32[128,1]{0,1:T(1,128)S(1)}, s32[128,1]{0,1:T(1,128)}, u32[]{:S(2)}) copy-start(s32[128,1]{0,1:T(1,128)} %param.12) | copy-start | bytes 1540
  2.8 43.3 %all-to-all-start = ((bf16[128,24,128]{2,1,0:T(8,128)(2,1)}), bf16[128,24,128]{2,1,0:T(8,128)(2,1)S(1)}, u32[]{:S(2)}, u32[]{:S(2)}) async-start(bf16[128,24,128]{2,1,0:T(8,128)(2,1)} %bitcast.1), calls=%async_computation | async-start | bytes 1572864 | tf_op jit(solution)/shard_map/all_to_all | solution.py:302
  21.6 32.6 %copy-start.8 = (s32[128]{0:T(128)S(1)}, s32[128]{0:T(128)}, u32[]{:S(2)}) copy-start(s32[128]{0:T(128)} %param.14) | copy-start | bytes 1540
  21.6 32.6 %copy-start.9 = (s32[128]{0:T(128)S(1)}, s32[128]{0:T(128)}, u32[]{:S(2)}) copy-start(s32[128]{0:T(128)} %param.13) | copy-start | bytes 1540
  21.6 34.7 %copy-start.4 = (bf16[256,256]{1,0:T(8,128)(2,1)S(1)}, bf16[256,256]{1,0:T(8,128)(2,1)}, u32[]{:S(2)}) copy-start(bf16[256,256]{1,0:T(8,128)(2,1)} %constant.61.clone) | copy-start | bytes 393220
  21.7 35.3 %collective-permute-start = (bf16[3,3,256,128]{3,2,1,0:T(8,128)(2,1)S(1)}, bf16[3,3,256,128]{3,2,1,0:T(8,128)(2,1)S(1)}, u32[]{:S(2)}, u32[]{:S(2)}) collective-permute-start(bf16[3,3,256,128]{3,2,1,0:T(8,128)(2,1)S(1)} %get-tuple-element.39), channel_id=1, source_target_pairs={{0,1},{1,2},{2,3},{4,5},{5,6},{6,7},{8,9},{9,10},{10,11},{12,13},{... | collective-permute-start | bytes 1769480 | tf_op jit(solution)/shard_map/ppermute | solution.py:296
  23.1 33.9 %collective-permute-start.1 = (bf16[3,3,256,128]{3,2,1,0:T(8,128)(2,1)S(1)}, bf16[3,3,256,128]{3,2,1,0:T(8,128)(2,1)S(1)}, u32[]{:S(2)}, u32[]{:S(2)}) collective-permute-start(bf16[3,3,256,128]{3,2,1,0:T(8,128)(2,1)S(1)} %get-tuple-element.38), channel_id=1, source_target_pairs={{1,0},{2,1},{3,2},{5,4},{6,5},{7,6},{9,8},{10,9},{11,10},{13,12},{... | collective-permute-start | bytes 1769480 | tf_op jit(solution)/shard_map/ppermute | solution.py:297
  47.6 31.6 %all-to-all-start.1 = ((bf16[128,24,128]{2,1,0:T(8,128)(2,1)}), bf16[128,24,128]{2,1,0:T(8,128)(2,1)S(1)}, u32[]{:S(2)}, u32[]{:S(2)}) async-start(bf16[128,24,128]{2,1,0:T(8,128)(2,1)} %gather_fusion), calls=%async_computation.1 | async-start | bytes 1572864 | tf_op jit(solution)/shard_map/all_to_all | solution.py:302
  57.0 0.9 copy-start.2
  57.8 0.8 copy-start.3
  79.2 18.1 %copy-start = (bf16[128,24,128]{2,1,0:T(8,128)(2,1)}, bf16[128,24,128]{2,1,0:T(8,128)(2,1)S(1)}, u32[]{:S(2)}) copy-start(bf16[128,24,128]{2,1,0:T(8,128)(2,1)S(1)} %all-to-all-done.1) | copy-start | bytes 2359300
  79.4 16.7 %collective-permute-start.2 = (bf16[3,3,256,128]{3,2,1,0:T(8,128)(2,1)S(1)}, bf16[3,3,256,128]{3,2,1,0:T(8,128)(2,1)S(1)}, u32[]{:S(2)}, u32[]{:S(2)}) collective-permute-start(bf16[3,3,256,128]{3,2,1,0:T(8,128)(2,1)S(1)} %get-tuple-element.37), channel_id=1, source_target_pairs={{0,1},{1,2},{2,3},{4,5},{5,6},{6,7},{8,9},{9,10},{10,11},{12,13},{... | collective-permute-start | bytes 1769480 | tf_op jit(solution)/shard_map/ppermute | solution.py:296
  80.7 16.6 %collective-permute-start.3 = (bf16[3,3,256,128]{3,2,1,0:T(8,128)(2,1)S(1)}, bf16[3,3,256,128]{3,2,1,0:T(8,128)(2,1)}, u32[]{:S(2)}, u32[]{:S(2)}) collective-permute-start(bf16[3,3,256,128]{3,2,1,0:T(8,128)(2,1)S(1)} %get-tuple-element.36), channel_id=1, source_target_pairs={{1,0},{2,1},{3,2},{5,4},{6,5},{7,6},{9,8},{10,9},{11,10},{13,12},{... | collective-permute-start | bytes 1769480 | tf_op jit(solution)/shard_map/ppermute | solution.py:297
  86.8 24.5 %all-to-all-start.2 = ((s32[128,1,2]{2,1,0:T(1,128)}), s32[128,1,2]{2,1,0:T(1,128)S(1)}, u32[]{:S(2)}, u32[]{:S(2)}) async-start(s32[128,1,2]{2,1,0:T(1,128)} %copy.28), calls=%async_computation.2 | async-start | bytes 131072 | tf_op jit(solution)/shard_map/all_to_all | solution.py:302
  96.1 1.2 copy-start.7
  111.4 10.9 %copy-start.1 = (bf16[3,4,256,128]{3,2,1,0:T(8,128)(2,1)S(1)}, bf16[3,4,256,128]{3,2,1,0:T(8,128)(2,1)}, u32[]{:S(2)}) copy-start(bf16[3,4,256,128]{3,2,1,0:T(8,128)(2,1)} %get-tuple-element.25) | copy-start | bytes 2359300
  111.4 52.6 %all-to-all-start.3 = ((bf16[128,8,768]{2,1,0:T(8,128)(2,1)}), bf16[128,8,768]{2,1,0:T(8,128)(2,1)S(1)}, u32[]{:S(2)}, u32[]{:S(2)}) async-start(bf16[128,8,768]{2,1,0:T(8,128)(2,1)} %bitcast.30), calls=%async_computation.3 | async-start | bytes 3145728 | tf_op jit(solution)/shard_map/all_to_all | solution.py:302

commit v4 on v3

--- a/solution.py
+++ b/solution.py
@@ -59,24 +59,32 @@
     return own_hi, k - HALO - depth
 
 
-def prepare_kernel(turn, across, along, own, own_lo, own_hi, a10, dxa, dya):
+def prepare_kernel(
+    turn, across, along, own, own_lo, own_hi, a10, dxa_in, dya_in, dxa_out, dya_out
+):
     depth, _, cols = own.shape[1:]
     for k in range(depth + 2 * HALO):
         ref, at = plane_of(own, own_lo, own_hi, k)
         a = dot(ref[0, at], turn[...]).astype(BF16)
         a10[0, k] = a
         if 0 < k < depth + 2 * HALO - 1:
-            dxa[0, k - 1] = dot(a, across[...])
-            if k % 2 == 0:
-                dy = dot(along[...], jnp.concatenate([before, a], axis=1))
-                dya[0, k - 2] = dy[:, :cols]
-                dya[0, k - 1] = dy[:, cols:]
-        before = a
+            dx, dy, n = place_of(dxa_in, dya_in, dxa_out, dya_out, depth, k)
+            dx[0, n] = dot(a, across[...])
+            dy[0, n] = dot(along[...], a)
+
+
+def place_of(dx_in, dy_in, dx_out, dy_out, depth, k):
+    if k < HALO:
+        return dx_out, dy_out, k - 1
+    if k < HALO + depth:
+        return dx_in, dy_in, k - HALO
+    return dx_out, dy_out, k - 1 - depth
 
 
 def prepare(turn, across, along, own, own_lo, own_hi):
     chans, depth, rows, cols = own.shape
     wide = depth + 2 * HALO
+    edge = 2 * (HALO - 1)
 
     def spec(n):
         return pl.BlockSpec((1, n, rows, cols), lambda c: (c, 0, 0, 0))
@@ -92,11 +100,72 @@
         grid=(chans,),
         in_specs=[whole(turn), whole(across), whole(along)]
         + [spec(depth), spec(HALO), spec(HALO)],
-        out_specs=[spec(wide), spec(wide - 2), spec(wide - 2)],
-        out_shape=[shape(wide, BF16), shape(wide - 2, F32), shape(wide - 2, F32)],
+        out_specs=[spec(wide), spec(depth), spec(depth), spec(edge), spec(edge)],
+        out_shape=[shape(wide, BF16)]
+        + [shape(depth, F32)] * 2
+        + [shape(edge, F32)] * 2,
         compiler_params=pltpu.CompilerParams(vmem_limit_bytes=60 << 20),
         name="prepare",
     )(turn, across, along, own, own_lo, own_hi)
+
+
+def inner_kernel(across, along, a10, dxa, dya, fac, part, dxb, dyb):
+    depth, rows, cols = fac.shape[1:]
+    half = jnp.float32(0.5)
+    for z in range(depth):
+        now = fac[0, z]
+        dxb[z] = dot(now, across[...])
+        if z % 2 == 1:
+            dy = dot(along[...], jnp.concatenate([fac[0, z - 1], now], axis=1))
+            dyb[z - 1] = dy[:, :cols]
+            dyb[z] = dy[:, cols:]
+
+    step = 64
+
+    def chunk(r, carry):
+        at_rows = pl.ds(pl.multiple_of(r * step, step), step)
+        a = [a10[0, HALO + z, at_rows, :].astype(F32) for z in range(depth)]
+        b = [fac[0, z, at_rows, :].astype(F32) for z in range(depth)]
+        for z in range(depth):
+            ya, yb = dya[0, z, at_rows, :], dyb[z, at_rows, :]
+            xa, xb = dxa[0, z, at_rows, :], dxb[z, at_rows, :]
+            p1 = a[z] * b[z] + ya * yb + xa * xb
+            p2 = b[z] * b[z] + yb * yb + xb * xb
+            if 0 < z < depth - 1:
+                dza = (a[z + 1] - a[z - 1]) * half
+                dzb = (b[z + 1] - b[z - 1]) * half
+                p1, p2 = p1 + dza * dzb, p2 + dzb * dzb
+            part[0, 2 * z, at_rows, :] = p1
+            part[0, 2 * z + 1, at_rows, :] = p2
+        return carry
+
+    lax.fori_loop(0, rows // step, chunk, 0)
+
+
+def inner(across, along, a10, dxa, dya, fac):
+    chans, depth, rows, cols = fac.shape
+
+    def spec(n):
+        return pl.BlockSpec((1, n, rows, cols), lambda c: (c, 0, 0, 0))
+
+    def whole(m):
+        return pl.BlockSpec(m.shape, lambda c: (0, 0))
+
+    held = pltpu.VMEM((depth, rows, cols), F32)
+    return pl.pallas_call(
+        inner_kernel,
+        grid=(chans,),
+        in_specs=[whole(across), whole(along)]
+        + [spec(depth + 2 * HALO), spec(depth), spec(depth), spec(depth)],
+        out_specs=spec(2 * depth),
+        out_shape=jax.ShapeDtypeStruct((chans, 2 * depth, rows, cols), F32),
+        scratch_shapes=[held, held],
+        compiler_params=pltpu.CompilerParams(vmem_limit_bytes=60 << 20),
+        cost_estimate=pl.CostEstimate(
+            flops=1000000000, bytes_accessed=10000000, transcendentals=0
+        ),
+        name="inner",
+    )(across, along, a10, dxa, dya, fac)
 
 
 def pack(code, planes, out, held, sems):
@@ -128,6 +197,7 @@
     a10,
     dxa,
     dya,
+    part,
     own,
     fac,
     fac_lo,
@@ -146,14 +216,15 @@
     wide = depth + 2 * HALO
     low, high = flags[0], flags[1]
     half = jnp.float32(0.5)
-    for k in range(1, wide - 1):
+    for k in (1, 2, wide - 3, wide - 2):
         ref, at = plane_of(fac, fac_lo, fac_hi, k)
         now = ref[0, at]
-        dxb[k - 1] = dot(now, across[...])
-        if k % 2 == 0:
+        n = k - 1 if k < HALO else k - 1 - depth
+        dxb[n] = dot(now, across[...])
+        if n % 2 == 1:
             dy = dot(along[...], jnp.concatenate([before, now], axis=1))
-            dyb[k - 2] = dy[:, :cols]
-            dyb[k - 1] = dy[:, cols:]
+            dyb[n - 1] = dy[:, :cols]
+            dyb[n] = dy[:, cols:]
         before = now
 
     step = 32
@@ -170,17 +241,22 @@
 
         one = [None] * depth
         two = [None] * depth
-        a_last, av, a_next = None, a_of(0), a_of(1)
-        b_last, bv, b_next = None, b_of(0), b_of(1)
         for k in range(1, wide - 1):
-            a_last, av, a_next = av, a_next, a_of(k + 1)
-            b_last, bv, b_next = bv, b_next, b_of(k + 1)
-            dza = (a_next - a_last) * half
-            dzb = (b_next - b_last) * half
-            ya, yb = dya[0, k - 1, at_rows, :], dyb[k - 1, at_rows, :]
-            xa, xb = dxa[0, k - 1, at_rows, :], dxb[k - 1, at_rows, :]
-            p1 = av * bv + ya * yb + dza * dzb + xa * xb
-            p2 = bv * bv + yb * yb + dzb * dzb + xb * xb
+            z = k - HALO
+            if 0 <= z < depth:
+                p1, p2 = part[0, 2 * z, at_rows, :], part[0, 2 * z + 1, at_rows, :]
+            if not 0 < z < depth - 1:
+                dza = (a_of(k + 1) - a_of(k - 1)) * half
+                dzb = (b_of(k + 1) - b_of(k - 1)) * half
+                if 0 <= z < depth:
+                    p1, p2 = p1 + dza * dzb, p2 + dzb * dzb
+                else:
+                    n = k - 1 if k < HALO else k - 1 - depth
+                    av, bv = a_of(k), b_of(k)
+                    ya, yb = dya[0, n, at_rows, :], dyb[n, at_rows, :]
+                    xa, xb = dxa[0, n, at_rows, :], dxb[n, at_rows, :]
+                    p1 = av * bv + ya * yb + dza * dzb + xa * xb
+                    p2 = bv * bv + yb * yb + dzb * dzb + xb * xb
             if k < HALO:
                 p1, p2 = p1 * low, p2 * low
             if k >= HALO + depth:
@@ -220,7 +296,7 @@
 
 
 def correct(
-    flags, across, along, smooth_x, smooth_y, code, a10, dxa, dya, own, fac, fac_lo, fac_hi, blocks
+    flags, across, along, smooth_x, smooth_y, code, a10, dxa, dya, part, own, fac, fac_lo, fac_hi, blocks
 ):
     chans, depth, rows, cols = own.shape
     wide = depth + 2 * HALO
@@ -232,13 +308,14 @@
     def whole(m):
         return pl.BlockSpec(m.shape, lambda c: (0, 0))
 
-    inner = pltpu.VMEM((wide - 2, rows, cols), F32)
+    edge = 2 * (HALO - 1)
+    held = pltpu.VMEM((edge, rows, cols), F32)
     return pl.pallas_call(
         correct_kernel,
         grid=(chans,),
         in_specs=[pl.BlockSpec(memory_space=pltpu.SMEM)]
         + [whole(m) for m in (across, along, smooth_x, smooth_y, code)]
-        + [spec(wide), spec(wide - 2), spec(wide - 2)]
+        + [spec(wide), spec(edge), spec(edge), spec(2 * depth)]
         + [spec(depth), spec(depth), spec(HALO), spec(HALO)],
         out_specs=[spec(depth), pl.BlockSpec(memory_space=pltpu.HBM)],
         out_shape=[
@@ -246,8 +323,8 @@
             jax.ShapeDtypeStruct(packed, BF16),
         ],
         scratch_shapes=[
-            inner,
-            inner,
+            held,
+            held,
             pltpu.VMEM((2 * depth, rows, 2 * cols), BF16),
             pltpu.VMEM(own.shape, BF16),
             pltpu.VMEM(packed, BF16),
@@ -258,7 +335,7 @@
             flops=4000000000, bytes_accessed=12000000, transcendentals=0
         ),
         name="correct",
-    )(flags, across, along, smooth_x, smooth_y, code, a10, dxa, dya, own, fac, fac_lo, fac_hi)
+    )(flags, across, along, smooth_x, smooth_y, code, a10, dxa, dya, part, own, fac, fac_lo, fac_hi)
 
 
 def join_kernel(code, got, out):
@@ -337,15 +414,30 @@
     )
     smooth_x = smooth_x * (partner[tile] != tile).astype(BF16)
     flags = jnp.stack([plane_idx > 0, plane_idx < nplane - 1]).astype(F32)
-    a10, dxa, dya = prepare(turn, across, along, own, own_lo, own_hi)
-    fac, labels, code, a10, dxa, dya, smooth_x, flags = lax.optimization_barrier(
-        (fac, labels, code, a10, dxa, dya, smooth_x, flags)
+    a10, dxa_in, dya_in, dxa, dya = prepare(turn, across, along, own, own_lo, own_hi)
+    fac, labels, code, a10, dxa_in, dya_in, dxa, dya, smooth_x, flags = lax.optimization_barrier(
+        (fac, labels, code, a10, dxa_in, dya_in, dxa, dya, smooth_x, flags)
     )
     fac_lo, fac_hi = halo(fac)
     info = swap(labels)
 
+    part = inner(across, along, a10, dxa_in, dya_in, fac)
     corrected, outgoing = correct(
-        flags, across, along, smooth_x, smooth_y, code, a10, dxa, dya, own, fac, fac_lo, fac_hi, ntile
+        flags,
+        across,
+        along,
+        smooth_x,
+        smooth_y,
+        code,
+        a10,
+        dxa,
+        dya,
+        part,
+        own,
+        fac,
+        fac_lo,
+        fac_hi,
+        ntile,
     )
     received = swap(outgoing.reshape(ntile, 8, outgoing.shape[1]))
 

time: 167 us -> 172 us (1.030)
  Pallas kernels: 21.9 us -> 27.3 us
  waiting for transfers between devices: 76.8 us -> 71.9 us
  starting transfers between devices: 51.8 us -> 55.4 us
    pallas_call x0 -> x1, Pallas kernels: none -> 6.09 us  [inner(): pl.pallas_call(inner_kernel, grid=(chans,), in_specs=[whole(across), whol...]
    all_to_all x4, starting transfers between devices: 39.2 us -> 42.9 us  [swap(): lax.all_to_all(blocks, 'tile', split_axis=0, concat_axis=0, tiled=True)]
    ppermute x2, waiting for transfers between devices: 3.46 us -> 0.01 us  [halo(): low = lax.ppermute(block[:, depth - HALO:], 'gz', forward)]
  transfers between devices with their start and end apart: 8 -> 8, of which waited for: 5 -> 3; matrix products, arithmetic and copies ran while one was open for 5% -> 5% of each run, Pallas kernels for 12% -> 15%
where the time goes in v4:
time: 172 us
  waiting for transfers between devices  71.9 us (42%)
  starting transfers between devices  55.4 us (32%)
  Pallas kernels  27.3 us (16%)
  local copies, waits for them, and re-layouts  12.9 us (8%)
  other arithmetic  2.43 us (1%)
    all_to_all x4, waiting for transfers between devices, swap(): lax.all_to_all(blocks, 'tile', split_axis=0, concat_axis=0, tiled=True)  71.9 us
    all_to_all x4, starting transfers between devices, swap(): lax.all_to_all(blocks, 'tile', split_axis=0, concat_axis=0, tiled=True)  42.9 us
    pallas_call x1, Pallas kernels, correct(): pl.pallas_call(correct_kernel, grid=(chans,), in_specs=[pl.BlockSpec(memo...  13 us
    ppermute x2, starting transfers between devices, halo(): high = lax.ppermute(block[:, :HALO], 'gz', backward)  9.96 us
    pallas_call x1, Pallas kernels, prepare(): pl.pallas_call(prepare_kernel, grid=(chans,), in_specs=[whole(turn), whol...  7.16 us
    unnamed x23, local copies, waits for them, and re-layouts  6.26 us
    pallas_call x1, Pallas kernels, inner(): pl.pallas_call(inner_kernel, grid=(chans,), in_specs=[whole(across), whol...  6.09 us
  transfers between devices with their start and end apart: 8, of which 3 were waited for; matrix products, arithmetic and copies ran while one was open for 5% of the time, Pallas kernels for 15%

profile of v4, /device:TPU:14, one launch (start us, length us, event | category | flops | bytes accessed | tf_op | source)
XLA Modules:
  0.0 171.5 jit_solution(8543265891141329093)
XLA Ops:
  0.6 2.1 %copy.40 = bf16[256,3,4,128]{3,0,2,1:T(8,128)(2,1)} copy(bf16[256,3,4,128]{3,2,1,0:T(4,128)(2,1)} %param.10) | data formatting | bytes 1572864 | tf_op args[0]
  2.8 17.4 %all-to-all-start = ((bf16[128,24,128]{2,1,0:T(8,128)(2,1)}), bf16[128,24,128]{2,1,0:T(8,128)(2,1)S(1)}, u32[]{:S(2)}, u32[]{:S(2)}) async-start(bf16[128,24,128]{2,1,0:T(8,128)(2,1)} %bitcast.1), calls=%async_computation | async-start | bytes 1572864 | tf_op jit(solution)/shard_map/all_to_all | solution.py:379
  20.2 0.0 copy-start.5
  20.2 0.0 copy-start.6
  20.2 1.3 fusion.5
  21.5 1.3 collective-permute-start
  22.8 4.6 %collective-permute-start.1 = (bf16[3,3,256,128]{3,2,1,0:T(8,128)(2,1)S(1)}, bf16[3,3,256,128]{3,2,1,0:T(8,128)(2,1)S(1)}, u32[]{:S(2)}, u32[]{:S(2)}) collective-permute-start(bf16[3,3,256,128]{3,2,1,0:T(8,128)(2,1)S(1)} %get-tuple-element.46), channel_id=1, source_target_pairs={{1,0},{2,1},{3,2},{5,4},{6,5},{7,6},{9,8},{10,9},{11,10},{13,12},{... | collective-permute-start | bytes 1769480 | tf_op jit(solution)/shard_map/ppermute | solution.py:374
  27.4 0.2 convert_reduce_fusion
  27.6 0.0 copy-start.8
  27.6 0.0 copy-start.9
  27.6 0.0 copy-start.4
  27.7 18.3 %all-to-all-done = bf16[128,24,128]{2,1,0:T(8,128)(2,1)S(1)} async-done(((bf16[128,24,128]{2,1,0:T(8,128)(2,1)}), bf16[128,24,128]{2,1,0:T(8,128)(2,1)S(1)}, u32[]{:S(2)}, u32[]{:S(2)}) %all-to-all-start) | async-done | bytes 786464 | tf_op jit(solution)/shard_map/all_to_all | solution.py:379
  45.9 1.6 gather_fusion
  47.5 5.8 %all-to-all-start.1 = ((bf16[128,24,128]{2,1,0:T(8,128)(2,1)}), bf16[128,24,128]{2,1,0:T(8,128)(2,1)S(1)}, u32[]{:S(2)}, u32[]{:S(2)}) async-start(bf16[128,24,128]{2,1,0:T(8,128)(2,1)} %gather_fusion), calls=%async_computation.1 | async-start | bytes 1572864 | tf_op jit(solution)/shard_map/all_to_all | solution.py:379
  53.3 0.1 iota_add_fusion
  53.4 0.1 add.93
  53.6 0.6 pad_add_fusion.1.code
  54.2 0.6 add_convert_fusion.flags
  54.8 0.6 dynamic_slice.3
  56.1 0.1 select_reduce_fusion
  56.2 0.7 broadcast_multiply_fusion.smooth_x
  56.9 0.0 collective-permute-done.own_lo
  56.9 0.8 copy-done.2
  57.7 0.8 copy-done.3
  58.5 7.2 %prepare.1 = (bf16[3,10,256,128]{3,2,1,0:T(8,128)(2,1)}, f32[3,4,256,128]{3,2,1,0:T(8,128)}, f32[3,4,256,128]{3,2,1,0:T(8,128)}, f32[3,4,256,128]{3,2,1,0:T(8,128)}, f32[3,4,256,128]{3,2,1,0:T(8,128)}) custom-call(bf16[128,128]{1,0:T(8,128)(2,1)} %constant.58.clone.turn, bf16[128,128]{1,0:T(8,128)(2,1)} %constant.59.clone.across, ...), custom_call_target="tpu_custom_call" | custom-call | tf_op jit(solution)/shard_map/prepare/pallas_call | solution.py:98
  65.7 13.4 %all-to-all-done.1 = bf16[128,24,128]{2,1,0:T(8,128)(2,1)S(1)} async-done(((bf16[128,24,128]{2,1,0:T(8,128)(2,1)}), bf16[128,24,128]{2,1,0:T(8,128)(2,1)S(1)}, u32[]{:S(2)}, u32[]{:S(2)}) %all-to-all-start.1) | async-done | bytes 786464 | tf_op jit(solution)/shard_map/all_to_all | solution.py:379
  79.1 0.2 fusion.4
  79.3 1.3 collective-permute-start.2
  80.6 5.4 %collective-permute-start.3 = (bf16[3,3,256,128]{3,2,1,0:T(8,128)(2,1)S(1)}, bf16[3,3,256,128]{3,2,1,0:T(8,128)(2,1)}, u32[]{:S(2)}, u32[]{:S(2)}) collective-permute-start(bf16[3,3,256,128]{3,2,1,0:T(8,128)(2,1)S(1)} %get-tuple-element.44), channel_id=1, source_target_pairs={{1,0},{2,1},{3,2},{5,4},{6,5},{7,6},{9,8},{10,9},{11,10},{13,12},{... | collective-permute-start | bytes 1769480 | tf_op jit(solution)/shard_map/ppermute | solution.py:374
  86.0 0.8 copy.28
  86.7 5.8 %all-to-all-start.2 = ((s32[128,1,2]{2,1,0:T(1,128)}), s32[128,1,2]{2,1,0:T(1,128)S(1)}, u32[]{:S(2)}, u32[]{:S(2)}) async-start(s32[128,1,2]{2,1,0:T(1,128)} %copy.28), calls=%async_computation.2 | async-start | bytes 131072 | tf_op jit(solution)/shard_map/all_to_all | solution.py:379
  92.6 6.1 %inner.1.part = f32[3,8,256,128]{3,2,1,0:T(8,128)} custom-call(bf16[128,128]{1,0:T(8,128)(2,1)} %constant.59.clone.across, bf16[256,256]{1,0:T(8,128)(2,1)} %constant.60.clone.along, bf16[3,10,256,128]{3,2,1,0:T(8,128)(2,1)} %get-tuple-element.27.a10, f32[3,4,256,128]{3,2,1,0:T(8,128)} %get-tuple-element.30.dxa, f32[3,4,256,128]{3,2,1,0:T(8,128)} %get-tuple-element.31.dya, ...), custom_call_target="tpu_custom_call" | custom-call | flops 1000000000 | bytes 10000000 | tf_op jit(solution)/shard_map/inner/pallas_call | solution.py:155
  98.7 0.8 copy-done.7
  99.5 13.0 %correct.1 = (bf16[3,4,256,128]{3,2,1,0:T(8,128)(2,1)}, bf16[1024,768]{1,0:T(8,128)(2,1)}) custom-call(f32[2]{0:T(128)} %add_convert_fusion.flags, bf16[128,128]{1,0:T(8,128)(2,1)} %constant.59.clone.across, bf16[256,256]{1,0:T(8,128)(2,1)} %constant.60.clone.along, bf16[256,256]{1,0:T(8,128)(2,1)} %broadcast_multiply_fusion.smooth_x, ...), custom_call_target="tpu_custom_call" | custom-call | flops 4000000000 | bytes 12000000 | tf_op jit(solution)/shard_map/correct/pallas_call | solution.py:313
  112.5 13.9 %all-to-all-start.3 = ((bf16[128,8,768]{2,1,0:T(8,128)(2,1)}), bf16[128,8,768]{2,1,0:T(8,128)(2,1)S(1)}, u32[]{:S(2)}, u32[]{:S(2)}) async-start(bf16[128,8,768]{2,1,0:T(8,128)(2,1)} %bitcast.31), calls=%async_computation.3 | async-start | bytes 3145728 | tf_op jit(solution)/shard_map/all_to_all | solution.py:379
  126.4 0.1 lt.41
  126.4 0.1 add_select_fusion.1
  126.5 0.1 copy.30
  126.6 0.1 copy.29
  126.7 0.1 add_select_fusion.2
  126.7 0.1 copy.35
  126.9 0.1 fusion.6
  126.9 0.1 stack_reshape.7
  127.1 0.1 stack_reshape.6
  127.2 1.5 copy.34
  128.7 40.2 %all-to-all-done.3 = bf16[128,8,768]{2,1,0:T(8,128)(2,1)S(1)} async-done(((bf16[128,8,768]{2,1,0:T(8,128)(2,1)}), bf16[128,8,768]{2,1,0:T(8,128)(2,1)S(1)}, u32[]{:S(2)}, u32[]{:S(2)}) %all-to-all-start.3) | async-done | bytes 1572896 | tf_op jit(solution)/shard_map/all_to_all | solution.py:379
  168.9 1.1 join.1
  170.1 1.5 copy.39
  (26 shorter events, 0.1 us)
Async XLA Ops:
  2.8 43.1 %all-to-all-start = ((bf16[128,24,128]{2,1,0:T(8,128)(2,1)}), bf16[128,24,128]{2,1,0:T(8,128)(2,1)S(1)}, u32[]{:S(2)}, u32[]{:S(2)}) async-start(bf16[128,24,128]{2,1,0:T(8,128)(2,1)} %bitcast.1), calls=%async_computation | async-start | bytes 1572864 | tf_op jit(solution)/shard_map/all_to_all | solution.py:379
  20.2 7.2 %copy-start.5 = (s32[128]{0:T(128)S(1)}, s32[128]{0:T(128)}, u32[]{:S(2)}) copy-start(s32[128]{0:T(128)} %param.11) | copy-start | bytes 1540
  20.2 7.3 %copy-start.6 = (s32[128,1]{0,1:T(1,128)S(1)}, s32[128,1]{0,1:T(1,128)}, u32[]{:S(2)}) copy-start(s32[128,1]{0,1:T(1,128)} %param.12) | copy-start | bytes 1540
  21.5 35.4 %collective-permute-start = (bf16[3,3,256,128]{3,2,1,0:T(8,128)(2,1)S(1)}, bf16[3,3,256,128]{3,2,1,0:T(8,128)(2,1)S(1)}, u32[]{:S(2)}, u32[]{:S(2)}) collective-permute-start(bf16[3,3,256,128]{3,2,1,0:T(8,128)(2,1)S(1)} %get-tuple-element.47), channel_id=1, source_target_pairs={{0,1},{1,2},{2,3},{4,5},{5,6},{6,7},{8,9},{9,10},{10,11},{12,13},{... | collective-permute-start | bytes 1769480 | tf_op jit(solution)/shard_map/ppermute | solution.py:373
  22.8 34.1 %collective-permute-start.1 = (bf16[3,3,256,128]{3,2,1,0:T(8,128)(2,1)S(1)}, bf16[3,3,256,128]{3,2,1,0:T(8,128)(2,1)S(1)}, u32[]{:S(2)}, u32[]{:S(2)}) collective-permute-start(bf16[3,3,256,128]{3,2,1,0:T(8,128)(2,1)S(1)} %get-tuple-element.46), channel_id=1, source_target_pairs={{1,0},{2,1},{3,2},{5,4},{6,5},{7,6},{9,8},{10,9},{11,10},{13,12},{... | collective-permute-start | bytes 1769480 | tf_op jit(solution)/shard_map/ppermute | solution.py:374
  27.6 26.5 %copy-start.8 = (s32[128]{0:T(128)S(1)}, s32[128]{0:T(128)}, u32[]{:S(2)}) copy-start(s32[128]{0:T(128)} %param.14) | copy-start | bytes 1540
  27.6 26.5 %copy-start.9 = (s32[128]{0:T(128)S(1)}, s32[128]{0:T(128)}, u32[]{:S(2)}) copy-start(s32[128]{0:T(128)} %param.13) | copy-start | bytes 1540
  27.6 28.5 %copy-start.4 = (bf16[256,256]{1,0:T(8,128)(2,1)S(1)}, bf16[256,256]{1,0:T(8,128)(2,1)}, u32[]{:S(2)}) copy-start(bf16[256,256]{1,0:T(8,128)(2,1)} %constant.61.clone) | copy-start | bytes 393220
  47.5 31.6 %all-to-all-start.1 = ((bf16[128,24,128]{2,1,0:T(8,128)(2,1)}), bf16[128,24,128]{2,1,0:T(8,128)(2,1)S(1)}, u32[]{:S(2)}, u32[]{:S(2)}) async-start(bf16[128,24,128]{2,1,0:T(8,128)(2,1)} %gather_fusion), calls=%async_computation.1 | async-start | bytes 1572864 | tf_op jit(solution)/shard_map/all_to_all | solution.py:379
  56.9 0.8 copy-start.2
  57.7 0.8 copy-start.3
  79.1 13.5 %copy-start = (bf16[128,24,128]{2,1,0:T(8,128)(2,1)}, bf16[128,24,128]{2,1,0:T(8,128)(2,1)S(1)}, u32[]{:S(2)}) copy-start(bf16[128,24,128]{2,1,0:T(8,128)(2,1)S(1)} %all-to-all-done.1) | copy-start | bytes 2359300
  79.3 19.4 %collective-permute-start.2 = (bf16[3,3,256,128]{3,2,1,0:T(8,128)(2,1)S(1)}, bf16[3,3,256,128]{3,2,1,0:T(8,128)(2,1)S(1)}, u32[]{:S(2)}, u32[]{:S(2)}) collective-permute-start(bf16[3,3,256,128]{3,2,1,0:T(8,128)(2,1)S(1)} %get-tuple-element.45), channel_id=1, source_target_pairs={{0,1},{1,2},{2,3},{4,5},{5,6},{6,7},{8,9},{9,10},{10,11},{12,13},{... | collective-permute-start | bytes 1769480 | tf_op jit(solution)/shard_map/ppermute | solution.py:373
  80.6 18.1 %collective-permute-start.3 = (bf16[3,3,256,128]{3,2,1,0:T(8,128)(2,1)S(1)}, bf16[3,3,256,128]{3,2,1,0:T(8,128)(2,1)}, u32[]{:S(2)}, u32[]{:S(2)}) collective-permute-start(bf16[3,3,256,128]{3,2,1,0:T(8,128)(2,1)S(1)} %get-tuple-element.44), channel_id=1, source_target_pairs={{1,0},{2,1},{3,2},{5,4},{6,5},{7,6},{9,8},{10,9},{11,10},{13,12},{... | collective-permute-start | bytes 1769480 | tf_op jit(solution)/shard_map/ppermute | solution.py:374
  86.7 25.7 %all-to-all-start.2 = ((s32[128,1,2]{2,1,0:T(1,128)}), s32[128,1,2]{2,1,0:T(1,128)S(1)}, u32[]{:S(2)}, u32[]{:S(2)}) async-start(s32[128,1,2]{2,1,0:T(1,128)} %copy.28), calls=%async_computation.2 | async-start | bytes 131072 | tf_op jit(solution)/shard_map/all_to_all | solution.py:379
  98.7 0.8 copy-start.7
  112.5 14.7 %copy-start.1 = (bf16[3,4,256,128]{3,2,1,0:T(8,128)(2,1)S(1)}, bf16[3,4,256,128]{3,2,1,0:T(8,128)(2,1)}, u32[]{:S(2)}) copy-start(bf16[3,4,256,128]{3,2,1,0:T(8,128)(2,1)} %get-tuple-element.33) | copy-start | bytes 2359300
  112.5 56.4 %all-to-all-start.3 = ((bf16[128,8,768]{2,1,0:T(8,128)(2,1)}), bf16[128,8,768]{2,1,0:T(8,128)(2,1)S(1)}, u32[]{:S(2)}, u32[]{:S(2)}) async-start(bf16[128,8,768]{2,1,0:T(8,128)(2,1)} %bitcast.31), calls=%async_computation.3 | async-start | bytes 3145728 | tf_op jit(solution)/shard_map/all_to_all | solution.py:379

commit v5 on v4

--- a/solution.py
+++ b/solution.py
@@ -59,76 +59,62 @@
     return own_hi, k - HALO - depth
 
 
-def prepare_kernel(
-    turn, across, along, own, own_lo, own_hi, a10, dxa_in, dya_in, dxa_out, dya_out
-):
-    depth, _, cols = own.shape[1:]
+def prepare_kernel(turn, own, own_lo, own_hi, a_in, a_out):
+    depth = own.shape[1]
     for k in range(depth + 2 * HALO):
         ref, at = plane_of(own, own_lo, own_hi, k)
         a = dot(ref[0, at], turn[...]).astype(BF16)
-        a10[0, k] = a
-        if 0 < k < depth + 2 * HALO - 1:
-            dx, dy, n = place_of(dxa_in, dya_in, dxa_out, dya_out, depth, k)
-            dx[0, n] = dot(a, across[...])
-            dy[0, n] = dot(along[...], a)
-
-
-def place_of(dx_in, dy_in, dx_out, dy_out, depth, k):
-    if k < HALO:
-        return dx_out, dy_out, k - 1
-    if k < HALO + depth:
-        return dx_in, dy_in, k - HALO
-    return dx_out, dy_out, k - 1 - depth
-
-
-def prepare(turn, across, along, own, own_lo, own_hi):
+        if HALO <= k < HALO + depth:
+            a_in[0, k - HALO] = a
+        else:
+            a_out[0, k if k < HALO else k - depth] = a
+
+
+def prepare(turn, own, own_lo, own_hi):
     chans, depth, rows, cols = own.shape
-    wide = depth + 2 * HALO
-    edge = 2 * (HALO - 1)
 
     def spec(n):
         return pl.BlockSpec((1, n, rows, cols), lambda c: (c, 0, 0, 0))
 
-    def whole(m):
-        return pl.BlockSpec(m.shape, lambda c: (0, 0))
-
-    def shape(n, dtype):
-        return jax.ShapeDtypeStruct((chans, n, rows, cols), dtype)
+    def shape(n):
+        return jax.ShapeDtypeStruct((chans, n, rows, cols), BF16)
 
     return pl.pallas_call(
         prepare_kernel,
         grid=(chans,),
-        in_specs=[whole(turn), whole(across), whole(along)]
+        in_specs=[pl.BlockSpec(turn.shape, lambda c: (0, 0))]
         + [spec(depth), spec(HALO), spec(HALO)],
-        out_specs=[spec(wide), spec(depth), spec(depth), spec(edge), spec(edge)],
-        out_shape=[shape(wide, BF16)]
-        + [shape(depth, F32)] * 2
-        + [shape(edge, F32)] * 2,
+        out_specs=[spec(depth), spec(2 * HALO)],
+        out_shape=[shape(depth), shape(2 * HALO)],
         compiler_params=pltpu.CompilerParams(vmem_limit_bytes=60 << 20),
         name="prepare",
-    )(turn, across, along, own, own_lo, own_hi)
-
-
-def inner_kernel(across, along, a10, dxa, dya, fac, part, dxb, dyb):
-    depth, rows, cols = fac.shape[1:]
+    )(turn, own, own_lo, own_hi)
+
+
+def differences(a, f, across, along, n, dxa, dxb, dya, dyb):
+    cols = a.shape[1]
+    dxa[n] = dot(a, across[...])
+    dxb[n] = dot(f, across[...])
+    dy = dot(along[...], jnp.concatenate([a, f], axis=1))
+    dya[n] = dy[:, :cols]
+    dyb[n] = dy[:, cols:]
+
+
+def inner_kernel(across, along, own, fac, part, dxa, dxb, dya, dyb):
+    depth, rows, _ = fac.shape[1:]
     half = jnp.float32(0.5)
     for z in range(depth):
-        now = fac[0, z]
-        dxb[z] = dot(now, across[...])
-        if z % 2 == 1:
-            dy = dot(along[...], jnp.concatenate([fac[0, z - 1], now], axis=1))
-            dyb[z - 1] = dy[:, :cols]
-            dyb[z] = dy[:, cols:]
+        differences(own[0, z], fac[0, z], across, along, z, dxa, dxb, dya, dyb)
 
     step = 64
 
     def chunk(r, carry):
         at_rows = pl.ds(pl.multiple_of(r * step, step), step)
-        a = [a10[0, HALO + z, at_rows, :].astype(F32) for z in range(depth)]
+        a = [own[0, z, at_rows, :].astype(F32) for z in range(depth)]
         b = [fac[0, z, at_rows, :].astype(F32) for z in range(depth)]
         for z in range(depth):
-            ya, yb = dya[0, z, at_rows, :], dyb[z, at_rows, :]
-            xa, xb = dxa[0, z, at_rows, :], dxb[z, at_rows, :]
+            ya, yb = dya[z, at_rows, :], dyb[z, at_rows, :]
+            xa, xb = dxa[z, at_rows, :], dxb[z, at_rows, :]
             p1 = a[z] * b[z] + ya * yb + xa * xb
             p2 = b[z] * b[z] + yb * yb + xb * xb
             if 0 < z < depth - 1:
@@ -142,7 +128,7 @@
     lax.fori_loop(0, rows // step, chunk, 0)
 
 
-def inner(across, along, a10, dxa, dya, fac):
+def inner(across, along, own, fac):
     chans, depth, rows, cols = fac.shape
 
     def spec(n):
@@ -151,21 +137,19 @@
     def whole(m):
         return pl.BlockSpec(m.shape, lambda c: (0, 0))
 
-    held = pltpu.VMEM((depth, rows, cols), F32)
     return pl.pallas_call(
         inner_kernel,
         grid=(chans,),
-        in_specs=[whole(across), whole(along)]
-        + [spec(depth + 2 * HALO), spec(depth), spec(depth), spec(depth)],
+        in_specs=[whole(across), whole(along), spec(depth), spec(depth)],
         out_specs=spec(2 * depth),
         out_shape=jax.ShapeDtypeStruct((chans, 2 * depth, rows, cols), F32),
-        scratch_shapes=[held, held],
+        scratch_shapes=[pltpu.VMEM((depth, rows, cols), F32)] * 4,
         compiler_params=pltpu.CompilerParams(vmem_limit_bytes=60 << 20),
         cost_estimate=pl.CostEstimate(
             flops=1000000000, bytes_accessed=10000000, transcendentals=0
         ),
         name="inner",
-    )(across, along, a10, dxa, dya, fac)
+    )(across, along, own, fac)
 
 
 def pack(code, planes, out, held, sems):
@@ -194,9 +178,8 @@
     smooth_x,
     smooth_y,
     code,
-    a10,
-    dxa,
-    dya,
+    a_in,
+    a_out,
     part,
     own,
     fac,
@@ -204,7 +187,9 @@
     fac_hi,
     out,
     sent,
+    dxa,
     dxb,
+    dya,
     dyb,
     deep,
     kept,
@@ -216,16 +201,18 @@
     wide = depth + 2 * HALO
     low, high = flags[0], flags[1]
     half = jnp.float32(0.5)
+    def a_at(k):
+        if k < HALO:
+            return a_out, k
+        if k < HALO + depth:
+            return a_in, k - HALO
+        return a_out, k - depth
+
     for k in (1, 2, wide - 3, wide - 2):
+        own_ref, own_at = a_at(k)
         ref, at = plane_of(fac, fac_lo, fac_hi, k)
-        now = ref[0, at]
         n = k - 1 if k < HALO else k - 1 - depth
-        dxb[n] = dot(now, across[...])
-        if n % 2 == 1:
-            dy = dot(along[...], jnp.concatenate([before, now], axis=1))
-            dyb[n - 1] = dy[:, :cols]
-            dyb[n] = dy[:, cols:]
-        before = now
+        differences(own_ref[0, own_at], ref[0, at], across, along, n, dxa, dxb, dya, dyb)
 
     step = 32
 
@@ -233,7 +220,8 @@
         at_rows = pl.ds(pl.multiple_of(r * step, step), step)
 
         def a_of(k):
-            return a10[0, k, at_rows, :].astype(F32)
+            ref, at = a_at(k)
+            return ref[0, at, at_rows, :].astype(F32)
 
         def b_of(k):
             ref, at = plane_of(fac, fac_lo, fac_hi, k)
@@ -253,8 +241,8 @@
                 else:
                     n = k - 1 if k < HALO else k - 1 - depth
                     av, bv = a_of(k), b_of(k)
-                    ya, yb = dya[0, n, at_rows, :], dyb[n, at_rows, :]
-                    xa, xb = dxa[0, n, at_rows, :], dxb[n, at_rows, :]
+                    ya, yb = dya[n, at_rows, :], dyb[n, at_rows, :]
+                    xa, xb = dxa[n, at_rows, :], dxb[n, at_rows, :]
                     p1 = av * bv + ya * yb + dza * dzb + xa * xb
                     p2 = bv * bv + yb * yb + dzb * dzb + xb * xb
             if k < HALO:
@@ -296,10 +284,9 @@
 
 
 def correct(
-    flags, across, along, smooth_x, smooth_y, code, a10, dxa, dya, part, own, fac, fac_lo, fac_hi, blocks
+    flags, across, along, smooth_x, smooth_y, code, a_in, a_out, part, own, fac, fac_lo, fac_hi, blocks
 ):
     chans, depth, rows, cols = own.shape
-    wide = depth + 2 * HALO
     packed = (blocks * 8, chans * depth // 2 * cols)
 
     def spec(n):
@@ -315,7 +302,7 @@
         grid=(chans,),
         in_specs=[pl.BlockSpec(memory_space=pltpu.SMEM)]
         + [whole(m) for m in (across, along, smooth_x, smooth_y, code)]
-        + [spec(wide), spec(edge), spec(edge), spec(2 * depth)]
+        + [spec(depth), spec(2 * HALO), spec(2 * depth)]
         + [spec(depth), spec(depth), spec(HALO), spec(HALO)],
         out_specs=[spec(depth), pl.BlockSpec(memory_space=pltpu.HBM)],
         out_shape=[
@@ -323,6 +310,8 @@
             jax.ShapeDtypeStruct(packed, BF16),
         ],
         scratch_shapes=[
+            held,
+            held,
             held,
             held,
             pltpu.VMEM((2 * depth, rows, 2 * cols), BF16),
@@ -335,7 +324,7 @@
             flops=4000000000, bytes_accessed=12000000, transcendentals=0
         ),
         name="correct",
-    )(flags, across, along, smooth_x, smooth_y, code, a10, dxa, dya, part, own, fac, fac_lo, fac_hi)
+    )(flags, across, along, smooth_x, smooth_y, code, a_in, a_out, part, own, fac, fac_lo, fac_hi)
 
 
 def join_kernel(code, got, out):
@@ -414,14 +403,14 @@
     )
     smooth_x = smooth_x * (partner[tile] != tile).astype(BF16)
     flags = jnp.stack([plane_idx > 0, plane_idx < nplane - 1]).astype(F32)
-    a10, dxa_in, dya_in, dxa, dya = prepare(turn, across, along, own, own_lo, own_hi)
-    fac, labels, code, a10, dxa_in, dya_in, dxa, dya, smooth_x, flags = lax.optimization_barrier(
-        (fac, labels, code, a10, dxa_in, dya_in, dxa, dya, smooth_x, flags)
+    a_in, a_out = prepare(turn, own, own_lo, own_hi)
+    fac, labels, code, a_in, a_out, smooth_x, flags = lax.optimization_barrier(
+        (fac, labels, code, a_in, a_out, smooth_x, flags)
     )
     fac_lo, fac_hi = halo(fac)
     info = swap(labels)
 
-    part = inner(across, along, a10, dxa_in, dya_in, fac)
+    part = inner(across, along, a_in, fac)
     corrected, outgoing = correct(
         flags,
         across,
@@ -429,9 +418,8 @@
         smooth_x,
         smooth_y,
         code,
-        a10,
-        dxa,
-        dya,
+        a_in,
+        a_out,
         part,
         own,
         fac,

time: 172 us -> 171 us (level)
  Pallas kernels: 27.3 us -> 22.9 us
  waiting for transfers between devices: 71.9 us -> 75 us
    all_to_all x4, waiting for transfers between devices: 71.9 us -> 75 us  [swap(): lax.all_to_all(blocks, 'tile', split_axis=0, concat_axis=0, tiled=True)]
    pallas_call x1, Pallas kernels: 7.16 us -> 4.1 us  [prepare(): pl.pallas_call(prepare_kernel, grid=(chans,), in_specs=[pl.BlockSpec(turn...]
  transfers between devices with their start and end apart: 8 -> 8, of which waited for: 3 -> 3; matrix products, arithmetic and copies ran while one was open for 5% -> 5% of each run, Pallas kernels for 15% -> 13%
where the time goes in v5:
time: 171 us; the launch traced here: 170 us
  waiting for transfers between devices  75 us (44%)
  starting transfers between devices  55.4 us (32%)
  Pallas kernels  22.9 us (13%)
  local copies, waits for them, and re-layouts  12.9 us (8%)
  other arithmetic  2.35 us (1%)
    all_to_all x4, waiting for transfers between devices, swap(): lax.all_to_all(blocks, 'tile', split_axis=0, concat_axis=0, tiled=True)  75 us
    all_to_all x4, starting transfers between devices, swap(): lax.all_to_all(blocks, 'tile', split_axis=0, concat_axis=0, tiled=True)  42.9 us
    pallas_call x1, Pallas kernels, correct(): pl.pallas_call(correct_kernel, grid=(chans,), in_specs=[pl.BlockSpec(memo...  12.8 us
    ppermute x2, starting transfers between devices, halo(): high = lax.ppermute(block[:, :HALO], 'gz', backward)  9.99 us
    unnamed x23, local copies, waits for them, and re-layouts  6.32 us
    pallas_call x1, Pallas kernels, inner(): pl.pallas_call(inner_kernel, grid=(chans,), in_specs=[whole(across), whol...  4.96 us
    pallas_call x1, Pallas kernels, prepare(): pl.pallas_call(prepare_kernel, grid=(chans,), in_specs=[pl.BlockSpec(turn...  4.1 us
  transfers between devices with their start and end apart: 8, of which 3 were waited for; matrix products, arithmetic and copies ran while one was open for 5% of the time, Pallas kernels for 13%

profile of v5, /device:TPU:14, one launch (start us, length us, event | category | flops | bytes accessed | tf_op | source)
XLA Modules:
  0.0 170.3 jit_solution(3430691624162090582)
XLA Ops:
  0.6 2.1 %copy.40 = bf16[256,3,4,128]{3,0,2,1:T(8,128)(2,1)} copy(bf16[256,3,4,128]{3,2,1,0:T(4,128)(2,1)} %param.10) | data formatting | bytes 1572864 | tf_op args[0]
  2.8 17.4 %all-to-all-start = ((bf16[128,24,128]{2,1,0:T(8,128)(2,1)}), bf16[128,24,128]{2,1,0:T(8,128)(2,1)S(1)}, u32[]{:S(2)}, u32[]{:S(2)}) async-start(bf16[128,24,128]{2,1,0:T(8,128)(2,1)} %bitcast.1), calls=%async_computation | async-start | bytes 1572864 | tf_op jit(solution)/shard_map/all_to_all | solution.py:368
  20.2 0.0 copy-start.5
  20.2 0.0 copy-start.6
  20.2 1.4 fusion.5
  21.5 1.3 collective-permute-start
  22.8 4.6 %collective-permute-start.1 = (bf16[3,3,256,128]{3,2,1,0:T(8,128)(2,1)S(1)}, bf16[3,3,256,128]{3,2,1,0:T(8,128)(2,1)S(1)}, u32[]{:S(2)}, u32[]{:S(2)}) collective-permute-start(bf16[3,3,256,128]{3,2,1,0:T(8,128)(2,1)S(1)} %get-tuple-element.34), channel_id=1, source_target_pairs={{1,0},{2,1},{3,2},{5,4},{6,5},{7,6},{9,8},{10,9},{11,10},{13,12},{... | collective-permute-start | bytes 1769480 | tf_op jit(solution)/shard_map/ppermute | solution.py:363
  27.5 0.2 convert_reduce_fusion
  27.6 0.0 copy-start.8
  27.7 0.0 copy-start.9
  27.7 0.0 copy-start.4
  27.7 18.2 %all-to-all-done = bf16[128,24,128]{2,1,0:T(8,128)(2,1)S(1)} async-done(((bf16[128,24,128]{2,1,0:T(8,128)(2,1)}), bf16[128,24,128]{2,1,0:T(8,128)(2,1)S(1)}, u32[]{:S(2)}, u32[]{:S(2)}) %all-to-all-start) | async-done | bytes 786464 | tf_op jit(solution)/shard_map/all_to_all | solution.py:368
  45.9 1.6 gather_fusion
  47.5 5.8 %all-to-all-start.1 = ((bf16[128,24,128]{2,1,0:T(8,128)(2,1)}), bf16[128,24,128]{2,1,0:T(8,128)(2,1)S(1)}, u32[]{:S(2)}, u32[]{:S(2)}) async-start(bf16[128,24,128]{2,1,0:T(8,128)(2,1)} %gather_fusion), calls=%async_computation.1 | async-start | bytes 1572864 | tf_op jit(solution)/shard_map/all_to_all | solution.py:368
  53.3 0.1 iota_add_fusion
  53.4 0.1 add.93
  53.6 0.5 pad_add_fusion.1.code
  54.1 0.6 add_convert_fusion.flags
  54.7 0.6 dynamic_slice.3
  56.0 0.1 select_reduce_fusion
  56.1 0.7 broadcast_multiply_fusion.smooth_x
  56.8 0.8 copy-done.2
  57.6 0.8 copy-done.3
  58.5 4.1 %prepare.1 = (bf16[3,4,256,128]{3,2,1,0:T(8,128)(2,1)}, bf16[3,6,256,128]{3,2,1,0:T(8,128)(2,1)}) custom-call(bf16[128,128]{1,0:T(8,128)(2,1)} %constant.58.clone.turn, bf16[3,4,256,128]{3,2,1,0:T(8,128)(2,1)} %bitcast.25.own, bf16[3,3,256,128]{3,2,1,0:T(8,128)(2,1)} %copy-done.2, bf16[3,3,256,128]{3,2,1,0:T(8,128)(2,1)} %copy-done.3), custom_call_target="tpu_custom_call" | custom-call | tf_op jit(solution)/shard_map/prepare/pallas_call | solution.py:82
  62.6 16.5 %all-to-all-done.1 = bf16[128,24,128]{2,1,0:T(8,128)(2,1)S(1)} async-done(((bf16[128,24,128]{2,1,0:T(8,128)(2,1)}), bf16[128,24,128]{2,1,0:T(8,128)(2,1)S(1)}, u32[]{:S(2)}, u32[]{:S(2)}) %all-to-all-start.1) | async-done | bytes 786464 | tf_op jit(solution)/shard_map/all_to_all | solution.py:368
  79.1 0.2 fusion.4
  79.3 1.3 collective-permute-start.2
  80.6 5.4 %collective-permute-start.3 = (bf16[3,3,256,128]{3,2,1,0:T(8,128)(2,1)S(1)}, bf16[3,3,256,128]{3,2,1,0:T(8,128)(2,1)}, u32[]{:S(2)}, u32[]{:S(2)}) collective-permute-start(bf16[3,3,256,128]{3,2,1,0:T(8,128)(2,1)S(1)} %get-tuple-element.32), channel_id=1, source_target_pairs={{1,0},{2,1},{3,2},{5,4},{6,5},{7,6},{9,8},{10,9},{11,10},{13,12},{... | collective-permute-start | bytes 1769480 | tf_op jit(solution)/shard_map/ppermute | solution.py:363
  86.0 0.7 copy.28
  86.8 5.8 %all-to-all-start.2 = ((s32[128,1,2]{2,1,0:T(1,128)}), s32[128,1,2]{2,1,0:T(1,128)S(1)}, u32[]{:S(2)}, u32[]{:S(2)}) async-start(s32[128,1,2]{2,1,0:T(1,128)} %copy.28), calls=%async_computation.2 | async-start | bytes 131072 | tf_op jit(solution)/shard_map/all_to_all | solution.py:368
  92.6 5.0 %inner.1.part = f32[3,8,256,128]{3,2,1,0:T(8,128)} custom-call(bf16[128,128]{1,0:T(8,128)(2,1)} %constant.59.clone.across, bf16[256,256]{1,0:T(8,128)(2,1)} %constant.60.clone.along, bf16[3,4,256,128]{3,2,1,0:T(8,128)(2,1)} %get-tuple-element.18.own.a_in, bf16[3,4,256,128]{3,2,1,0:T(8,128)(2,1)} %bitcast.29), custom_call_target="tpu_custom_call" | custom-call | flops 1000000000 | bytes 10000000 | tf_op jit(solution)/shard_map/inner/pallas_call | solution.py:140
  97.5 0.0 collective-permute-done.2.fac_lo
  97.6 0.9 copy-done.7
  98.4 12.8 %correct.1 = (bf16[3,4,256,128]{3,2,1,0:T(8,128)(2,1)}, bf16[1024,768]{1,0:T(8,128)(2,1)}) custom-call(f32[2]{0:T(128)} %add_convert_fusion.flags, bf16[128,128]{1,0:T(8,128)(2,1)} %constant.59.clone.across, bf16[256,256]{1,0:T(8,128)(2,1)} %constant.60.clone.along, bf16[256,256]{1,0:T(8,128)(2,1)} %broadcast_multiply_fusion.smooth_x, ...), custom_call_target="tpu_custom_call" | custom-call | flops 4000000000 | bytes 12000000 | tf_op jit(solution)/shard_map/correct/pallas_call | solution.py:300
  111.2 13.9 %all-to-all-start.3 = ((bf16[128,8,768]{2,1,0:T(8,128)(2,1)}), bf16[128,8,768]{2,1,0:T(8,128)(2,1)S(1)}, u32[]{:S(2)}, u32[]{:S(2)}) async-start(bf16[128,8,768]{2,1,0:T(8,128)(2,1)} %bitcast.31), calls=%async_computation.3 | async-start | bytes 3145728 | tf_op jit(solution)/shard_map/all_to_all | solution.py:368
  125.1 0.1 lt.41
  125.2 0.1 add_select_fusion.1
  125.2 0.1 copy.30
  125.3 0.1 copy.29
  125.4 0.1 add_select_fusion.2
  125.5 0.1 copy.35
  125.6 0.1 fusion.6
  125.7 0.1 stack_reshape.7
  125.8 0.1 stack_reshape.6
  125.9 1.5 copy.34
  127.4 40.2 %all-to-all-done.3 = bf16[128,8,768]{2,1,0:T(8,128)(2,1)S(1)} async-done(((bf16[128,8,768]{2,1,0:T(8,128)(2,1)}), bf16[128,8,768]{2,1,0:T(8,128)(2,1)S(1)}, u32[]{:S(2)}, u32[]{:S(2)}) %all-to-all-start.3) | async-done | bytes 1572896 | tf_op jit(solution)/shard_map/all_to_all | solution.py:368
  167.7 1.1 join.1
  168.8 1.5 copy.39
  (26 shorter events, 0.1 us)
Async XLA Ops:
  2.8 43.1 %all-to-all-start = ((bf16[128,24,128]{2,1,0:T(8,128)(2,1)}), bf16[128,24,128]{2,1,0:T(8,128)(2,1)S(1)}, u32[]{:S(2)}, u32[]{:S(2)}) async-start(bf16[128,24,128]{2,1,0:T(8,128)(2,1)} %bitcast.1), calls=%async_computation | async-start | bytes 1572864 | tf_op jit(solution)/shard_map/all_to_all | solution.py:368
  20.2 7.3 %copy-start.5 = (s32[128]{0:T(128)S(1)}, s32[128]{0:T(128)}, u32[]{:S(2)}) copy-start(s32[128]{0:T(128)} %param.11) | copy-start | bytes 1540
  20.2 7.3 %copy-start.6 = (s32[128,1]{0,1:T(1,128)S(1)}, s32[128,1]{0,1:T(1,128)}, u32[]{:S(2)}) copy-start(s32[128,1]{0,1:T(1,128)} %param.12) | copy-start | bytes 1540
  21.5 35.2 %collective-permute-start = (bf16[3,3,256,128]{3,2,1,0:T(8,128)(2,1)S(1)}, bf16[3,3,256,128]{3,2,1,0:T(8,128)(2,1)S(1)}, u32[]{:S(2)}, u32[]{:S(2)}) collective-permute-start(bf16[3,3,256,128]{3,2,1,0:T(8,128)(2,1)S(1)} %get-tuple-element.35), channel_id=1, source_target_pairs={{0,1},{1,2},{2,3},{4,5},{5,6},{6,7},{8,9},{9,10},{10,11},{12,13},{... | collective-permute-start | bytes 1769480 | tf_op jit(solution)/shard_map/ppermute | solution.py:362
  22.8 34.0 %collective-permute-start.1 = (bf16[3,3,256,128]{3,2,1,0:T(8,128)(2,1)S(1)}, bf16[3,3,256,128]{3,2,1,0:T(8,128)(2,1)S(1)}, u32[]{:S(2)}, u32[]{:S(2)}) collective-permute-start(bf16[3,3,256,128]{3,2,1,0:T(8,128)(2,1)S(1)} %get-tuple-element.34), channel_id=1, source_target_pairs={{1,0},{2,1},{3,2},{5,4},{6,5},{7,6},{9,8},{10,9},{11,10},{13,12},{... | collective-permute-start | bytes 1769480 | tf_op jit(solution)/shard_map/ppermute | solution.py:363
  27.6 26.5 %copy-start.8 = (s32[128]{0:T(128)S(1)}, s32[128]{0:T(128)}, u32[]{:S(2)}) copy-start(s32[128]{0:T(128)} %param.14) | copy-start | bytes 1540
  27.7 26.5 %copy-start.9 = (s32[128]{0:T(128)S(1)}, s32[128]{0:T(128)}, u32[]{:S(2)}) copy-start(s32[128]{0:T(128)} %param.13) | copy-start | bytes 1540
  27.7 28.4 %copy-start.4 = (bf16[256,256]{1,0:T(8,128)(2,1)S(1)}, bf16[256,256]{1,0:T(8,128)(2,1)}, u32[]{:S(2)}) copy-start(bf16[256,256]{1,0:T(8,128)(2,1)} %constant.61.clone) | copy-start | bytes 393220
  47.5 31.6 %all-to-all-start.1 = ((bf16[128,24,128]{2,1,0:T(8,128)(2,1)}), bf16[128,24,128]{2,1,0:T(8,128)(2,1)S(1)}, u32[]{:S(2)}, u32[]{:S(2)}) async-start(bf16[128,24,128]{2,1,0:T(8,128)(2,1)} %gather_fusion), calls=%async_computation.1 | async-start | bytes 1572864 | tf_op jit(solution)/shard_map/all_to_all | solution.py:368
  56.8 0.9 copy-start.2
  57.6 0.8 copy-start.3
  79.1 13.5 %copy-start = (bf16[128,24,128]{2,1,0:T(8,128)(2,1)}, bf16[128,24,128]{2,1,0:T(8,128)(2,1)S(1)}, u32[]{:S(2)}) copy-start(bf16[128,24,128]{2,1,0:T(8,128)(2,1)S(1)} %all-to-all-done.1) | copy-start | bytes 2359300
  79.3 18.3 %collective-permute-start.2 = (bf16[3,3,256,128]{3,2,1,0:T(8,128)(2,1)S(1)}, bf16[3,3,256,128]{3,2,1,0:T(8,128)(2,1)S(1)}, u32[]{:S(2)}, u32[]{:S(2)}) collective-permute-start(bf16[3,3,256,128]{3,2,1,0:T(8,128)(2,1)S(1)} %get-tuple-element.33), channel_id=1, source_target_pairs={{0,1},{1,2},{2,3},{4,5},{5,6},{6,7},{8,9},{9,10},{10,11},{12,13},{... | collective-permute-start | bytes 1769480 | tf_op jit(solution)/shard_map/ppermute | solution.py:362
  80.6 17.0 %collective-permute-start.3 = (bf16[3,3,256,128]{3,2,1,0:T(8,128)(2,1)S(1)}, bf16[3,3,256,128]{3,2,1,0:T(8,128)(2,1)}, u32[]{:S(2)}, u32[]{:S(2)}) collective-permute-start(bf16[3,3,256,128]{3,2,1,0:T(8,128)(2,1)S(1)} %get-tuple-element.32), channel_id=1, source_target_pairs={{1,0},{2,1},{3,2},{5,4},{6,5},{7,6},{9,8},{10,9},{11,10},{13,12},{... | collective-permute-start | bytes 1769480 | tf_op jit(solution)/shard_map/ppermute | solution.py:363
  86.8 24.4 %all-to-all-start.2 = ((s32[128,1,2]{2,1,0:T(1,128)}), s32[128,1,2]{2,1,0:T(1,128)S(1)}, u32[]{:S(2)}, u32[]{:S(2)}) async-start(s32[128,1,2]{2,1,0:T(1,128)} %copy.28), calls=%async_computation.2 | async-start | bytes 131072 | tf_op jit(solution)/shard_map/all_to_all | solution.py:368
  97.5 0.9 copy-start.7
  111.2 14.7 %copy-start.1 = (bf16[3,4,256,128]{3,2,1,0:T(8,128)(2,1)S(1)}, bf16[3,4,256,128]{3,2,1,0:T(8,128)(2,1)}, u32[]{:S(2)}) copy-start(bf16[3,4,256,128]{3,2,1,0:T(8,128)(2,1)} %get-tuple-element.21) | copy-start | bytes 2359300
  111.2 56.5 %all-to-all-start.3 = ((bf16[128,8,768]{2,1,0:T(8,128)(2,1)}), bf16[128,8,768]{2,1,0:T(8,128)(2,1)S(1)}, u32[]{:S(2)}, u32[]{:S(2)}) async-start(bf16[128,8,768]{2,1,0:T(8,128)(2,1)} %bitcast.31), calls=%async_computation.3 | async-start | bytes 3145728 | tf_op jit(solution)/shard_map/all_to_all | solution.py:368

commit v6 on v3

--- a/solution.py
+++ b/solution.py
@@ -59,44 +59,30 @@
     return own_hi, k - HALO - depth
 
 
-def prepare_kernel(turn, across, along, own, own_lo, own_hi, a10, dxa, dya):
-    depth, _, cols = own.shape[1:]
+def prepare_kernel(turn, own, own_lo, own_hi, a10):
+    depth = own.shape[1]
     for k in range(depth + 2 * HALO):
         ref, at = plane_of(own, own_lo, own_hi, k)
-        a = dot(ref[0, at], turn[...]).astype(BF16)
-        a10[0, k] = a
-        if 0 < k < depth + 2 * HALO - 1:
-            dxa[0, k - 1] = dot(a, across[...])
-            if k % 2 == 0:
-                dy = dot(along[...], jnp.concatenate([before, a], axis=1))
-                dya[0, k - 2] = dy[:, :cols]
-                dya[0, k - 1] = dy[:, cols:]
-        before = a
-
-
-def prepare(turn, across, along, own, own_lo, own_hi):
+        a10[0, k] = dot(ref[0, at], turn[...]).astype(BF16)
+
+
+def prepare(turn, own, own_lo, own_hi):
     chans, depth, rows, cols = own.shape
     wide = depth + 2 * HALO
 
     def spec(n):
         return pl.BlockSpec((1, n, rows, cols), lambda c: (c, 0, 0, 0))
-
-    def whole(m):
-        return pl.BlockSpec(m.shape, lambda c: (0, 0))
-
-    def shape(n, dtype):
-        return jax.ShapeDtypeStruct((chans, n, rows, cols), dtype)
 
     return pl.pallas_call(
         prepare_kernel,
         grid=(chans,),
-        in_specs=[whole(turn), whole(across), whole(along)]
+        in_specs=[pl.BlockSpec(turn.shape, lambda c: (0, 0))]
         + [spec(depth), spec(HALO), spec(HALO)],
-        out_specs=[spec(wide), spec(wide - 2), spec(wide - 2)],
-        out_shape=[shape(wide, BF16), shape(wide - 2, F32), shape(wide - 2, F32)],
+        out_specs=spec(wide),
+        out_shape=jax.ShapeDtypeStruct((chans, wide, rows, cols), BF16),
         compiler_params=pltpu.CompilerParams(vmem_limit_bytes=60 << 20),
         name="prepare",
-    )(turn, across, along, own, own_lo, own_hi)
+    )(turn, own, own_lo, own_hi)
 
 
 def pack(code, planes, out, held, sems):
@@ -126,15 +112,15 @@
     smooth_y,
     code,
     a10,
-    dxa,
-    dya,
     own,
     fac,
     fac_lo,
     fac_hi,
     out,
     sent,
+    dxa,
     dxb,
+    dya,
     dyb,
     deep,
     kept,
@@ -148,13 +134,12 @@
     half = jnp.float32(0.5)
     for k in range(1, wide - 1):
         ref, at = plane_of(fac, fac_lo, fac_hi, k)
-        now = ref[0, at]
-        dxb[k - 1] = dot(now, across[...])
-        if k % 2 == 0:
-            dy = dot(along[...], jnp.concatenate([before, now], axis=1))
-            dyb[k - 2] = dy[:, :cols]
-            dyb[k - 1] = dy[:, cols:]
-        before = now
+        a, f = a10[0, k], ref[0, at]
+        dxa[k - 1] = dot(a, across[...])
+        dxb[k - 1] = dot(f, across[...])
+        dy = dot(along[...], jnp.concatenate([a, f], axis=1))
+        dya[k - 1] = dy[:, :cols]
+        dyb[k - 1] = dy[:, cols:]
 
     step = 32
 
@@ -177,8 +162,8 @@
             b_last, bv, b_next = bv, b_next, b_of(k + 1)
             dza = (a_next - a_last) * half
             dzb = (b_next - b_last) * half
-            ya, yb = dya[0, k - 1, at_rows, :], dyb[k - 1, at_rows, :]
-            xa, xb = dxa[0, k - 1, at_rows, :], dxb[k - 1, at_rows, :]
+            ya, yb = dya[k - 1, at_rows, :], dyb[k - 1, at_rows, :]
+            xa, xb = dxa[k - 1, at_rows, :], dxb[k - 1, at_rows, :]
             p1 = av * bv + ya * yb + dza * dzb + xa * xb
             p2 = bv * bv + yb * yb + dzb * dzb + xb * xb
             if k < HALO:
@@ -220,7 +205,7 @@
 
 
 def correct(
-    flags, across, along, smooth_x, smooth_y, code, a10, dxa, dya, own, fac, fac_lo, fac_hi, blocks
+    flags, across, along, smooth_x, smooth_y, code, a10, own, fac, fac_lo, fac_hi, blocks
 ):
     chans, depth, rows, cols = own.shape
     wide = depth + 2 * HALO
@@ -238,7 +223,7 @@
         grid=(chans,),
         in_specs=[pl.BlockSpec(memory_space=pltpu.SMEM)]
         + [whole(m) for m in (across, along, smooth_x, smooth_y, code)]
-        + [spec(wide), spec(wide - 2), spec(wide - 2)]
+        + [spec(wide)]
         + [spec(depth), spec(depth), spec(HALO), spec(HALO)],
         out_specs=[spec(depth), pl.BlockSpec(memory_space=pltpu.HBM)],
         out_shape=[
@@ -246,6 +231,8 @@
             jax.ShapeDtypeStruct(packed, BF16),
         ],
         scratch_shapes=[
+            inner,
+            inner,
             inner,
             inner,
             pltpu.VMEM((2 * depth, rows, 2 * cols), BF16),
@@ -258,7 +245,7 @@
             flops=4000000000, bytes_accessed=12000000, transcendentals=0
         ),
         name="correct",
-    )(flags, across, along, smooth_x, smooth_y, code, a10, dxa, dya, own, fac, fac_lo, fac_hi)
+    )(flags, across, along, smooth_x, smooth_y, code, a10, own, fac, fac_lo, fac_hi)
 
 
 def join_kernel(code, got, out):
@@ -337,15 +324,15 @@
     )
     smooth_x = smooth_x * (partner[tile] != tile).astype(BF16)
     flags = jnp.stack([plane_idx > 0, plane_idx < nplane - 1]).astype(F32)
-    a10, dxa, dya = prepare(turn, across, along, own, own_lo, own_hi)
-    fac, labels, code, a10, dxa, dya, smooth_x, flags = lax.optimization_barrier(
-        (fac, labels, code, a10, dxa, dya, smooth_x, flags)
+    a10 = prepare(turn, own, own_lo, own_hi)
+    fac, labels, code, a10, smooth_x, flags = lax.optimization_barrier(
+        (fac, labels, code, a10, smooth_x, flags)
     )
     fac_lo, fac_hi = halo(fac)
     info = swap(labels)
 
     corrected, outgoing = correct(
-        flags, across, along, smooth_x, smooth_y, code, a10, dxa, dya, own, fac, fac_lo, fac_hi, ntile
+        flags, across, along, smooth_x, smooth_y, code, a10, own, fac, fac_lo, fac_hi, ntile
     )
     received = swap(outgoing.reshape(ntile, 8, outgoing.shape[1]))
 

time: 167 us -> 167 us (level)
  waiting for transfers between devices: 76.8 us -> 79.5 us
  Pallas kernels: 21.9 us -> 19.2 us
    all_to_all x4, waiting for transfers between devices: 72.2 us -> 74.9 us  [swap(): lax.all_to_all(blocks, 'tile', split_axis=0, concat_axis=0, tiled=True)]
    pallas_call x1, Pallas kernels: 6.77 us -> 4.16 us  [prepare(): pl.pallas_call(prepare_kernel, grid=(chans,), in_specs=[pl.BlockSpec(turn...]
  transfers between devices with their start and end apart: 8 -> 8, of which waited for: 5 -> 5; matrix products, arithmetic and copies ran while one was open for 5% -> 5% of each run, Pallas kernels for 12% -> 11%
where the time goes in v6:
time: 167 us; the launch traced here: 166 us
  waiting for transfers between devices  79.5 us (48%)
  starting transfers between devices  51.6 us (31%)
  Pallas kernels  19.2 us (11%)
  local copies, waits for them, and re-layouts  12 us (7%)
  other arithmetic  2.49 us (1%)
    all_to_all x4, waiting for transfers between devices, swap(): lax.all_to_all(blocks, 'tile', split_axis=0, concat_axis=0, tiled=True)  74.9 us
    all_to_all x4, starting transfers between devices, swap(): lax.all_to_all(blocks, 'tile', split_axis=0, concat_axis=0, tiled=True)  39 us
    pallas_call x1, Pallas kernels, correct(): pl.pallas_call(correct_kernel, grid=(chans,), in_specs=[pl.BlockSpec(memo...  13.9 us
    ppermute x2, starting transfers between devices, halo(): high = lax.ppermute(block[:, :HALO], 'gz', backward)  9.97 us
    unnamed x23, local copies, waits for them, and re-layouts  5.45 us
    pallas_call x1, Pallas kernels, prepare(): pl.pallas_call(prepare_kernel, grid=(chans,), in_specs=[pl.BlockSpec(turn...  4.16 us
    ppermute x2, waiting for transfers between devices, halo(): low = lax.ppermute(block[:, depth - HALO:], 'gz', forward)  3.47 us
  transfers between devices with their start and end apart: 8, of which 5 were waited for; matrix products, arithmetic and copies ran while one was open for 5% of the time, Pallas kernels for 11%

profile of v6, /device:TPU:14, one launch (start us, length us, event | category | flops | bytes accessed | tf_op | source)
XLA Modules:
  0.0 166.4 jit_solution(8512590327259462427)
XLA Ops:
  0.6 2.1 %copy.40 = bf16[256,3,4,128]{3,0,2,1:T(8,128)(2,1)} copy(bf16[256,3,4,128]{3,2,1,0:T(4,128)(2,1)} %param.10) | data formatting | bytes 1572864 | tf_op args[0]
  2.8 17.4 %all-to-all-start = ((bf16[128,24,128]{2,1,0:T(8,128)(2,1)}), bf16[128,24,128]{2,1,0:T(8,128)(2,1)S(1)}, u32[]{:S(2)}, u32[]{:S(2)}) async-start(bf16[128,24,128]{2,1,0:T(8,128)(2,1)} %bitcast.1), calls=%async_computation | async-start | bytes 1572864 | tf_op jit(solution)/shard_map/all_to_all | solution.py:289
  20.2 0.0 copy-start.5
  20.2 0.0 copy-start.6
  20.2 1.3 fusion.5
  21.5 1.3 collective-permute-start
  22.8 4.6 %collective-permute-start.1 = (bf16[3,3,256,128]{3,2,1,0:T(8,128)(2,1)S(1)}, bf16[3,3,256,128]{3,2,1,0:T(8,128)(2,1)S(1)}, u32[]{:S(2)}, u32[]{:S(2)}) collective-permute-start(bf16[3,3,256,128]{3,2,1,0:T(8,128)(2,1)S(1)} %get-tuple-element.28), channel_id=1, source_target_pairs={{1,0},{2,1},{3,2},{5,4},{6,5},{7,6},{9,8},{10,9},{11,10},{13,12},{... | collective-permute-start | bytes 1769480 | tf_op jit(solution)/shard_map/ppermute | solution.py:284
  27.4 0.2 convert_reduce_fusion
  27.6 0.0 copy-start.8
  27.6 0.0 copy-start.9
  27.6 0.0 copy-start.4
  27.7 18.3 %all-to-all-done = bf16[128,24,128]{2,1,0:T(8,128)(2,1)S(1)} async-done(((bf16[128,24,128]{2,1,0:T(8,128)(2,1)}), bf16[128,24,128]{2,1,0:T(8,128)(2,1)S(1)}, u32[]{:S(2)}, u32[]{:S(2)}) %all-to-all-start) | async-done | bytes 786464 | tf_op jit(solution)/shard_map/all_to_all | solution.py:289
  45.9 1.6 gather_fusion
  47.5 5.8 %all-to-all-start.1 = ((bf16[128,24,128]{2,1,0:T(8,128)(2,1)}), bf16[128,24,128]{2,1,0:T(8,128)(2,1)S(1)}, u32[]{:S(2)}, u32[]{:S(2)}) async-start(bf16[128,24,128]{2,1,0:T(8,128)(2,1)} %gather_fusion), calls=%async_computation.1 | async-start | bytes 1572864 | tf_op jit(solution)/shard_map/all_to_all | solution.py:289
  53.3 0.1 iota_add_fusion
  53.4 0.1 add.93
  53.6 0.6 pad_add_fusion.1.code
  54.2 0.7 add_convert_fusion.flags
  54.9 0.6 dynamic_slice.3
  56.1 0.1 select_reduce_fusion
  56.2 0.7 broadcast_multiply_fusion.smooth_x
  56.9 0.0 collective-permute-done.own_lo
  56.9 0.8 copy-done.2
  57.7 0.8 copy-done.3
  58.6 4.2 %prepare.1.a10 = bf16[3,10,256,128]{3,2,1,0:T(8,128)(2,1)} custom-call(bf16[128,128]{1,0:T(8,128)(2,1)} %constant.58.clone.turn, bf16[3,4,256,128]{3,2,1,0:T(8,128)(2,1)} %bitcast.25.own, bf16[3,3,256,128]{3,2,1,0:T(8,128)(2,1)} %copy-done.2, bf16[3,3,256,128]{3,2,1,0:T(8,128)(2,1)} %copy-done.3), custom_call_target="tpu_custom_call" | custom-call | tf_op jit(solution)/shard_map/prepare/pallas_call | solution.py:76
  62.7 16.3 %all-to-all-done.1 = bf16[128,24,128]{2,1,0:T(8,128)(2,1)S(1)} async-done(((bf16[128,24,128]{2,1,0:T(8,128)(2,1)}), bf16[128,24,128]{2,1,0:T(8,128)(2,1)S(1)}, u32[]{:S(2)}, u32[]{:S(2)}) %all-to-all-start.1) | async-done | bytes 786464 | tf_op jit(solution)/shard_map/all_to_all | solution.py:289
  79.1 0.2 fusion.4
  79.3 1.3 collective-permute-start.2
  80.6 5.4 %collective-permute-start.3 = (bf16[3,3,256,128]{3,2,1,0:T(8,128)(2,1)S(1)}, bf16[3,3,256,128]{3,2,1,0:T(8,128)(2,1)}, u32[]{:S(2)}, u32[]{:S(2)}) collective-permute-start(bf16[3,3,256,128]{3,2,1,0:T(8,128)(2,1)S(1)} %get-tuple-element.26), channel_id=1, source_target_pairs={{1,0},{2,1},{3,2},{5,4},{6,5},{7,6},{9,8},{10,9},{11,10},{13,12},{... | collective-permute-start | bytes 1769480 | tf_op jit(solution)/shard_map/ppermute | solution.py:284
  86.0 0.7 copy.28
  86.7 5.8 %all-to-all-start.2 = ((s32[128,1,2]{2,1,0:T(1,128)}), s32[128,1,2]{2,1,0:T(1,128)S(1)}, u32[]{:S(2)}, u32[]{:S(2)}) async-start(s32[128,1,2]{2,1,0:T(1,128)} %copy.28), calls=%async_computation.2 | async-start | bytes 131072 | tf_op jit(solution)/shard_map/all_to_all | solution.py:289
  92.5 3.5 %collective-permute-done.2.fac_lo = bf16[3,3,256,128]{3,2,1,0:T(8,128)(2,1)S(1)} collective-permute-done((bf16[3,3,256,128]{3,2,1,0:T(8,128)(2,1)S(1)}, bf16[3,3,256,128]{3,2,1,0:T(8,128)(2,1)S(1)}, u32[]{:S(2)}, u32[]{:S(2)}) %collective-permute-start.2) | collective-permute-done | bytes 589856 | tf_op jit(solution)/shard_map/ppermute | solution.py:283
  96.0 1.2 collective-permute-done.3.fac_hi
  97.2 13.9 %correct.1 = (bf16[3,4,256,128]{3,2,1,0:T(8,128)(2,1)}, bf16[1024,768]{1,0:T(8,128)(2,1)}) custom-call(f32[2]{0:T(128)} %add_convert_fusion.flags, bf16[128,128]{1,0:T(8,128)(2,1)} %constant.59.clone.across, bf16[256,256]{1,0:T(8,128)(2,1)} %constant.60.clone.along, bf16[256,256]{1,0:T(8,128)(2,1)} %broadcast_multiply_fusion.smooth_x, ...), custom_call_target="tpu_custom_call" | custom-call | flops 4000000000 | bytes 12000000 | tf_op jit(solution)/shard_map/correct/pallas_call | solution.py:221
  111.1 10.0 %all-to-all-start.3 = ((bf16[128,8,768]{2,1,0:T(8,128)(2,1)}), bf16[128,8,768]{2,1,0:T(8,128)(2,1)S(1)}, u32[]{:S(2)}, u32[]{:S(2)}) async-start(bf16[128,8,768]{2,1,0:T(8,128)(2,1)} %bitcast.30), calls=%async_computation.3 | async-start | bytes 3145728 | tf_op jit(solution)/shard_map/all_to_all | solution.py:289
  121.2 0.1 lt.41
  121.3 0.1 add_select_fusion.1
  121.3 0.1 copy.30
  121.4 0.1 copy.29
  121.5 0.1 add_select_fusion.2
  121.6 0.1 copy.35
  121.7 0.1 fusion.6
  121.8 0.1 stack_reshape.7
  121.9 0.1 stack_reshape.6
  122.0 1.5 copy.34
  123.5 40.2 %all-to-all-done.3 = bf16[128,8,768]{2,1,0:T(8,128)(2,1)S(1)} async-done(((bf16[128,8,768]{2,1,0:T(8,128)(2,1)}), bf16[128,8,768]{2,1,0:T(8,128)(2,1)S(1)}, u32[]{:S(2)}, u32[]{:S(2)}) %all-to-all-start.3) | async-done | bytes 1572896 | tf_op jit(solution)/shard_map/all_to_all | solution.py:289
  163.8 1.1 join.1
  164.9 1.5 copy.39
  (25 shorter events, 0.1 us)
Async XLA Ops:
  2.8 43.1 %all-to-all-start = ((bf16[128,24,128]{2,1,0:T(8,128)(2,1)}), bf16[128,24,128]{2,1,0:T(8,128)(2,1)S(1)}, u32[]{:S(2)}, u32[]{:S(2)}) async-start(bf16[128,24,128]{2,1,0:T(8,128)(2,1)} %bitcast.1), calls=%async_computation | async-start | bytes 1572864 | tf_op jit(solution)/shard_map/all_to_all | solution.py:289
  20.2 7.2 %copy-start.5 = (s32[128]{0:T(128)S(1)}, s32[128]{0:T(128)}, u32[]{:S(2)}) copy-start(s32[128]{0:T(128)} %param.11) | copy-start | bytes 1540
  20.2 7.3 %copy-start.6 = (s32[128,1]{0,1:T(1,128)S(1)}, s32[128,1]{0,1:T(1,128)}, u32[]{:S(2)}) copy-start(s32[128,1]{0,1:T(1,128)} %param.12) | copy-start | bytes 1540
  21.5 35.4 %collective-permute-start = (bf16[3,3,256,128]{3,2,1,0:T(8,128)(2,1)S(1)}, bf16[3,3,256,128]{3,2,1,0:T(8,128)(2,1)S(1)}, u32[]{:S(2)}, u32[]{:S(2)}) collective-permute-start(bf16[3,3,256,128]{3,2,1,0:T(8,128)(2,1)S(1)} %get-tuple-element.29), channel_id=1, source_target_pairs={{0,1},{1,2},{2,3},{4,5},{5,6},{6,7},{8,9},{9,10},{10,11},{12,13},{... | collective-permute-start | bytes 1769480 | tf_op jit(solution)/shard_map/ppermute | solution.py:283
  22.8 34.1 %collective-permute-start.1 = (bf16[3,3,256,128]{3,2,1,0:T(8,128)(2,1)S(1)}, bf16[3,3,256,128]{3,2,1,0:T(8,128)(2,1)S(1)}, u32[]{:S(2)}, u32[]{:S(2)}) collective-permute-start(bf16[3,3,256,128]{3,2,1,0:T(8,128)(2,1)S(1)} %get-tuple-element.28), channel_id=1, source_target_pairs={{1,0},{2,1},{3,2},{5,4},{6,5},{7,6},{9,8},{10,9},{11,10},{13,12},{... | collective-permute-start | bytes 1769480 | tf_op jit(solution)/shard_map/ppermute | solution.py:284
  27.6 26.5 %copy-start.8 = (s32[128]{0:T(128)S(1)}, s32[128]{0:T(128)}, u32[]{:S(2)}) copy-start(s32[128]{0:T(128)} %param.14) | copy-start | bytes 1540
  27.6 26.5 %copy-start.9 = (s32[128]{0:T(128)S(1)}, s32[128]{0:T(128)}, u32[]{:S(2)}) copy-start(s32[128]{0:T(128)} %param.13) | copy-start | bytes 1540
  27.6 28.6 %copy-start.4 = (bf16[256,256]{1,0:T(8,128)(2,1)S(1)}, bf16[256,256]{1,0:T(8,128)(2,1)}, u32[]{:S(2)}) copy-start(bf16[256,256]{1,0:T(8,128)(2,1)} %constant.61.clone) | copy-start | bytes 393220
  47.5 31.6 %all-to-all-start.1 = ((bf16[128,24,128]{2,1,0:T(8,128)(2,1)}), bf16[128,24,128]{2,1,0:T(8,128)(2,1)S(1)}, u32[]{:S(2)}, u32[]{:S(2)}) async-start(bf16[128,24,128]{2,1,0:T(8,128)(2,1)} %gather_fusion), calls=%async_computation.1 | async-start | bytes 1572864 | tf_op jit(solution)/shard_map/all_to_all | solution.py:289
  56.9 0.8 copy-start.2
  57.7 0.8 copy-start.3
  79.1 18.1 %copy-start = (bf16[128,24,128]{2,1,0:T(8,128)(2,1)}, bf16[128,24,128]{2,1,0:T(8,128)(2,1)S(1)}, u32[]{:S(2)}) copy-start(bf16[128,24,128]{2,1,0:T(8,128)(2,1)S(1)} %all-to-all-done.1) | copy-start | bytes 2359300
  79.3 16.7 %collective-permute-start.2 = (bf16[3,3,256,128]{3,2,1,0:T(8,128)(2,1)S(1)}, bf16[3,3,256,128]{3,2,1,0:T(8,128)(2,1)S(1)}, u32[]{:S(2)}, u32[]{:S(2)}) collective-permute-start(bf16[3,3,256,128]{3,2,1,0:T(8,128)(2,1)S(1)} %get-tuple-element.27), channel_id=1, source_target_pairs={{0,1},{1,2},{2,3},{4,5},{5,6},{6,7},{8,9},{9,10},{10,11},{12,13},{... | collective-permute-start | bytes 1769480 | tf_op jit(solution)/shard_map/ppermute | solution.py:283
  80.6 16.6 %collective-permute-start.3 = (bf16[3,3,256,128]{3,2,1,0:T(8,128)(2,1)S(1)}, bf16[3,3,256,128]{3,2,1,0:T(8,128)(2,1)}, u32[]{:S(2)}, u32[]{:S(2)}) collective-permute-start(bf16[3,3,256,128]{3,2,1,0:T(8,128)(2,1)S(1)} %get-tuple-element.26), channel_id=1, source_target_pairs={{1,0},{2,1},{3,2},{5,4},{6,5},{7,6},{9,8},{10,9},{11,10},{13,12},{... | collective-permute-start | bytes 1769480 | tf_op jit(solution)/shard_map/ppermute | solution.py:284
  86.7 24.4 %all-to-all-start.2 = ((s32[128,1,2]{2,1,0:T(1,128)}), s32[128,1,2]{2,1,0:T(1,128)S(1)}, u32[]{:S(2)}, u32[]{:S(2)}) async-start(s32[128,1,2]{2,1,0:T(1,128)} %copy.28), calls=%async_computation.2 | async-start | bytes 131072 | tf_op jit(solution)/shard_map/all_to_all | solution.py:289
  96.0 1.2 copy-start.7
  111.1 10.9 %copy-start.1 = (bf16[3,4,256,128]{3,2,1,0:T(8,128)(2,1)S(1)}, bf16[3,4,256,128]{3,2,1,0:T(8,128)(2,1)}, u32[]{:S(2)}) copy-start(bf16[3,4,256,128]{3,2,1,0:T(8,128)(2,1)} %get-tuple-element.15) | copy-start | bytes 2359300
  111.1 52.6 %all-to-all-start.3 = ((bf16[128,8,768]{2,1,0:T(8,128)(2,1)}), bf16[128,8,768]{2,1,0:T(8,128)(2,1)S(1)}, u32[]{:S(2)}, u32[]{:S(2)}) async-start(bf16[128,8,768]{2,1,0:T(8,128)(2,1)} %bitcast.30), calls=%async_computation.3 | async-start | bytes 3145728 | tf_op jit(solution)/shard_map/all_to_all | solution.py:289

commit v7 on v3

--- a/solution.py
+++ b/solution.py
@@ -156,7 +156,7 @@
             dyb[k - 1] = dy[:, cols:]
         before = now
 
-    step = 32
+    step = 16
 
     def chunk(r, carry):
         at_rows = pl.ds(pl.multiple_of(r * step, step), step)

time: 167 us -> 167 us (level)
  transfers between devices with their start and end apart: 8 -> 8, of which waited for: 5 -> 5; matrix products, arithmetic and copies ran while one was open for 5% -> 5% of each run, Pallas kernels for 12% -> 13%
where the time goes in v7:
time: 167 us
  waiting for transfers between devices  76.8 us (46%)
  starting transfers between devices  51.8 us (31%)
  Pallas kernels  21.9 us (13%)
  local copies, waits for them, and re-layouts  12.1 us (7%)
  other arithmetic  2.41 us (1%)
    all_to_all x4, waiting for transfers between devices, swap(): lax.all_to_all(blocks, 'tile', split_axis=0, concat_axis=0, tiled=True)  72.2 us
    all_to_all x4, starting transfers between devices, swap(): lax.all_to_all(blocks, 'tile', split_axis=0, concat_axis=0, tiled=True)  39.1 us
    pallas_call x1, Pallas kernels, correct(): pl.pallas_call(correct_kernel, grid=(chans,), in_specs=[pl.BlockSpec(memo...  14.1 us
    ppermute x2, starting transfers between devices, halo(): high = lax.ppermute(block[:, :HALO], 'gz', backward)  9.97 us
    pallas_call x1, Pallas kernels, prepare(): pl.pallas_call(prepare_kernel, grid=(chans,), in_specs=[whole(turn), whol...  6.77 us
    unnamed x23, local copies, waits for them, and re-layouts  5.49 us
    ppermute x2, waiting for transfers between devices, halo(): low = lax.ppermute(block[:, depth - HALO:], 'gz', forward)  3.46 us
  transfers between devices with their start and end apart: 8, of which 5 were waited for; matrix products, arithmetic and copies ran while one was open for 5% of the time, Pallas kernels for 13%

profile of v7, /device:TPU:14, one launch (start us, length us, event | category | flops | bytes accessed | tf_op | source)
XLA Modules:
  0.0 166.6 jit_solution(2894721656113443331)
XLA Ops:
  0.6 2.1 %copy.40 = bf16[256,3,4,128]{3,0,2,1:T(8,128)(2,1)} copy(bf16[256,3,4,128]{3,2,1,0:T(4,128)(2,1)} %param.10) | data formatting | bytes 1572864 | tf_op args[0]
  2.8 17.5 %all-to-all-start = ((bf16[128,24,128]{2,1,0:T(8,128)(2,1)}), bf16[128,24,128]{2,1,0:T(8,128)(2,1)S(1)}, u32[]{:S(2)}, u32[]{:S(2)}) async-start(bf16[128,24,128]{2,1,0:T(8,128)(2,1)} %bitcast.1), calls=%async_computation | async-start | bytes 1572864 | tf_op jit(solution)/shard_map/all_to_all | solution.py:302
  20.3 1.3 fusion.5
  21.6 0.0 copy-start.8
  21.6 0.0 copy-start.9
  21.6 0.0 copy-start.4
  21.7 1.4 collective-permute-start
  23.1 4.6 %collective-permute-start.1 = (bf16[3,3,256,128]{3,2,1,0:T(8,128)(2,1)S(1)}, bf16[3,3,256,128]{3,2,1,0:T(8,128)(2,1)S(1)}, u32[]{:S(2)}, u32[]{:S(2)}) collective-permute-start(bf16[3,3,256,128]{3,2,1,0:T(8,128)(2,1)S(1)} %get-tuple-element.38), channel_id=1, source_target_pairs={{1,0},{2,1},{3,2},{5,4},{6,5},{7,6},{9,8},{10,9},{11,10},{13,12},{... | collective-permute-start | bytes 1769480 | tf_op jit(solution)/shard_map/ppermute | solution.py:297
  27.7 0.2 convert_reduce_fusion
  27.9 18.1 %all-to-all-done = bf16[128,24,128]{2,1,0:T(8,128)(2,1)S(1)} async-done(((bf16[128,24,128]{2,1,0:T(8,128)(2,1)}), bf16[128,24,128]{2,1,0:T(8,128)(2,1)S(1)}, u32[]{:S(2)}, u32[]{:S(2)}) %all-to-all-start) | async-done | bytes 786464 | tf_op jit(solution)/shard_map/all_to_all | solution.py:302
  46.0 1.6 gather_fusion
  47.6 5.8 %all-to-all-start.1 = ((bf16[128,24,128]{2,1,0:T(8,128)(2,1)}), bf16[128,24,128]{2,1,0:T(8,128)(2,1)S(1)}, u32[]{:S(2)}, u32[]{:S(2)}) async-start(bf16[128,24,128]{2,1,0:T(8,128)(2,1)} %gather_fusion), calls=%async_computation.1 | async-start | bytes 1572864 | tf_op jit(solution)/shard_map/all_to_all | solution.py:302
  53.4 0.1 iota_add_fusion
  53.5 0.1 add.93
  53.7 0.5 pad_add_fusion.1.code
  54.3 0.7 add_convert_fusion.flags
  54.9 0.6 dynamic_slice.3
  56.2 0.1 select_reduce_fusion
  56.3 0.7 broadcast_multiply_fusion.smooth_x
  57.0 0.0 collective-permute-done.own_lo
  57.0 0.0 collective-permute-done.1.own_hi
  57.0 0.8 copy-done.2
  57.8 0.8 copy-done.3
  58.7 6.8 %prepare.1 = (bf16[3,10,256,128]{3,2,1,0:T(8,128)(2,1)}, f32[3,8,256,128]{3,2,1,0:T(8,128)}, f32[3,8,256,128]{3,2,1,0:T(8,128)}) custom-call(bf16[128,128]{1,0:T(8,128)(2,1)} %constant.58.clone.turn, bf16[128,128]{1,0:T(8,128)(2,1)} %constant.59.clone.across, bf16[256,256]{1,0:T(8,128)(2,1)} %constant.60.clone.along, bf16[3,4,256,128]{3,2,1,0:T(8,128)(2,1)} %bitcast.25.own, ...), custom_call_target="tpu_custom_call" | custom-call | tf_op jit(solution)/shard_map/prepare/pallas_call | solution.py:90
  65.4 13.8 %all-to-all-done.1 = bf16[128,24,128]{2,1,0:T(8,128)(2,1)S(1)} async-done(((bf16[128,24,128]{2,1,0:T(8,128)(2,1)}), bf16[128,24,128]{2,1,0:T(8,128)(2,1)S(1)}, u32[]{:S(2)}, u32[]{:S(2)}) %all-to-all-start.1) | async-done | bytes 786464 | tf_op jit(solution)/shard_map/all_to_all | solution.py:302
  79.2 0.2 fusion.4
  79.4 1.3 collective-permute-start.2
  80.7 5.4 %collective-permute-start.3 = (bf16[3,3,256,128]{3,2,1,0:T(8,128)(2,1)S(1)}, bf16[3,3,256,128]{3,2,1,0:T(8,128)(2,1)}, u32[]{:S(2)}, u32[]{:S(2)}) collective-permute-start(bf16[3,3,256,128]{3,2,1,0:T(8,128)(2,1)S(1)} %get-tuple-element.36), channel_id=1, source_target_pairs={{1,0},{2,1},{3,2},{5,4},{6,5},{7,6},{9,8},{10,9},{11,10},{13,12},{... | collective-permute-start | bytes 1769480 | tf_op jit(solution)/shard_map/ppermute | solution.py:297
  86.1 0.7 copy.28
  86.8 5.8 %all-to-all-start.2 = ((s32[128,1,2]{2,1,0:T(1,128)}), s32[128,1,2]{2,1,0:T(1,128)S(1)}, u32[]{:S(2)}, u32[]{:S(2)}) async-start(s32[128,1,2]{2,1,0:T(1,128)} %copy.28), calls=%async_computation.2 | async-start | bytes 131072 | tf_op jit(solution)/shard_map/all_to_all | solution.py:302
  92.7 3.5 %collective-permute-done.2.fac_lo = bf16[3,3,256,128]{3,2,1,0:T(8,128)(2,1)S(1)} collective-permute-done((bf16[3,3,256,128]{3,2,1,0:T(8,128)(2,1)S(1)}, bf16[3,3,256,128]{3,2,1,0:T(8,128)(2,1)S(1)}, u32[]{:S(2)}, u32[]{:S(2)}) %collective-permute-start.2) | collective-permute-done | bytes 589856 | tf_op jit(solution)/shard_map/ppermute | solution.py:296
  96.1 1.2 collective-permute-done.3.fac_hi
  97.3 14.1 %correct.1 = (bf16[3,4,256,128]{3,2,1,0:T(8,128)(2,1)}, bf16[1024,768]{1,0:T(8,128)(2,1)}) custom-call(f32[2]{0:T(128)} %add_convert_fusion.flags, bf16[128,128]{1,0:T(8,128)(2,1)} %constant.59.clone.across, bf16[256,256]{1,0:T(8,128)(2,1)} %constant.60.clone.along, bf16[256,256]{1,0:T(8,128)(2,1)} %broadcast_multiply_fusion.smooth_x, ...), custom_call_target="tpu_custom_call" | custom-call | flops 4000000000 | bytes 12000000 | tf_op jit(solution)/shard_map/correct/pallas_call | solution.py:236
  111.4 0.0 all-to-all-done.2
  111.4 10.0 %all-to-all-start.3 = ((bf16[128,8,768]{2,1,0:T(8,128)(2,1)}), bf16[128,8,768]{2,1,0:T(8,128)(2,1)S(1)}, u32[]{:S(2)}, u32[]{:S(2)}) async-start(bf16[128,8,768]{2,1,0:T(8,128)(2,1)} %bitcast.30), calls=%async_computation.3 | async-start | bytes 3145728 | tf_op jit(solution)/shard_map/all_to_all | solution.py:302
  121.4 0.1 lt.41
  121.5 0.1 add_select_fusion.1
  121.6 0.1 copy.30
  121.6 0.1 copy.29
  121.7 0.1 add_select_fusion.2
  121.8 0.1 copy.35
  121.9 0.1 fusion.6
  122.0 0.1 stack_reshape.7
  122.1 0.1 stack_reshape.6
  122.3 1.5 copy.34
  123.8 40.2 %all-to-all-done.3 = bf16[128,8,768]{2,1,0:T(8,128)(2,1)S(1)} async-done(((bf16[128,8,768]{2,1,0:T(8,128)(2,1)}), bf16[128,8,768]{2,1,0:T(8,128)(2,1)S(1)}, u32[]{:S(2)}, u32[]{:S(2)}) %all-to-all-start.3) | async-done | bytes 1572896 | tf_op jit(solution)/shard_map/all_to_all | solution.py:302
  164.0 1.1 join.1
  165.1 1.5 copy.39
  (25 shorter events, 0.1 us)
Async XLA Ops:
  2.8 24.9 %copy-start.5 = (s32[128]{0:T(128)S(1)}, s32[128]{0:T(128)}, u32[]{:S(2)}) copy-start(s32[128]{0:T(128)} %param.11) | copy-start | bytes 1540
  2.8 24.9 %copy-start.6 = (s32[128,1]{0,1:T(1,128)S(1)}, s32[128,1]{0,1:T(1,128)}, u32[]{:S(2)}) copy-start(s32[128,1]{0,1:T(1,128)} %param.12) | copy-start | bytes 1540
  2.8 43.3 %all-to-all-start = ((bf16[128,24,128]{2,1,0:T(8,128)(2,1)}), bf16[128,24,128]{2,1,0:T(8,128)(2,1)S(1)}, u32[]{:S(2)}, u32[]{:S(2)}) async-start(bf16[128,24,128]{2,1,0:T(8,128)(2,1)} %bitcast.1), calls=%async_computation | async-start | bytes 1572864 | tf_op jit(solution)/shard_map/all_to_all | solution.py:302
  21.6 32.6 %copy-start.8 = (s32[128]{0:T(128)S(1)}, s32[128]{0:T(128)}, u32[]{:S(2)}) copy-start(s32[128]{0:T(128)} %param.14) | copy-start | bytes 1540
  21.6 32.6 %copy-start.9 = (s32[128]{0:T(128)S(1)}, s32[128]{0:T(128)}, u32[]{:S(2)}) copy-start(s32[128]{0:T(128)} %param.13) | copy-start | bytes 1540
  21.6 34.7 %copy-start.4 = (bf16[256,256]{1,0:T(8,128)(2,1)S(1)}, bf16[256,256]{1,0:T(8,128)(2,1)}, u32[]{:S(2)}) copy-start(bf16[256,256]{1,0:T(8,128)(2,1)} %constant.61.clone) | copy-start | bytes 393220
  21.7 35.3 %collective-permute-start = (bf16[3,3,256,128]{3,2,1,0:T(8,128)(2,1)S(1)}, bf16[3,3,256,128]{3,2,1,0:T(8,128)(2,1)S(1)}, u32[]{:S(2)}, u32[]{:S(2)}) collective-permute-start(bf16[3,3,256,128]{3,2,1,0:T(8,128)(2,1)S(1)} %get-tuple-element.39), channel_id=1, source_target_pairs={{0,1},{1,2},{2,3},{4,5},{5,6},{6,7},{8,9},{9,10},{10,11},{12,13},{... | collective-permute-start | bytes 1769480 | tf_op jit(solution)/shard_map/ppermute | solution.py:296
  23.1 33.9 %collective-permute-start.1 = (bf16[3,3,256,128]{3,2,1,0:T(8,128)(2,1)S(1)}, bf16[3,3,256,128]{3,2,1,0:T(8,128)(2,1)S(1)}, u32[]{:S(2)}, u32[]{:S(2)}) collective-permute-start(bf16[3,3,256,128]{3,2,1,0:T(8,128)(2,1)S(1)} %get-tuple-element.38), channel_id=1, source_target_pairs={{1,0},{2,1},{3,2},{5,4},{6,5},{7,6},{9,8},{10,9},{11,10},{13,12},{... | collective-permute-start | bytes 1769480 | tf_op jit(solution)/shard_map/ppermute | solution.py:297
  47.6 31.6 %all-to-all-start.1 = ((bf16[128,24,128]{2,1,0:T(8,128)(2,1)}), bf16[128,24,128]{2,1,0:T(8,128)(2,1)S(1)}, u32[]{:S(2)}, u32[]{:S(2)}) async-start(bf16[128,24,128]{2,1,0:T(8,128)(2,1)} %gather_fusion), calls=%async_computation.1 | async-start | bytes 1572864 | tf_op jit(solution)/shard_map/all_to_all | solution.py:302
  57.0 0.9 copy-start.2
  57.8 0.8 copy-start.3
  79.2 18.1 %copy-start = (bf16[128,24,128]{2,1,0:T(8,128)(2,1)}, bf16[128,24,128]{2,1,0:T(8,128)(2,1)S(1)}, u32[]{:S(2)}) copy-start(bf16[128,24,128]{2,1,0:T(8,128)(2,1)S(1)} %all-to-all-done.1) | copy-start | bytes 2359300
  79.4 16.7 %collective-permute-start.2 = (bf16[3,3,256,128]{3,2,1,0:T(8,128)(2,1)S(1)}, bf16[3,3,256,128]{3,2,1,0:T(8,128)(2,1)S(1)}, u32[]{:S(2)}, u32[]{:S(2)}) collective-permute-start(bf16[3,3,256,128]{3,2,1,0:T(8,128)(2,1)S(1)} %get-tuple-element.37), channel_id=1, source_target_pairs={{0,1},{1,2},{2,3},{4,5},{5,6},{6,7},{8,9},{9,10},{10,11},{12,13},{... | collective-permute-start | bytes 1769480 | tf_op jit(solution)/shard_map/ppermute | solution.py:296
  80.7 16.6 %collective-permute-start.3 = (bf16[3,3,256,128]{3,2,1,0:T(8,128)(2,1)S(1)}, bf16[3,3,256,128]{3,2,1,0:T(8,128)(2,1)}, u32[]{:S(2)}, u32[]{:S(2)}) collective-permute-start(bf16[3,3,256,128]{3,2,1,0:T(8,128)(2,1)S(1)} %get-tuple-element.36), channel_id=1, source_target_pairs={{1,0},{2,1},{3,2},{5,4},{6,5},{7,6},{9,8},{10,9},{11,10},{13,12},{... | collective-permute-start | bytes 1769480 | tf_op jit(solution)/shard_map/ppermute | solution.py:297
  86.8 24.6 %all-to-all-start.2 = ((s32[128,1,2]{2,1,0:T(1,128)}), s32[128,1,2]{2,1,0:T(1,128)S(1)}, u32[]{:S(2)}, u32[]{:S(2)}) async-start(s32[128,1,2]{2,1,0:T(1,128)} %copy.28), calls=%async_computation.2 | async-start | bytes 131072 | tf_op jit(solution)/shard_map/all_to_all | solution.py:302
  96.1 1.2 copy-start.7
  111.4 10.9 %copy-start.1 = (bf16[3,4,256,128]{3,2,1,0:T(8,128)(2,1)S(1)}, bf16[3,4,256,128]{3,2,1,0:T(8,128)(2,1)}, u32[]{:S(2)}) copy-start(bf16[3,4,256,128]{3,2,1,0:T(8,128)(2,1)} %get-tuple-element.25) | copy-start | bytes 2359300
  111.4 52.6 %all-to-all-start.3 = ((bf16[128,8,768]{2,1,0:T(8,128)(2,1)}), bf16[128,8,768]{2,1,0:T(8,128)(2,1)S(1)}, u32[]{:S(2)}, u32[]{:S(2)}) async-start(bf16[128,8,768]{2,1,0:T(8,128)(2,1)} %bitcast.30), calls=%async_computation.3 | async-start | bytes 3145728 | tf_op jit(solution)/shard_map/all_to_all | solution.py:302
